TPU v7x, 512 devices: a whole 4x4x16 slice. The times are simulated.
512 devices in a mesh: dp: 4 (over x), ctx: 32 (over z, core), tp: 4 (over y).
Axes of the slice: x: 4, y: 4, z: 16, core: 2. Of those that a mesh axis runs over, the one named last changes fastest.
Arguments:
- inputs: bfloat16 [4, 4096, 8192], P('dp', 'ctx', 'tp'), may hold values from -6 to 6
- grad_out: bfloat16 [4, 4096, 8192], P('dp', 'ctx', 'tp'), may hold values from -6 to 6
- input_map: bfloat16 [4, 4096, 128], P('dp', 'ctx'), may hold values from -0.5 to 0.5
- output_map: bfloat16 [4, 4096, 128], P('dp', 'ctx'), may hold values from -0.25 to 0.25
- step_size: float32 [4, 128, 4096], P('dp', 'tp', 'ctx'), may hold values from 0.3 to 1.5
- log_decay: float32 [4, 128, 4096], P('dp', 'tp', 'ctx'), may hold values from -2 to 0
- skip_gain: float32 [128], P('tp'), may hold values from 0.5 to 1.5
Outputs:
- mixed: bfloat16 [4, 4096, 8192], P('dp', 'ctx', 'tp')
- grad_inputs: bfloat16 [4, 4096, 8192], P('dp', 'ctx', 'tp')
- grad_step: float32 [4, 128, 4096], P('dp', 'tp', 'ctx')
- grad_decay: float32 [4, 128, 4096], P('dp', 'tp', 'ctx')
- grad_input_map: float32 [4, 4096, 128], P('dp', ('ctx', 'tp'))
- grad_output_map: float32 [4, 4096, 128], P('dp', ('ctx', 'tp'))
- grad_skip: float32 [128], P('tp')
All inputs are finite; a program needn't handle non-finite values.
Results may differ from a plain program's by a relative error of at most 0.0011.
Values sent between devices are 32-bit elements; how exact they have to be, the bound alone decides.
No kernel may reach another device: no remote copies, remote signals or barrier semaphores. Data moves between devices by JAX's collectives and lax.ppermute only.
A program may use at most 192 MiB of HBM per device.

v0:
```python
import math

import jax
import jax.numpy as jnp
from jax import lax
from jax.sharding import PartitionSpec as P

precise = lax.Precision.HIGHEST


def entering(part, axis, combine, identity, reverse):
    count = lax.axis_size(axis)
    place = lax.axis_index(axis)
    ahead = count - 1 - place if reverse else place
    gathered = jax.tree.map(lambda a: lax.all_gather(a, axis), part)
    state = jax.tree.map(lambda a, e: jnp.zeros_like(a) + jnp.asarray(e, a.dtype), part, identity)

    def one(hop, state):
        source = count - 1 - hop if reverse else hop
        return combine(
            state, jax.tree.map(lambda a: lax.dynamic_index_in_dim(a, source, 0, False), gathered)
        )

    return lax.fori_loop(0, ahead, one, state)


def combine_pair(earlier, later_part):
    return (earlier[0] * later_part[0], later_part[0][..., None, None] * earlier[1] + later_part[1])


def block_forward(values, in_map, out_map, steps, logs):
    cumulative = jnp.cumsum(logs, axis=-1)
    length = cumulative.shape[-1]
    row_ids = lax.broadcasted_iota(jnp.int32, (length, length), 0)
    column_ids = lax.broadcasted_iota(jnp.int32, (length, length), 1)
    causal = row_ids >= column_ids
    spread = cumulative[..., :, None] - cumulative[..., None, :]
    decays = jnp.where(causal, jnp.exp(jnp.where(causal, spread, 0.0)), 0.0)
    affinity = jnp.einsum("btn,bsn->bts", out_map, in_map, precision=precise)
    mixing = decays * affinity[:, None]
    scaled = values * jnp.transpose(steps, (0, 2, 1))[..., None]
    remain = jnp.exp(cumulative[..., -1:] - cumulative)
    weighted = remain[..., None] * in_map[:, None]
    local_state = jnp.einsum("bshp,bhsn->bhpn", scaled, weighted, precision=precise)
    through = jnp.exp(cumulative[..., -1])
    return (cumulative, decays, mixing, scaled, remain, local_state, through)


def block_output(values, out_map, skip_gain, cumulative, mixing, scaled, incoming):
    within = jnp.einsum("bhts,bshp->bthp", mixing, scaled, precision=precise)
    carried = jnp.einsum("bhpn,btn->bthp", incoming, out_map, precision=precise)
    carried = carried * jnp.transpose(jnp.exp(cumulative), (0, 2, 1))[..., None]
    return (within + carried + skip_gain[:, None] * values, carried)


def block_source(cotangent, out_map, cumulative):
    weighted = jnp.exp(cumulative)[..., None] * out_map[:, None]
    return jnp.einsum("bshp,bhsn->bhpn", cotangent, weighted, precision=precise)


def block_backward(
    values,
    cotangent,
    in_map,
    out_map,
    steps,
    skip_gain,
    cumulative,
    decays,
    mixing,
    scaled,
    remain,
    local_state,
    through,
    incoming,
    carried,
    arriving,
):
    remain_col = jnp.transpose(remain, (0, 2, 1))[..., None]
    starts = jnp.transpose(jnp.exp(cumulative), (0, 2, 1))[..., None]
    steps_col = jnp.transpose(steps, (0, 2, 1))[..., None]
    from_later = jnp.einsum("bhpn,btn->bthp", arriving, in_map, precision=precise)
    state_grad = (
        jnp.einsum("bhst,bshp->bthp", mixing, cotangent, precision=precise)
        + remain_col * from_later
    )
    grad_values = steps_col * state_grad + skip_gain[:, None] * cotangent
    grad_steps = jnp.transpose(jnp.sum(values * state_grad, axis=-1), (0, 2, 1))
    products = jnp.einsum("bthp,bshp->bhts", cotangent, scaled, precision=precise)
    summed = jnp.sum(decays * products, axis=1)
    grad_in_map = jnp.einsum("bts,btn->bsn", summed, out_map, precision=precise) + jnp.einsum(
        "bthp,bhpn->btn", scaled * remain_col, arriving, precision=precise
    )
    grad_out_map = jnp.einsum("bts,bsn->btn", summed, in_map, precision=precise) + jnp.einsum(
        "bthp,bhpn->btn", cotangent * starts, incoming, precision=precise
    )
    paired = mixing * products
    change = jnp.sum(paired, axis=-1) - jnp.sum(paired, axis=-2)
    change = change + jnp.transpose(jnp.sum(cotangent * carried, axis=-1), (0, 2, 1))
    change = change - remain * jnp.transpose(jnp.sum(scaled * from_later, axis=-1), (0, 2, 1))
    final_edge = jnp.sum(arriving * local_state, axis=(2, 3)) + through * jnp.sum(
        arriving * incoming, axis=(2, 3)
    )
    length = change.shape[-1]
    ending = lax.broadcasted_iota(jnp.int32, (length,), 0) == length - 1
    change = change + jnp.where(ending, final_edge[..., None], 0.0)
    grad_logs = lax.cumsum(change, axis=2, reverse=True)
    skip_part = jnp.sum(cotangent * values, axis=(0, 1, 3))
    return (grad_values, grad_steps, grad_in_map, grad_out_map, grad_logs, skip_part)


def shards(inputs, grad_out, input_map, output_map, step_size, log_decay, skip_gain):
    sequences, length, features = inputs.shape
    heads = step_size.shape[1]
    per_head = features // heads
    values = inputs.reshape(sequences, length, heads, per_head).astype(jnp.float32)
    cotangent = grad_out.reshape(sequences, length, heads, per_head).astype(jnp.float32)
    in_map = input_map.astype(jnp.float32)
    out_map = output_map.astype(jnp.float32)
    cumulative, decays, mixing, scaled, remain, local_state, through = block_forward(
        values, in_map, out_map, step_size, log_decay
    )
    source = block_source(cotangent, out_map, cumulative)
    neutral = (jnp.ones_like(through), jnp.zeros_like(local_state))
    ahead = entering((through, local_state), "ctx", combine_pair, neutral, False)
    behind = entering((through, source), "ctx", combine_pair, neutral, True)
    incoming = ahead[1]
    arriving = behind[1]
    mixed, carried = block_output(values, out_map, skip_gain, cumulative, mixing, scaled, incoming)
    results = block_backward(
        values,
        cotangent,
        in_map,
        out_map,
        step_size,
        skip_gain,
        cumulative,
        decays,
        mixing,
        scaled,
        remain,
        local_state,
        through,
        incoming,
        carried,
        arriving,
    )
    grad_values, grad_steps, grad_in_part, grad_out_part, grad_logs, skip_part = results
    grad_in_map, grad_out_map = (
        lax.psum_scatter(grad_in_part, "tp", scatter_dimension=1, tiled=True),
        lax.psum_scatter(grad_out_part, "tp", scatter_dimension=1, tiled=True),
    )
    skip_total = lax.psum(skip_part, ("dp", "ctx"))
    factor = 1.0 / math.sqrt(
        sequences * lax.axis_size("dp") * length * lax.axis_size("ctx") * per_head
    )
    mixed_out = mixed.reshape(sequences, length, features).astype(jnp.bfloat16)
    grad_inputs = grad_values.reshape(sequences, length, features).astype(jnp.bfloat16)
    return (
        mixed_out,
        grad_inputs,
        grad_steps,
        grad_logs,
        grad_in_map,
        grad_out_map,
        skip_total * factor,
    )


def solution(mesh):
    in_specs = (
        P("dp", "ctx", "tp"),
        P("dp", "ctx", "tp"),
        P("dp", "ctx", None),
        P("dp", "ctx", None),
        P("dp", "tp", "ctx"),
        P("dp", "tp", "ctx"),
        P("tp"),
    )
    out_specs = (
        P("dp", "ctx", "tp"),
        P("dp", "ctx", "tp"),
        P("dp", "tp", "ctx"),
        P("dp", "tp", "ctx"),
        P("dp", ("ctx", "tp"), None),
        P("dp", ("ctx", "tp"), None),
        P("tp"),
    )
    return jax.shard_map(shards, mesh=mesh, in_specs=in_specs, out_specs=out_specs, check_vma=False)
```

profile of v0, /device:TPU:1, one launch (start us, length us, event | category | flops | bytes accessed | tf_op | source)
XLA Modules:
  0.0 736.0 jit_solution(14283848565593800011)
XLA Ops:
  7.2 1.0 reduce_window_sum.21
  8.5 1.3 copy.78
  9.9 3.2 fusion.3
  13.2 0.3 copy.84
  13.5 2.4 fusion.16
  16.0 37.4 %all-gather = f32[32,32,1]{1,2,0:T(1,128)S(1)} all-gather(f32[1,32,1]{1,2,0:T(1,128)S(1)} %exp.61), channel_id=2, replica_groups=mesh['dp'=4,'ctx'=32,'tp'=4] {'ctx'}, dimensions={0}, use_global_device_ids=true | all-gather | bytes 4224 | tf_op jit(solution)/shard_map/all_gather | solution.py:15
  53.5 0.1 fusion.65
  53.6 3.1 fusion.20
  56.7 153.6 %all-gather.6.cloned.1.call-done = f32[1024,64,128]{2,1,0:T(8,128)} async-done(((f32[32,64,128]{2,1,0:T(8,128)}), f32[1024,64,128]{2,1,0:T(8,128)}) %all-gather.6.cloned.1.call-update) | async-done | bytes 33554448 | tf_op jit(solution)/shard_map/all_gather | solution.py:15
  210.3 0.1 broadcast_in_dim.53.clone
  210.4 1.5 while.26
  210.5 1.4 bitcast_add_fusion.5
  211.9 189.6 %all-gather.8.cloned.1.call-done = f32[1024,64,128]{2,1,0:T(8,128)} async-done(((f32[32,64,128]{2,1,0:T(8,128)}), f32[1024,64,128]{2,1,0:T(8,128)}) %all-gather.8.cloned.1.call-update) | async-done | bytes 33554448 | tf_op jit(solution)/shard_map/all_gather | solution.py:15
  401.5 0.1 broadcast_in_dim.53.clone.1
  401.6 44.8 %while.27 = (s32[]{:T(128)}, f32[1,32,64,128]{3,2,1,0:T(8,128)S(1)}, s32[]{:T(128)}, f32[32,1,32]{2,1,0:T(1,128)S(1)}, f32[32,1,32,64,128]{4,3,2,1,0:T(8,128)}, ...) while((s32[]{:T(128)}, f32[1,32,64,128]{3,2,1,0:T(8,128)S(1)}, s32[]{:T(128)}, f32[32,1,32]{2,1,0:T(1,128)S(1)}, ...), condition=%wide.region_4.5_spmd, body=%wide.region_3.4_spmd.sunk | while | flops 524294 | bytes 3146259 | solution.py:24
  401.7 1.4 bitcast_add_fusion.6
  403.2 1.4 bitcast_add_fusion.6
  404.7 1.4 bitcast_add_fusion.6
  406.2 1.4 bitcast_add_fusion.6
  407.7 1.4 bitcast_add_fusion.6
  409.2 1.4 bitcast_add_fusion.6
  410.7 1.4 bitcast_add_fusion.6
  412.1 1.4 bitcast_add_fusion.6
  413.6 1.4 bitcast_add_fusion.6
  415.1 1.4 bitcast_add_fusion.6
  416.6 1.4 bitcast_add_fusion.6
  418.1 1.4 bitcast_add_fusion.6
  419.6 1.4 bitcast_add_fusion.6
  421.1 1.4 bitcast_add_fusion.6
  422.6 1.4 bitcast_add_fusion.6
  424.1 1.4 bitcast_add_fusion.6
  425.6 1.4 bitcast_add_fusion.6
  427.1 1.4 bitcast_add_fusion.6
  428.6 1.4 bitcast_add_fusion.6
  430.1 1.4 bitcast_add_fusion.6
  431.6 1.4 bitcast_add_fusion.6
  433.1 1.4 bitcast_add_fusion.6
  434.6 1.4 bitcast_add_fusion.6
  436.1 1.4 bitcast_add_fusion.6
  437.6 1.4 bitcast_add_fusion.6
  439.1 1.4 bitcast_add_fusion.6
  440.5 1.4 bitcast_add_fusion.6
  442.0 1.4 bitcast_add_fusion.6
  443.5 1.4 bitcast_add_fusion.6
  445.0 1.4 bitcast_add_fusion.6
  446.5 1.6 multiply_reduce_fusion.2
  448.1 0.4 fusion.36
  448.5 0.7 copy-done.2
  449.2 1.6 multiply_reduce_fusion.3
  450.9 1.3 multiply_reduce_fusion
  452.2 1.9 convolution_bitcast_fusion.2
  454.1 0.9 fusion.34
  455.0 0.2 reduce-scatter.3.cloned.1.call-start
  455.2 3.8 fusion.31
  459.1 3.2 multiply_reduce_fusion.4
  462.2 1.9 convolution_bitcast_fusion.3
  464.2 1.0 copy.90
  465.2 1.0 copy.89
  466.2 0.1 reduce_sum.113
  466.3 247.9 %psum.7 = f32[32]{0:T(128)S(1)} all-reduce(f32[32]{0:T(128)S(1)} %reduce_sum.113), channel_id=1, replica_groups=mesh['dp'=4,'ctx'=32,'tp'=4] {'dp','ctx'}, use_global_device_ids=true, to_apply=%region_18.19 | all-reduce | flops 32 | bytes 256 | tf_op jit(solution)/shard_map/psum | solution.py:153
  714.2 0.8 fusion.35
  715.0 1.8 reduce_window_sum.22
  716.9 0.5 broadcast_multiply_fusion
  717.4 12.1 %reduce-scatter.3.cloned.1.call-done = f32[1,32,128]{2,1,0:T(8,128)} async-done(((f32[1,128,128]{2,1,0:T(8,128)}), f32[1,32,128]{2,1,0:T(8,128)}) %reduce-scatter.3.cloned.1.call-update) | async-done | bytes 16400 | tf_op jit(solution)/shard_map/reduce_scatter | solution.py:150
  (77 shorter events, 1.0 us)
Async XLA Ops:
  7.2 2.7 copy-start.8
  7.2 2.8 copy-start.11
  7.2 203.1 %all-gather.6.cloned.1.call-start = ((), (), s32[]{:S(2)}) async-start(), calls=%async_computation.4 | async-start | bytes 34603008 | tf_op jit(solution)/shard_map/all_gather | solution.py:15
  9.8 3.3 copy-start.4
  9.8 3.4 copy-start.10
  9.9 3.6 copy-start.9
  13.1 388.4 %all-gather.8.cloned.1.call-start = ((), (), s32[]{:S(2)}) async-start(), calls=%async_computation.5 | async-start | bytes 34603008 | tf_op jit(solution)/shard_map/all_gather | solution.py:15
  13.5 43.1 %copy-start.1 = (bf16[1,128,2048]{1,2,0:T(8,128)(2,1)}, bf16[1,128,2048]{1,2,0:T(8,128)(2,1)S(1)}, u32[]{:S(2)}) copy-start(bf16[1,128,2048]{1,2,0:T(8,128)(2,1)S(1)} %copy.84) | copy-start | bytes 1572868
  16.0 701.4 %reduce-scatter.5.cloned.1.call-start = ((), (), s32[]{:S(2)}) async-start(), calls=%async_computation.3 | async-start | bytes 81920 | tf_op jit(solution)/shard_map/reduce_scatter | solution.py:151
  446.5 1.6 copy-start
  448.1 1.0 copy-start.2
  449.2 1.7 copy-start.5
  450.9 4.3 copy-start.12
  455.0 274.5 %reduce-scatter.3.cloned.1.call-start = ((), (), s32[]{:S(2)}) async-start(), calls=%async_computation.2 | async-start | bytes 81920 | tf_op jit(solution)/shard_map/reduce_scatter | solution.py:150
  455.2 3.8 copy-start.3
  455.2 3.8 copy-start.7
  459.0 3.2 copy-start.6
Sparse Core Ops, SparseCore 0:
  13.3 196.9 all-gather.5
  212.4 189.0 all-gather.7
  455.1 17.8 reduce-scatter.4
  715.2 14.3 reduce-scatter.2
where the time goes:
time: 739 us; the launch traced here: 736 us
  waiting for transfers between devices  355 us (48%)
  blocking collectives  285 us (39%)
  other arithmetic  50.2 us (7%)
  matrix products  24.4 us (3%)
  between operations  14.1 us (2%)
    all_gather x2, waiting for transfers between devices, entering(): gathered = jax.tree.map(lambda a: lax.all_gather(a, axis), part)  343 us
    psum x1, blocking collectives, shards(): skip_total = lax.psum(skip_part, ('dp', 'ctx'))  248 us
    add x31, other arithmetic, combine_pair(): later_part[0][..., None, None] * earlier[1] + later_part[1]  44.9 us
    all_gather x1, blocking collectives, entering(): gathered = jax.tree.map(lambda a: lax.all_gather(a, axis), part)  37.4 us
  transfers between devices with their start and end apart: 4, of which 3 were waited for; matrix products, arithmetic and copies ran while one was open for 3% of the time, Pallas kernels for 0%

commit v1 on v0

v1 whole, which is shorter than its diff:
```python
import math

import jax
import jax.numpy as jnp
from jax import lax
from jax.experimental import pallas as pl
from jax.experimental.pallas import tpu as pltpu
from jax.sharding import PartitionSpec as P

F32 = jnp.float32
BF16 = jnp.bfloat16
HIGHEST = lax.Precision.HIGHEST
TOK = 128
HEADS = 32
PH = 64
NS = 128
QH = 8
QR = QH * PH
VMEM_LIMIT = 48 * 1024 * 1024


def iota(shape, dim):
    return lax.broadcasted_iota(jnp.int32, shape, dim)


def split(value):
    high = value.astype(BF16)
    low = (value - high.astype(F32)).astype(BF16)
    return high, low


def dot(a, b, ca, cb, precision=None):
    return lax.dot_general(a, b, (((ca,), (cb,)), ((), ())), preferred_element_type=F32, precision=precision)


def running_sum(logs):
    upto = (iota((TOK, TOK), 0) <= iota((TOK, TOK), 1)).astype(F32)
    return dot(logs, upto, 1, 0, HIGHEST)


def expander(heads, first, width):
    row = iota((2 * heads, width), 0)
    row = jnp.where(row >= heads, row - heads, row)
    return (row == (iota((2 * heads, width), 1) + first) // PH).astype(F32).astype(BF16)


def spread_heads(factors, first, width):
    high, low = split(factors.T)
    return dot(jnp.concatenate([high, low], axis=1), expander(factors.shape[0], first, width), 1, 0)


def states_kernel(where_ref, x_ref, g_ref, b_ref, c_ref, step_ref, log_ref, send_ref, own_ref):
    cum = running_sum(log_ref[...])
    from_source = step_ref[...] * jnp.exp(cum[:, TOK - 1 : TOK] - cum)
    from_start = jnp.exp(cum)

    def summed(values_ref, factors, map_ref, out_ref):
        doubled = jnp.concatenate([map_ref[...], map_ref[...]], axis=0)
        for first in range(0, HEADS * PH, QR):
            weighted = values_ref[:, first : first + QR].astype(F32) * spread_heads(factors, first, QR)
            high, low = split(weighted)
            out_ref[first : first + QR, :] = dot(jnp.concatenate([high, low], axis=0), doubled, 0, 0)

    forward = where_ref[0] == 1

    @pl.when(forward)
    def _():
        summed(g_ref, from_start, c_ref, send_ref)
        summed(x_ref, from_source, b_ref, own_ref)

    @pl.when(jnp.logical_not(forward))
    def _():
        summed(x_ref, from_source, b_ref, send_ref)
        summed(g_ref, from_start, c_ref, own_ref)


def chip_kernel(where_ref, decay_ref, got_ref, own_ref, *out_refs):
    place = where_ref[1]
    for k, out_ref in enumerate(out_refs):
        quarter = jnp.bitwise_xor(place, k)
        for j in range(QH):
            rows = pl.ds(pl.multiple_of(quarter * QR, QR) + j * PH, PH)
            out_ref[j * PH : (j + 1) * PH, :] = decay_ref[0, quarter * QH + j] * got_ref[rows, :] + own_ref[rows, :]


def group_kernel(where_ref, table_ref, *refs):
    parts, out_ref = refs[:4], refs[4]
    head = where_ref[1] * QH
    for j in range(QH):
        rows = slice(j * PH, (j + 1) * PH)
        total = table_ref[0, head + j] * parts[0][rows, :]
        for k in range(1, 4):
            total = total + table_ref[k, head + j] * parts[k][rows, :]
        out_ref[rows, :] = total


def prefix_kernel(where_ref, table_ref, *refs):
    parts, tops, out_refs = refs[:4], refs[4:7], refs[7:]
    head = where_ref[1] * QH
    for j in range(QH):
        rows = slice(j * PH, (j + 1) * PH)
        entering = table_ref[4, head + j] * tops[0][rows, :]
        for k in range(1, 3):
            entering = entering + table_ref[4 + k, head + j] * tops[k][rows, :]
        pieces = [p[rows, :] for p in parts]
        for k in range(4):
            total = table_ref[7 + k, head + j] * entering
            for i in range(4):
                if i != k:
                    total = total + table_ref[11 + 4 * k + i, head + j] * pieces[i]
            out_refs[k][rows, :] = total


def slab_kernel(x_ref, g_ref, b_ref, c_ref, step_ref, log_ref, after_ref, within_ref, back_ref, maps_ref, skip_ref, summed):
    quarter = pl.program_id(0)

    @pl.when(quarter == 0)
    def _():
        summed[...] = jnp.zeros_like(summed)

    affinity = dot(c_ref[...], b_ref[...], 1, 1)
    causal = iota((TOK, TOK), 0) >= iota((TOK, TOK), 1)
    cum = running_sum(log_ref[...])
    columns = cum.T
    left = iota((TOK, 2 * PH), 1) < PH
    zero = jnp.zeros((TOK, 2 * PH), BF16)
    for pair in range(QH // 2):
        lanes = slice(pair * 2 * PH, (pair + 1) * 2 * PH)
        x, g = x_ref[:, lanes], g_ref[:, lanes]
        xs = (jnp.where(left, x, zero), jnp.where(left, zero, x))
        gs = (jnp.where(left, g, zero), jnp.where(left, zero, g))
        mixes = []
        for side in range(2):
            j = 2 * pair + side
            gap = columns[:, j : j + 1] - cum[j : j + 1, :]
            decays = jnp.exp(jnp.where(causal, gap, -1e30)) * step_ref[j : j + 1, :]
            summed[...] += decays * dot(gs[side], x, 1, 1)
            mixes.extend(split(affinity * decays))
        within_ref[:, lanes] = dot(
            jnp.concatenate(mixes, axis=1), jnp.concatenate([xs[0], xs[0], xs[1], xs[1]], axis=0), 1, 0
        )
        back_ref[:, lanes] = dot(
            jnp.concatenate(mixes, axis=0), jnp.concatenate([gs[0], gs[0], gs[1], gs[1]], axis=0), 0, 0
        )
    products = jnp.sum(x_ref[...].astype(F32) * g_ref[...].astype(F32), axis=0, keepdims=True)
    owner = (iota((QH, QR), 1) // PH == iota((QH, QR), 0)).astype(F32)
    skip_ref[...] = jnp.broadcast_to(jnp.sum(owner * products, axis=1, keepdims=True), (QH, TOK))

    @pl.when(quarter == pl.num_programs(0) - 1)
    def _():
        high, low = split(summed[...])
        b, c = b_ref[...], c_ref[...]
        maps_ref[:, :NS] = dot(jnp.concatenate([high, low], axis=0), jnp.concatenate([c, c], axis=0), 0, 0)
        maps_ref[:, NS:] = dot(jnp.concatenate([high, low], axis=1), jnp.concatenate([b, b], axis=0), 1, 0)


def cross_kernel(
    where_ref, table_ref, x_ref, g_ref, within_ref, back_ref, step_ref, log_ref, gain_ref, b_ref, c_ref,
    near_ref, far_ref, first_ref, send_ref, own_ref, maps_in_ref, *refs,
):
    mixed_ref, ginputs_ref, gstep_ref, gdecay_ref, maps_ref, entering, arriving = refs[-7:]
    forward = where_ref[0] == 1
    head = where_ref[2] * QH
    cum = running_sum(log_ref[...])
    through = jnp.exp(cum[:, TOK - 1 : TOK])
    slots = []
    for j in range(QH):
        rows = slice(j * PH, (j + 1) * PH)
        slots.append(table_ref[27, head + j] * near_ref[rows, :] + first_ref[rows, :])
    scanned = jnp.concatenate(slots, axis=0)
    other = far_ref[...]
    entering[...] = jnp.where(forward, scanned, other)
    arriving[...] = jnp.where(forward, other, scanned)
    local = jnp.where(forward, own_ref[...], send_ref[...])

    x, g = x_ref[...].astype(F32), g_ref[...].astype(F32)
    starts = spread_heads(jnp.exp(cum), 0, QR)
    sources = spread_heads(step_ref[...] * jnp.exp(cum[:, TOK - 1 : TOK] - cum), 0, QR)
    ent, arr = entering[...], arriving[...]
    ent_high, ent_low = split(ent)
    arr_high, arr_low = split(arr)
    b, c = b_ref[...], c_ref[...]
    x_high, x_low = split(x * sources)
    maps_ref[:, :NS] = maps_in_ref[:, :NS] + (
        dot(x_high, arr_high, 1, 0) + (dot(x_low, arr_high, 1, 0) + dot(x_high, arr_low, 1, 0))
    )
    g_high, g_low = split(g * starts)
    maps_ref[:, NS:] = maps_in_ref[:, NS:] + (
        dot(g_high, ent_high, 1, 0) + (dot(g_low, ent_high, 1, 0) + dot(g_high, ent_low, 1, 0))
    )
    carried = dot(jnp.concatenate([c, c], axis=1), jnp.concatenate([ent_high, ent_low], axis=1), 1, 1) * starts
    later = dot(jnp.concatenate([b, b], axis=1), jnp.concatenate([arr_high, arr_low], axis=1), 1, 1) * sources
    output = within_ref[...] + carried
    back = back_ref[...] + later
    gain = gain_ref[...]
    mixed_ref[...] = (output + gain * x).astype(BF16)
    ginputs_ref[...] = (back + gain * g).astype(BF16)

    owner = (iota((QR, QH), 0) // PH == iota((QR, QH), 1)).astype(F32).astype(BF16)
    doubled = jnp.concatenate([owner, owner], axis=0)

    def by_head(values):
        high, low = split(values)
        return dot(jnp.concatenate([high, low], axis=1), doubled, 1, 0).T

    steps_part = x * back
    gstep_ref[...] = by_head(steps_part) / step_ref[...]
    change = by_head(g * output - steps_part)
    edges = []
    for j in range(QH):
        rows = slice(j * PH, (j + 1) * PH)
        leaving = local[rows, :] + through[j : j + 1, :] * ent[rows, :]
        edges.append(jnp.sum(arr[rows, :] * leaving, axis=0, keepdims=True))
    edge = jnp.sum(jnp.concatenate(edges, axis=0), axis=1, keepdims=True)
    change = change + jnp.where(iota((QH, TOK), 1) == TOK - 1, edge, 0.0)
    after = (iota((TOK, TOK), 0) >= iota((TOK, TOK), 1)).astype(F32)
    gdecay_ref[...] = dot(change, after, 1, 0, HIGHEST)


def call(kernel, outs, n_smem, n_in, scratch=()):
    smem = pl.BlockSpec(memory_space=pltpu.SMEM)
    vmem = pl.BlockSpec(memory_space=pltpu.VMEM)
    return pl.pallas_call(
        kernel,
        out_shape=[jax.ShapeDtypeStruct(s, F32) for s in outs],
        in_specs=[smem] * n_smem + [vmem] * n_in,
        out_specs=[vmem] * len(outs),
        scratch_shapes=list(scratch),
        compiler_params=pltpu.CompilerParams(vmem_limit_bytes=VMEM_LIMIT),
    )


def exchange(value, pairs):
    return lax.ppermute(value, "ctx", pairs)


def core_pairs(n):
    return [(i, i ^ 1) for i in range(n)]


def chip_pairs(n, k):
    return [(i, i ^ (2 * k)) for i in range(n)]


def group_pairs(n, k):
    pairs = [(i, i ^ (8 * k)) for i in range(n)]
    return [(i, j) for i, j in pairs if (j > i) == (i % 2 == 1)]


def decay_table(sums, me):
    forward = me % 2 == 1
    chip = me // 2
    base, place = (chip // 4) * 4, chip % 4
    group = chip // 4
    low, high, valid = [], [], []

    def add(f_low, f_high, f_ok, b_low, b_high, b_ok):
        low.append(jnp.where(forward, f_low, b_low))
        high.append(jnp.where(forward, f_high, b_high))
        valid.append(jnp.where(forward, f_ok, b_ok))

    for k in range(4):
        j = base + (place ^ k)
        add(j + 1, base + 4, True, base, j, True)
    for k in range(1, 4):
        s = group ^ k
        add(4 * (s + 1), 4 * group, s < group, 4 * (group + 1), 4 * s, s > group)
    for k in range(4):
        j = base + (place ^ k)
        add(base, j, True, j + 1, base + 4, True)
    for k in range(4):
        j = base + (place ^ k)
        for i in range(4):
            m = base + (place ^ i)
            add(m + 1, j, m < j, j + 1, m, m > j)
    low, high, valid = jnp.stack(low) * 2, jnp.stack(high) * 2, jnp.stack(valid)
    low = jnp.concatenate([low, (me ^ 1)[None]])
    high = jnp.concatenate([high, (me ^ 1)[None] + 1])
    valid = jnp.concatenate([valid, jnp.ones((1,), bool)])
    device = jnp.arange(sums.shape[0])
    inside = (device >= low[:, None]) & (device < high[:, None])
    total = jnp.sum(jnp.where(inside[:, :, None], sums[None], 0.0), axis=1)
    return jnp.where(valid[:, None], jnp.exp(total), 0.0)


def shards(inputs, grad_out, input_map, output_map, step_size, log_decay, skip_gain):
    n = lax.axis_size("ctx")
    me = lax.axis_index("ctx")
    x, g = inputs[0], grad_out[0]
    b, c = input_map[0], output_map[0]
    steps, logs = step_size[0], log_decay[0]
    features = HEADS * PH
    place = (me // 2) % 4
    where = [jnp.stack([me % 2, place, place ^ k]).astype(jnp.int32) for k in range(4)]

    sums = jnp.sum(logs, axis=1)
    table = decay_table(lax.all_gather(sums, "ctx"), me)

    send, own = call(states_kernel, [(features, NS)] * 2, 1, 6)(where[0], x, g, b, c, steps, logs)
    first = exchange(send, core_pairs(n))
    parts = call(chip_kernel, [(QR, NS)] * 4, 2, 2)(where[0], jnp.exp(sums)[None], first, own)
    mine = [parts[0]] + [exchange(parts[k], chip_pairs(n, k)) for k in range(1, 4)]

    quarter = lambda rows, cols, by_row: pl.BlockSpec((rows, cols), (lambda i: (i, 0)) if by_row else (lambda i: (0, i)))
    whole = lambda rows, cols: pl.BlockSpec((rows, cols), lambda i: (0, 0))
    within, back, maps, skips = pl.pallas_call(
        slab_kernel,
        grid=(HEADS // QH,),
        out_shape=[
            jax.ShapeDtypeStruct((TOK, features), F32),
            jax.ShapeDtypeStruct((TOK, features), F32),
            jax.ShapeDtypeStruct((TOK, 2 * NS), F32),
            jax.ShapeDtypeStruct((HEADS, TOK), F32),
        ],
        in_specs=[
            quarter(TOK, QR, False), quarter(TOK, QR, False), whole(TOK, NS), whole(TOK, NS),
            quarter(QH, TOK, True), quarter(QH, TOK, True), pl.BlockSpec((8, NS), lambda i: (0, 0)),
        ],
        out_specs=[quarter(TOK, QR, False), quarter(TOK, QR, False), whole(TOK, 2 * NS), quarter(QH, TOK, True)],
        scratch_shapes=[pltpu.VMEM((TOK, TOK), F32)],
        compiler_params=pltpu.CompilerParams(vmem_limit_bytes=VMEM_LIMIT),
    )(x, g, b, c, steps, logs, parts[0])
    skip_total = lax.psum(skips[:, 0], ("dp", "ctx"))

    (total,) = call(group_kernel, [(QR, NS)], 2, 4)(where[0], table, *mine)
    tops = [exchange(total, group_pairs(n, k)) for k in range(1, 4)]
    ready = call(prefix_kernel, [(QR, NS)] * 4, 2, 7)(where[0], table, *mine, *tops)
    near = [ready[0]] + [exchange(ready[k], chip_pairs(n, k)) for k in range(1, 4)]
    far = [exchange(near[k], core_pairs(n)) for k in range(4)]

    gains = jnp.repeat(skip_gain, PH)[None]
    outs = None
    shapes = [
        jax.ShapeDtypeStruct((TOK, features), BF16),
        jax.ShapeDtypeStruct((TOK, features), BF16),
        jax.ShapeDtypeStruct((HEADS, TOK), F32),
        jax.ShapeDtypeStruct((HEADS, TOK), F32),
        jax.ShapeDtypeStruct((TOK, 2 * NS), F32),
    ]
    for k in range(4):
        cols = pl.BlockSpec((TOK, QR), lambda i, w, t: (0, w[2]))
        rows = pl.BlockSpec((QH, TOK), lambda i, w, t: (w[2], 0))
        state = pl.BlockSpec((QR, NS), lambda i, w, t: (w[2], 0))
        fixed = lambda r, l: pl.BlockSpec((r, l), lambda i, w, t: (0, 0))
        in_specs = [
            cols, cols, cols, cols, rows, rows, pl.BlockSpec((1, QR), lambda i, w, t: (0, w[2])),
            fixed(TOK, NS), fixed(TOK, NS), fixed(QR, NS), fixed(QR, NS), state, state, state, fixed(TOK, 2 * NS),
        ]
        operands = [where[k], table, x, g, within, back, steps, logs, gains, b, c, near[k], far[k], first, send, own, maps]
        aliases = {}
        if k > 0:
            in_specs += [pl.BlockSpec(memory_space=pl.ANY)] * 4
            aliases = {len(operands) + i: i for i in range(4)}
            operands += outs[:4]
        outs = pl.pallas_call(
            cross_kernel,
            grid_spec=pltpu.PrefetchScalarGridSpec(
                num_scalar_prefetch=2,
                grid=(1,),
                in_specs=in_specs,
                out_specs=[cols, cols, rows, rows, fixed(TOK, 2 * NS)],
                scratch_shapes=[pltpu.VMEM((QR, NS), F32)] * 2,
            ),
            out_shape=shapes,
            input_output_aliases=aliases,
            compiler_params=pltpu.CompilerParams(vmem_limit_bytes=VMEM_LIMIT),
        )(*operands)
        maps = outs[4]
    mixed, ginputs, gstep, gdecay, maps = outs
    tp = lax.axis_size("tp")
    swapped = lax.all_to_all(maps.reshape(tp, TOK // tp, 2 * NS), "tp", 0, 0)
    reduced = jnp.sum(swapped, axis=0)
    factor = 1.0 / math.sqrt(lax.axis_size("dp") * TOK * n * PH)
    return (
        mixed[None],
        ginputs[None],
        gstep[None],
        gdecay[None],
        reduced[None, :, :NS],
        reduced[None, :, NS:],
        skip_total * factor,
    )


def solution(mesh):
    in_specs = (
        P("dp", "ctx", "tp"),
        P("dp", "ctx", "tp"),
        P("dp", "ctx", None),
        P("dp", "ctx", None),
        P("dp", "tp", "ctx"),
        P("dp", "tp", "ctx"),
        P("tp"),
    )
    out_specs = (
        P("dp", "ctx", "tp"),
        P("dp", "ctx", "tp"),
        P("dp", "tp", "ctx"),
        P("dp", "tp", "ctx"),
        P("dp", ("ctx", "tp"), None),
        P("dp", ("ctx", "tp"), None),
        P("tp"),
    )
    return jax.shard_map(shards, mesh=mesh, in_specs=in_specs, out_specs=out_specs, check_vma=False)
```

time: 739 us -> 458 us (0.62)
  waiting for transfers between devices: 355 us -> 40.5 us
  starting transfers between devices: 0.34 us -> 66.2 us
  other arithmetic: 50.2 us -> 1.39 us
  Pallas kernels: 0 us -> 29.2 us
  matrix products: 24.4 us -> 0 us
  local copies, waits for them, and re-layouts: 5.03 us -> 19.1 us
  between operations: 14.1 us -> 1.97 us
  blocking collectives: 285 us -> 294 us
    all_gather x2 -> x0, waiting for transfers between devices: 343 us -> none  [entering(): gathered = jax.tree.map(lambda a: lax.all_gather(a, axis), part)]
    ppermute x0 -> x14, starting transfers between devices: none -> 62 us  [exchange(): return lax.ppermute(value, 'ctx', pairs)]
    unnamed x0 -> x1, blocking collectives: none -> 46.4 us
    add x32 -> x0, other arithmetic: 44.9 us -> none  [the longest x31 44.9 us: combine_pair(): later_part[0][..., None, None] * earlier[1] + later_part[1]]
    all_gather x1 -> x0, blocking collectives: 37.4 us -> none  [entering(): gathered = jax.tree.map(lambda a: lax.all_gather(a, axis), part)]
    ppermute x0 -> x14, waiting for transfers between devices: none -> 36.2 us  [exchange(): return lax.ppermute(value, 'ctx', pairs)]
    pallas_call x0 -> x9, Pallas kernels: none -> 29.2 us  [the longest x4 17.2 us: shards(): pl.pallas_call(cross_kernel, grid_spec=pltpu.PrefetchScalarGridSpec(num_s...]
    dot_general x12 -> x0, matrix products: 24.4 us -> none  [the longest x1 3.77 us: block_output(): within = jnp.einsum('bhts,bshp->bthp', mixing, scaled, precision=precise)]
  transfers between devices with their start and end apart: 4 -> 15, of which waited for: 3 -> 4; matrix products, arithmetic and copies ran while one was open for 3% -> 1% of each run, Pallas kernels for 0% -> 4%
where the time goes in v1:
time: 458 us; the launch traced here: 453 us
  blocking collectives  294 us (64%)
  starting transfers between devices  66.2 us (14%)
  waiting for transfers between devices  40.5 us (9%)
  Pallas kernels  29.2 us (6%)
  local copies, waits for them, and re-layouts  19.1 us (4%)
    psum x1, blocking collectives, shards(): skip_total = lax.psum(skips[:, 0], ('dp', 'ctx'))  248 us
    ppermute x14, starting transfers between devices, exchange(): return lax.ppermute(value, 'ctx', pairs)  62 us
    unnamed x1, blocking collectives  46.4 us
    ppermute x14, waiting for transfers between devices, exchange(): return lax.ppermute(value, 'ctx', pairs)  36.2 us
    pallas_call x4, Pallas kernels, shards(): pl.pallas_call(cross_kernel, grid_spec=pltpu.PrefetchScalarGridSpec(num_s...  17.2 us
    unnamed x51, local copies, waits for them, and re-layouts  16.5 us
  transfers between devices with their start and end apart: 15, of which 4 were waited for; matrix products, arithmetic and copies ran while one was open for 1% of the time, Pallas kernels for 4%

profile of v1, /device:TPU:1, one launch (start us, length us, event | category | flops | bytes accessed | tf_op | source)
XLA Modules:
  0.0 452.8 jit_solution(17241828434112601654)
XLA Ops:
  0.7 0.1 pad_add_fusion.4.where_ref
  0.8 0.6 copy-done.18
  1.4 1.0 copy-done.1
  2.5 1.0 copy-done.3
  3.5 0.7 copy-done.19
  4.2 2.6 shard_map.126
  6.9 8.8 %collective-permute-start = (f32[2048,128]{1,0:T(8,128)S(1)}, f32[2048,128]{1,0:T(8,128)S(1)}, u32[]{:S(2)}, u32[]{:S(2)}) collective-permute-start(f32[2048,128]{1,0:T(8,128)S(1)} %get-tuple-element.41.send_ref), channel_id=1, source_target_pairs={{0,4},{4,0},{8,12},{12,8},{16,20},{20,16},{24,28},{28,24},{32,36},... | collective-permute-start | bytes 3145736 | tf_op jit(solution)/shard_map/ppermute | solution.py:234
  15.8 0.1 reduce_sum.27
  16.0 1.3 dynamic-slice
  17.9 0.2 dynamic-update-slice
  18.2 46.4 %all-reduce = f32[1024]{0:T(1024)S(1)} all-reduce(f32[1024]{0:T(1024)S(1)} %dynamic-update-slice), channel_id=2, replica_groups=mesh['dp'=4,'ctx'=32,'tp'=4] {'ctx'}, use_global_device_ids=true, to_apply=%add | all-reduce | flops 1024 | bytes 8192
  64.7 0.1 stack.333
  64.8 0.1 stack.305
  64.9 0.1 pad_add_fusion.2
  65.1 1.5 shard_map.127
  66.6 1.9 collective-permute-start.1
  68.5 1.9 collective-permute-start.2
  70.5 5.4 %collective-permute-start.3 = (f32[512,128]{1,0:T(8,128)}, f32[512,128]{1,0:T(8,128)S(1)}, u32[]{:S(2)}, u32[]{:S(2)}) collective-permute-start(f32[512,128]{1,0:T(8,128)} %get-tuple-element.48), channel_id=1, source_target_pairs={{0,24},{4,28},{8,16},{12,20},{16,8},{20,12},{24,0},{28,4},{32,56},... | collective-permute-start | bytes 786440 | tf_op jit(solution)/shard_map/ppermute | solution.py:234
  75.9 0.2 select_reduce_fusion
  76.2 0.1 concatenate.9
  76.4 13.3 %collective-permute-done.2.refs_2_ = f32[512,128]{1,0:T(8,128)S(1)} collective-permute-done((f32[512,128]{1,0:T(8,128)}, f32[512,128]{1,0:T(8,128)S(1)}, u32[]{:S(2)}, u32[]{:S(2)}) %collective-permute-start.2) | collective-permute-done | bytes 262176 | tf_op jit(solution)/shard_map/ppermute | solution.py:234
  89.8 0.9 shard_map.129
  90.7 0.7 copy-done.12
  91.4 0.7 copy-done.14
  92.1 0.7 copy-done.16
  92.8 6.1 %collective-permute-start.4 = (f32[512,128]{1,0:T(8,128)S(1)}, f32[512,128]{1,0:T(8,128)S(1)}, u32[]{:S(2)}, u32[]{:S(2)}) collective-permute-start(f32[512,128]{1,0:T(8,128)S(1)} %shard_map.129), channel_id=1, source_target_pairs={{4,36},{12,44},{20,52},{28,60},{32,0},{40,8},{48,16},{56,24},{68,1... | collective-permute-start | bytes 786440 | tf_op jit(solution)/shard_map/ppermute | solution.py:234
  98.9 5.6 %collective-permute-start.5 = (f32[512,128]{1,0:T(8,128)S(1)}, f32[512,128]{1,0:T(8,128)S(1)}, u32[]{:S(2)}, u32[]{:S(2)}) collective-permute-start(f32[512,128]{1,0:T(8,128)S(1)} %shard_map.129), channel_id=1, source_target_pairs={{4,68},{12,76},{20,84},{28,92},{36,100},{44,108},{52,116},{60,124}... | collective-permute-start | bytes 786440 | tf_op jit(solution)/shard_map/ppermute | solution.py:234
  104.5 1.3 collective-permute-start.6
  105.8 2.1 collective-permute-done.5.refs_5_
  107.9 20.8 %collective-permute-done.6.refs_6_ = f32[512,128]{1,0:T(8,128)S(1)} collective-permute-done((f32[512,128]{1,0:T(8,128)S(1)}, f32[512,128]{1,0:T(8,128)S(1)}, u32[]{:S(2)}, u32[]{:S(2)}) %collective-permute-start.6) | collective-permute-done | bytes 262176 | tf_op jit(solution)/shard_map/ppermute | solution.py:234
  128.7 0.9 copy-done.13
  129.7 0.9 copy-done.15
  130.6 0.9 copy-done.17
  131.6 1.8 shard_map.130
  133.3 1.9 collective-permute-start.11
  135.2 1.9 collective-permute-start.9
  137.2 5.4 %collective-permute-start.7 = (f32[512,128]{1,0:T(8,128)S(1)}, f32[512,128]{1,0:T(8,128)}, u32[]{:S(2)}, u32[]{:S(2)}) collective-permute-start(f32[512,128]{1,0:T(8,128)S(1)} %get-tuple-element.49), channel_id=1, source_target_pairs={{0,24},{4,28},{8,16},{12,20},{16,8},{20,12},{24,0},{28,4},{32,56},... | collective-permute-start | bytes 786440 | tf_op jit(solution)/shard_map/ppermute | solution.py:234
  142.6 0.1 pad_add_fusion.6.where_ref
  142.7 8.5 %collective-permute-start.13 = (f32[512,128]{1,0:T(8,128)}, f32[512,128]{1,0:T(8,128)}, u32[]{:S(2)}, u32[]{:S(2)}) collective-permute-start(f32[512,128]{1,0:T(8,128)} %get-tuple-element.52.near_ref), channel_id=1, source_target_pairs={{0,4},{4,0},{8,12},{12,8},{16,20},{20,16},{24,28},{28,24},{32,36},... | collective-permute-start | bytes 786440 | tf_op jit(solution)/shard_map/ppermute | solution.py:234
  151.2 1.9 collective-permute-start.12
  153.1 9.3 %collective-permute-start.10 = (f32[512,128]{1,0:T(8,128)}, f32[512,128]{1,0:T(8,128)}, u32[]{:S(2)}, u32[]{:S(2)}) collective-permute-start(f32[512,128]{1,0:T(8,128)} %collective-permute-done.9.near_ref), channel_id=1, source_target_pairs={{0,4},{4,0},{8,12},{12,8},{16,20},{20,16},{24,28},{28,24},{32,36},... | collective-permute-start | bytes 786440 | tf_op jit(solution)/shard_map/ppermute | solution.py:234
  162.5 1.9 collective-permute-start.8
  164.4 0.1 pad_add_fusion.5.where_ref
  164.5 0.6 copy-done.23
  165.1 0.7 broadcast_in_dim.71
  165.8 0.8 broadcast_in_dim_reshape.3.gain_ref
  166.6 0.1 pad_add_fusion.where_ref
  166.7 5.3 %shard_map.128 = (f32[128,2048]{1,0:T(8,128)S(1)}, f32[128,2048]{1,0:T(8,128)S(1)}, f32[128,256]{1,0:T(8,128)S(1)}, f32[32,128]{1,0:T(8,128)S(1)}) custom-call(bf16[128,2048]{1,0:T(8,128)(2,1)S(1)} %bitcast.94, bf16[128,2048]{1,0:T(8,128)(2,1)S(1)} %bitcast.100, bf16[128,128]{1,0:T(8,128)(2,1)S(1)} %bitcast.106, bf16[128,128]{1,0:T(8,128)(2,1)S(1)} %bitcast.112, ...), custom_call_target="tpu_custom_call" | custom-call | tf_op jit(solution)/shard_map/pallas_call | solution.py:306
  171.9 1.0 copy-done.5
  172.9 1.0 copy-done.8
  173.9 0.7 copy-done.21
  174.5 0.1 slice_reduce_fusion
  174.7 248.0 %psum.7 = f32[32]{0:T(128)S(1)} all-reduce(f32[32]{0:T(128)S(1)} %slice_reduce_fusion), channel_id=1, replica_groups=mesh['dp'=4,'ctx'=32,'tp'=4] {'dp','ctx'}, use_global_device_ids=true, to_apply=%region_3.4 | all-reduce | flops 32 | bytes 256 | tf_op jit(solution)/shard_map/psum | solution.py:323
  422.6 1.2 copy-done.6
  423.8 1.2 copy-done.9
  425.1 0.9 copy-done.22
  426.0 4.3 shard_map.131
  430.3 4.3 shard_map.132
  434.5 4.3 shard_map.133
  438.8 4.3 shard_map.134
  443.2 4.2 all-to-all-start
  447.3 0.5 broadcast_multiply_fusion
  447.9 4.3 all-to-all-done
  452.2 0.6 slice_bitcast_fusion
  (50 shorter events, 0.4 us)
Async XLA Ops:
  0.6 0.7 copy-start.18
  0.7 0.8 copy-start.11
  0.7 0.8 copy-start.10
  1.4 1.0 copy-start.1
  2.5 1.0 copy-start.3
  3.5 0.7 copy-start.19
  6.9 59.8 %copy-start = (f32[2048,128]{1,0:T(8,128)}, f32[2048,128]{1,0:T(8,128)S(1)}, u32[]{:S(2)}) copy-start(f32[2048,128]{1,0:T(8,128)S(1)} %get-tuple-element.42.own_ref) | copy-start | bytes 3145732
  6.9 58.2 %collective-permute-start = (f32[2048,128]{1,0:T(8,128)S(1)}, f32[2048,128]{1,0:T(8,128)S(1)}, u32[]{:S(2)}, u32[]{:S(2)}) collective-permute-start(f32[2048,128]{1,0:T(8,128)S(1)} %get-tuple-element.41.send_ref), channel_id=1, source_target_pairs={{0,4},{4,0},{8,12},{12,8},{16,20},{20,16},{24,28},{28,24},{32,36},... | collective-permute-start | bytes 3145736 | tf_op jit(solution)/shard_map/ppermute | solution.py:234
  66.6 9.8 %collective-permute-start.1 = (f32[512,128]{1,0:T(8,128)}, f32[512,128]{1,0:T(8,128)S(1)}, u32[]{:S(2)}, u32[]{:S(2)}) collective-permute-start(f32[512,128]{1,0:T(8,128)} %get-tuple-element.46), channel_id=1, source_target_pairs={{0,8},{4,12},{8,0},{12,4},{16,24},{20,28},{24,16},{28,20},{32,40},... | collective-permute-start | bytes 786440 | tf_op jit(solution)/shard_map/ppermute | solution.py:234
  68.5 21.2 %collective-permute-start.2 = (f32[512,128]{1,0:T(8,128)}, f32[512,128]{1,0:T(8,128)S(1)}, u32[]{:S(2)}, u32[]{:S(2)}) collective-permute-start(f32[512,128]{1,0:T(8,128)} %get-tuple-element.47), channel_id=1, source_target_pairs={{0,16},{4,20},{8,24},{12,28},{16,0},{20,4},{24,8},{28,12},{32,48},... | collective-permute-start | bytes 786440 | tf_op jit(solution)/shard_map/ppermute | solution.py:234
  70.5 19.3 %collective-permute-start.3 = (f32[512,128]{1,0:T(8,128)}, f32[512,128]{1,0:T(8,128)S(1)}, u32[]{:S(2)}, u32[]{:S(2)}) collective-permute-start(f32[512,128]{1,0:T(8,128)} %get-tuple-element.48), channel_id=1, source_target_pairs={{0,24},{4,28},{8,16},{12,20},{16,8},{20,12},{24,0},{28,4},{32,56},... | collective-permute-start | bytes 786440 | tf_op jit(solution)/shard_map/ppermute | solution.py:234
  90.7 0.7 copy-start.12
  91.4 0.7 copy-start.14
  92.1 0.7 copy-start.16
  92.8 73.9 %copy-start.2 = (bf16[1,128,2048]{2,1,0:T(8,128)(2,1)S(1)}, bf16[1,128,2048]{2,1,0:T(8,128)(2,1)}, u32[]{:S(2)}) copy-start(bf16[1,128,2048]{2,1,0:T(8,128)(2,1)} %param.7) | copy-start | bytes 1572868
  92.8 73.9 %copy-start.4 = (bf16[1,128,2048]{2,1,0:T(8,128)(2,1)S(1)}, bf16[1,128,2048]{2,1,0:T(8,128)(2,1)}, u32[]{:S(2)}) copy-start(bf16[1,128,2048]{2,1,0:T(8,128)(2,1)} %param.8) | copy-start | bytes 1572868
  92.8 13.1 %collective-permute-start.4 = (f32[512,128]{1,0:T(8,128)S(1)}, f32[512,128]{1,0:T(8,128)S(1)}, u32[]{:S(2)}, u32[]{:S(2)}) collective-permute-start(f32[512,128]{1,0:T(8,128)S(1)} %shard_map.129), channel_id=1, source_target_pairs={{4,36},{12,44},{20,52},{28,60},{32,0},{40,8},{48,16},{56,24},{68,1... | collective-permute-start | bytes 786440 | tf_op jit(solution)/shard_map/ppermute | solution.py:234
  98.9 9.0 %collective-permute-start.5 = (f32[512,128]{1,0:T(8,128)S(1)}, f32[512,128]{1,0:T(8,128)S(1)}, u32[]{:S(2)}, u32[]{:S(2)}) collective-permute-start(f32[512,128]{1,0:T(8,128)S(1)} %shard_map.129), channel_id=1, source_target_pairs={{4,68},{12,76},{20,84},{28,92},{36,100},{44,108},{52,116},{60,124}... | collective-permute-start | bytes 786440 | tf_op jit(solution)/shard_map/ppermute | solution.py:234
  104.5 24.2 %collective-permute-start.6 = (f32[512,128]{1,0:T(8,128)S(1)}, f32[512,128]{1,0:T(8,128)S(1)}, u32[]{:S(2)}, u32[]{:S(2)}) collective-permute-start(f32[512,128]{1,0:T(8,128)S(1)} %shard_map.129), channel_id=1, source_target_pairs={{4,100},{12,108},{20,116},{28,124},{36,68},{44,76},{52,84},{60,92}... | collective-permute-start | bytes 786440 | tf_op jit(solution)/shard_map/ppermute | solution.py:234
  128.7 0.9 copy-start.13
  129.7 0.9 copy-start.15
  130.6 0.9 copy-start.17
  133.3 17.9 %collective-permute-start.11 = (f32[512,128]{1,0:T(8,128)S(1)}, f32[512,128]{1,0:T(8,128)}, u32[]{:S(2)}, u32[]{:S(2)}) collective-permute-start(f32[512,128]{1,0:T(8,128)S(1)} %get-tuple-element.51), channel_id=1, source_target_pairs={{0,8},{4,12},{8,0},{12,4},{16,24},{20,28},{24,16},{28,20},{32,40},... | collective-permute-start | bytes 786440 | tf_op jit(solution)/shard_map/ppermute | solution.py:234
  135.2 17.9 %collective-permute-start.9 = (f32[512,128]{1,0:T(8,128)S(1)}, f32[512,128]{1,0:T(8,128)}, u32[]{:S(2)}, u32[]{:S(2)}) collective-permute-start(f32[512,128]{1,0:T(8,128)S(1)} %get-tuple-element.50), channel_id=1, source_target_pairs={{0,16},{4,20},{8,24},{12,28},{16,0},{20,4},{24,8},{28,12},{32,48},... | collective-permute-start | bytes 786440 | tf_op jit(solution)/shard_map/ppermute | solution.py:234
  137.2 25.3 %collective-permute-start.7 = (f32[512,128]{1,0:T(8,128)S(1)}, f32[512,128]{1,0:T(8,128)}, u32[]{:S(2)}, u32[]{:S(2)}) collective-permute-start(f32[512,128]{1,0:T(8,128)S(1)} %get-tuple-element.49), channel_id=1, source_target_pairs={{0,24},{4,28},{8,16},{12,20},{16,8},{20,12},{24,0},{28,4},{32,56},... | collective-permute-start | bytes 786440 | tf_op jit(solution)/shard_map/ppermute | solution.py:234
  142.7 279.9 %collective-permute-start.13 = (f32[512,128]{1,0:T(8,128)}, f32[512,128]{1,0:T(8,128)}, u32[]{:S(2)}, u32[]{:S(2)}) collective-permute-start(f32[512,128]{1,0:T(8,128)} %get-tuple-element.52.near_ref), channel_id=1, source_target_pairs={{0,4},{4,0},{8,12},{12,8},{16,20},{20,16},{24,28},{28,24},{32,36},... | collective-permute-start | bytes 786440 | tf_op jit(solution)/shard_map/ppermute | solution.py:234
  151.2 279.1 %collective-permute-start.12 = (f32[512,128]{1,0:T(8,128)}, f32[512,128]{1,0:T(8,128)}, u32[]{:S(2)}, u32[]{:S(2)}) collective-permute-start(f32[512,128]{1,0:T(8,128)} %collective-permute-done.11.near_ref), channel_id=1, source_target_pairs={{0,4},{4,0},{8,12},{12,8},{16,20},{20,16},{24,28},{28,24},{32,36},... | collective-permute-start | bytes 786440 | tf_op jit(solution)/shard_map/ppermute | solution.py:234
  153.1 281.4 %collective-permute-start.10 = (f32[512,128]{1,0:T(8,128)}, f32[512,128]{1,0:T(8,128)}, u32[]{:S(2)}, u32[]{:S(2)}) collective-permute-start(f32[512,128]{1,0:T(8,128)} %collective-permute-done.9.near_ref), channel_id=1, source_target_pairs={{0,4},{4,0},{8,12},{12,8},{16,20},{20,16},{24,28},{28,24},{32,36},... | collective-permute-start | bytes 786440 | tf_op jit(solution)/shard_map/ppermute | solution.py:234
  162.5 276.3 %collective-permute-start.8 = (f32[512,128]{1,0:T(8,128)}, f32[512,128]{1,0:T(8,128)}, u32[]{:S(2)}, u32[]{:S(2)}) collective-permute-start(f32[512,128]{1,0:T(8,128)} %collective-permute-done.7.near_ref), channel_id=1, source_target_pairs={{0,4},{4,0},{8,12},{12,8},{16,20},{20,16},{24,28},{28,24},{32,36},... | collective-permute-start | bytes 786440 | tf_op jit(solution)/shard_map/ppermute | solution.py:234
  164.4 0.7 copy-start.23
  165.8 0.9 copy-start.20
  171.9 1.0 copy-start.5
  172.9 1.0 copy-start.8
  173.9 0.7 copy-start.21
  422.6 1.2 copy-start.6
  423.8 1.2 copy-start.9
  425.1 0.9 copy-start.22
  426.0 4.3 copy-start.7
  443.2 9.0 %all-to-all-start = ((f32[4,32,256]{2,1,0:T(8,128)}), f32[4,32,256]{2,1,0:T(8,128)S(1)}, u32[]{:S(2)}, u32[]{:S(2)}) async-start(f32[4,32,256]{2,1,0:T(8,128)} %bitcast.87), calls=%async_computation | async-start | bytes 262144 | tf_op jit(solution)/shard_map/all_to_all | solution.py:371

commit v2 on v1

v2 whole, which is shorter than its diff:
```python
import math

import jax
import jax.numpy as jnp
from jax import lax
from jax.experimental import pallas as pl
from jax.experimental.pallas import tpu as pltpu
from jax.sharding import PartitionSpec as P

F32 = jnp.float32
BF16 = jnp.bfloat16
HIGHEST = lax.Precision.HIGHEST
TOK = 128
HEADS = 32
PH = 64
NS = 128
FEATS = HEADS * PH
QH = 8
QR = QH * PH
CHUNKS = 2
CH = QH // CHUNKS
CR = CH * PH
SIDE = 2 * HEADS
VMEM_LIMIT = 48 * 1024 * 1024


def iota(shape, dim):
    return lax.broadcasted_iota(jnp.int32, shape, dim)


def split(value):
    high = value.astype(BF16)
    low = (value - high.astype(F32)).astype(BF16)
    return high, low


def dot(a, b, ca, cb, precision=None):
    return lax.dot_general(a, b, (((ca,), (cb,)), ((), ())), preferred_element_type=F32, precision=precision)


def running_sum(logs):
    upto = (iota((TOK, TOK), 0) <= iota((TOK, TOK), 1)).astype(F32)
    return dot(logs, upto, 1, 0, HIGHEST)


def expander(heads, first, width):
    row = iota((2 * heads, width), 0)
    row = jnp.where(row >= heads, row - heads, row)
    return (row == (iota((2 * heads, width), 1) + first) // PH).astype(F32).astype(BF16)


def spread_heads(factors, first, width):
    high, low = split(factors.T)
    return dot(jnp.concatenate([high, low], axis=1), expander(factors.shape[0], first, width), 1, 0)


def gate(flag, value):
    return jnp.where(flag, value, 0.0)


def states_kernel(own, where_ref, x_ref, g_ref, b_ref, c_ref, step_ref, log_ref, out_ref):
    cum = running_sum(log_ref[...])

    def summed(values_ref, factors, map_ref):
        doubled = jnp.concatenate([map_ref[...], map_ref[...]], axis=0)
        for first in range(0, FEATS, QR):
            weighted = values_ref[:, first : first + QR].astype(F32) * spread_heads(factors, first, QR)
            high, low = split(weighted)
            out_ref[first : first + QR, :] = dot(jnp.concatenate([high, low], axis=0), doubled, 0, 0)

    forward = where_ref[0] == (1 if own else 0)

    @pl.when(forward)
    def _():
        summed(x_ref, step_ref[...] * jnp.exp(cum[:, TOK - 1 : TOK] - cum), b_ref)

    @pl.when(jnp.logical_not(forward))
    def _():
        summed(g_ref, jnp.exp(cum), c_ref)

    out_ref[FEATS : FEATS + HEADS, :] = jnp.broadcast_to(cum[:, TOK - 1 : TOK], (HEADS, NS))
    products = jnp.sum(x_ref[...].astype(F32) * g_ref[...].astype(F32), axis=0, keepdims=True)
    owner = (iota((HEADS, FEATS), 1) // PH == iota((HEADS, FEATS), 0)).astype(F32)
    skips = jnp.sum(owner * products, axis=1, keepdims=True)
    out_ref[FEATS + HEADS : FEATS + SIDE, :] = jnp.broadcast_to(skips, (HEADS, NS))


def chip_kernel(where_ref, got_ref, own_ref, *out_refs):
    place = where_ref[1]
    for k in range(4):
        quarter = jnp.bitwise_xor(place, k)
        rows = pl.ds(pl.multiple_of(FEATS + quarter * QH, QH), QH)
        logs, got_logs = own_ref[rows, :], got_ref[rows, :]
        rows = pl.ds(pl.multiple_of(FEATS + HEADS + quarter * QH, QH), QH)
        skips = own_ref[rows, :] + got_ref[rows, :]
        decay = jnp.exp(logs)
        logs = logs + got_logs
        for part in range(CHUNKS):
            out_ref = out_refs[k * CHUNKS + part]
            for j in range(CH):
                h = part * CH + j
                rows = pl.ds(pl.multiple_of(quarter * QR + h * PH, PH), PH)
                out_ref[j * PH : (j + 1) * PH, :] = decay[h : h + 1, :] * got_ref[rows, :] + own_ref[rows, :]
            heads = slice(part * CH, (part + 1) * CH)
            out_ref[CR : CR + CH, :] = logs[heads, :]
            out_ref[CR + CH : CR + 2 * CH, :] = skips[heads, :]


def order(where_ref, index):
    me = where_ref[index]
    places = [jnp.bitwise_xor(me, k) for k in range(4)]
    return [jnp.where(where_ref[0] == 1, p, 3 - p) for p in places]


def group_kernel(where_ref, *refs):
    parts, out_ref = refs[:4], refs[4]
    place = order(where_ref, 1)
    logs = [p[CR : CR + CH, :] for p in parts]
    weights = []
    for k in range(4):
        later = [gate(place[i] > place[k], logs[i]) for i in range(4) if i != k]
        weights.append(jnp.exp(later[0] + later[1] + later[2]))
    for j in range(CH):
        rows = slice(j * PH, (j + 1) * PH)
        terms = [weights[k][j : j + 1, :] * parts[k][rows, :] for k in range(4)]
        out_ref[rows, :] = (terms[0] + terms[1]) + (terms[2] + terms[3])
    side = slice(CR, CR + 2 * CH)
    out_ref[side, :] = (parts[0][side, :] + parts[1][side, :]) + (parts[2][side, :] + parts[3][side, :])


def prefix_kernel(where_ref, *refs):
    place, group = order(where_ref, 1), order(where_ref, 3)
    out_refs = refs[7 * CHUNKS :]
    skips = []
    for part in range(CHUNKS):
        parts, tops = refs[7 * part : 7 * part + 4], refs[7 * part + 4 : 7 * part + 7]
        logs = [p[CR : CR + CH, :] for p in parts]
        top_logs = [t[CR : CR + CH, :] for t in tops]
        top_weights = []
        for k in range(3):
            between = [
                gate((group[k + 1] < group[i + 1]) & (group[i + 1] < group[0]), top_logs[i])
                for i in range(3)
                if i != k
            ]
            top_weights.append(jnp.exp(between[0] + between[1]))
        group_weights, pair_weights = [], {}
        for k in range(4):
            before = [gate(place[i] < place[k], logs[i]) for i in range(4) if i != k]
            group_weights.append(jnp.exp(before[0] + before[1] + before[2]))
            for i in range(4):
                if i != k:
                    between = [
                        gate((place[i] < place[m]) & (place[m] < place[k]), logs[m])
                        for m in range(4)
                        if m not in (i, k)
                    ]
                    pair_weights[k, i] = gate(place[i] < place[k], jnp.exp(between[0] + between[1]))
        for j in range(CH):
            rows = slice(j * PH, (j + 1) * PH)
            at = slice(j, j + 1)
            entering = top_weights[0][at, :] * tops[0][rows, :] + top_weights[1][at, :] * tops[1][rows, :]
            entering = entering + top_weights[2][at, :] * tops[2][rows, :]
            pieces = [p[rows, :] for p in parts]
            first = (part * CH + j) * PH
            for k in range(4):
                total = group_weights[k][at, :] * entering
                for i in range(4):
                    if i != k:
                        total = total + pair_weights[k, i][at, :] * pieces[i]
                out_refs[k][first : first + PH, :] = total
        side = slice(CR + CH, CR + 2 * CH)
        mine = (parts[0][side, :] + parts[1][side, :]) + (parts[2][side, :] + parts[3][side, :])
        skips.append(gate(where_ref[0] == 1, mine) + (tops[0][side, :] + tops[1][side, :] + tops[2][side, :]))
    for k in range(4):
        out_refs[k][QR : QR + QH, :] = jnp.concatenate(skips, axis=0)


def slab_kernel(x_ref, g_ref, b_ref, c_ref, step_ref, log_ref, after_ref, within_ref, back_ref, maps_ref, summed):
    quarter = pl.program_id(0)

    @pl.when(quarter == 0)
    def _():
        summed[...] = jnp.zeros_like(summed)

    affinity = dot(c_ref[...], b_ref[...], 1, 1)
    causal = iota((TOK, TOK), 0) >= iota((TOK, TOK), 1)
    cum = running_sum(log_ref[...])
    columns = cum.T
    left = iota((TOK, 2 * PH), 1) < PH
    zero = jnp.zeros((TOK, 2 * PH), BF16)
    for pair in range(QH // 2):
        lanes = slice(pair * 2 * PH, (pair + 1) * 2 * PH)
        x, g = x_ref[:, lanes], g_ref[:, lanes]
        xs = (jnp.where(left, x, zero), jnp.where(left, zero, x))
        gs = (jnp.where(left, g, zero), jnp.where(left, zero, g))
        mixes = []
        for side in range(2):
            j = 2 * pair + side
            gap = columns[:, j : j + 1] - cum[j : j + 1, :]
            decays = jnp.exp(jnp.where(causal, gap, -1e30)) * step_ref[j : j + 1, :]
            summed[...] += decays * dot(gs[side], x, 1, 1)
            mixes.extend(split(affinity * decays))
        within_ref[:, lanes] = dot(
            jnp.concatenate(mixes, axis=1), jnp.concatenate([xs[0], xs[0], xs[1], xs[1]], axis=0), 1, 0
        )
        back_ref[:, lanes] = dot(
            jnp.concatenate(mixes, axis=0), jnp.concatenate([gs[0], gs[0], gs[1], gs[1]], axis=0), 0, 0
        )

    @pl.when(quarter == pl.num_programs(0) - 1)
    def _():
        high, low = split(summed[...])
        b, c = b_ref[...], c_ref[...]
        maps_ref[:, :NS] = dot(jnp.concatenate([high, low], axis=0), jnp.concatenate([c, c], axis=0), 0, 0)
        maps_ref[:, NS:] = dot(jnp.concatenate([high, low], axis=1), jnp.concatenate([b, b], axis=0), 1, 0)


def cross_kernel(
    last, where_ref, x_ref, g_ref, within_ref, back_ref, step_ref, log_ref, gain_ref, b_ref, c_ref,
    near_ref, far_ref, first_ref, other_ref, send_ref, own_ref, maps_in_ref, *refs,
):
    count = 9 if last else 6
    mixed_ref, ginputs_ref, gstep_ref, gdecay_ref, skip_ref = refs[-count : 5 - count]
    maps_refs = refs[5 - count :]
    forward = where_ref[0] == 1
    cum = running_sum(log_ref[...])
    through = jnp.exp(cum[:, TOK - 1 : TOK])
    skip_ref[...] = near_ref[QR : QR + QH, :] + far_ref[QR : QR + QH, :]
    decay = jnp.exp(other_ref[...])
    slots = []
    for j in range(QH):
        rows = slice(j * PH, (j + 1) * PH)
        slots.append(decay[j : j + 1, :] * near_ref[rows, :] + first_ref[rows, :])
    scanned = jnp.concatenate(slots, axis=0)
    other = far_ref[:QR, :]
    ent = jnp.where(forward, scanned, other)
    arr = jnp.where(forward, other, scanned)

    x, g = x_ref[...].astype(F32), g_ref[...].astype(F32)
    starts = spread_heads(jnp.exp(cum), 0, QR)
    sources = spread_heads(step_ref[...] * jnp.exp(cum[:, TOK - 1 : TOK] - cum), 0, QR)
    ent_high, ent_low = split(ent)
    arr_high, arr_low = split(arr)
    b, c = b_ref[...], c_ref[...]
    x_high, x_low = split(x * sources)
    from_arr = dot(x_high, arr_high, 1, 0) + (dot(x_low, arr_high, 1, 0) + dot(x_high, arr_low, 1, 0))
    g_high, g_low = split(g * starts)
    from_ent = dot(g_high, ent_high, 1, 0) + (dot(g_low, ent_high, 1, 0) + dot(g_high, ent_low, 1, 0))
    maps = maps_in_ref[...] + jnp.concatenate([from_arr, from_ent], axis=1)
    if last:
        rows = TOK // 4
        for k in range(4):
            part = jnp.bitwise_xor(where_ref[4], k)
            total = gate(part == 0, maps[:rows, :])
            for i in range(1, 4):
                total = jnp.where(part == i, maps[i * rows : (i + 1) * rows, :], total)
            maps_refs[k][...] = total
    else:
        maps_refs[0][...] = maps
    carried = dot(jnp.concatenate([c, c], axis=1), jnp.concatenate([ent_high, ent_low], axis=1), 1, 1) * starts
    later = dot(jnp.concatenate([b, b], axis=1), jnp.concatenate([arr_high, arr_low], axis=1), 1, 1) * sources
    output = within_ref[...] + carried
    back = back_ref[...] + later
    gain = gain_ref[...]
    mixed_ref[...] = (output + gain * x).astype(BF16)
    ginputs_ref[...] = (back + gain * g).astype(BF16)

    owner = (iota((QR, QH), 0) // PH == iota((QR, QH), 1)).astype(F32).astype(BF16)
    doubled = jnp.concatenate([owner, owner], axis=0)

    def by_head(values):
        high, low = split(values)
        return dot(jnp.concatenate([high, low], axis=1), doubled, 1, 0).T

    steps_part = x * back
    gstep_ref[...] = by_head(steps_part) / step_ref[...]
    change = by_head(g * output - steps_part)
    local = jnp.where(forward, own_ref[...], send_ref[...])
    edges = []
    for j in range(QH):
        rows = slice(j * PH, (j + 1) * PH)
        leaving = local[rows, :] + through[j : j + 1, :] * ent[rows, :]
        edges.append(jnp.sum(arr[rows, :] * leaving, axis=0, keepdims=True))
    edge = jnp.sum(jnp.concatenate(edges, axis=0), axis=1, keepdims=True)
    change = change + jnp.where(iota((QH, TOK), 1) == TOK - 1, edge, 0.0)
    after = (iota((TOK, TOK), 0) >= iota((TOK, TOK), 1)).astype(F32)
    gdecay_ref[...] = dot(change, after, 1, 0, HIGHEST)


def call(kernel, outs, n_in):
    smem = pl.BlockSpec(memory_space=pltpu.SMEM)
    vmem = pl.BlockSpec(memory_space=pltpu.VMEM)
    return pl.pallas_call(
        kernel,
        out_shape=[jax.ShapeDtypeStruct(s, F32) for s in outs],
        in_specs=[smem] + [vmem] * n_in,
        out_specs=[vmem] * len(outs),
        compiler_params=pltpu.CompilerParams(vmem_limit_bytes=VMEM_LIMIT),
    )


def tied(value, *others):
    return lax.optimization_barrier((value, *others))[0]


def core_pairs(n):
    return [(i, i ^ 1) for i in range(n)]


def chip_pairs(n, k):
    return [(i, i ^ (2 * k)) for i in range(n)]


def group_pairs(n, k):
    pairs = [(i, i ^ (8 * k)) for i in range(n)]
    return [(i, j) for i, j in pairs if (j > i) == (i % 2 == 1)]


def partners(value, axis, k):
    n = lax.axis_size(axis)
    return lax.ppermute(value, axis, [(i, i ^ k) for i in range(n) if i ^ k < n])


def shards(inputs, grad_out, input_map, output_map, step_size, log_decay, skip_gain):
    n = lax.axis_size("ctx")
    me = lax.axis_index("ctx")
    x, g = inputs[0], grad_out[0]
    b, c = input_map[0], output_map[0]
    steps, logs = step_size[0], log_decay[0]
    place, group = (me // 2) % 4, me // 8
    member = lax.axis_index("tp")
    where = [jnp.stack([me % 2, place, place ^ k, group, member]).astype(jnp.int32) for k in range(4)]
    gains = jnp.repeat(skip_gain, PH)[None]
    slab = [(FEATS + SIDE, NS)]

    def states(own):
        return call(lambda *refs: states_kernel(own, *refs), slab, 6)(where[0], x, g, b, c, steps, logs)[0]

    send = states(False)
    first = lax.ppermute(send, "ctx", core_pairs(n))
    own = states(True)
    piece = (CR + 2 * CH, NS)
    parts = call(chip_kernel, [piece] * (4 * CHUNKS), 2)(where[0], first, own)
    mine = []
    for i in range(CHUNKS):
        mine.append([parts[i]] + [lax.ppermute(parts[k * CHUNKS + i], "ctx", chip_pairs(n, k)) for k in range(1, 4)])

    quarter = lambda rows, cols, by_row: pl.BlockSpec((rows, cols), (lambda i: (i, 0)) if by_row else (lambda i: (0, i)))
    whole = lambda rows, cols: pl.BlockSpec((rows, cols), lambda i: (0, 0))
    within, back, maps = pl.pallas_call(
        slab_kernel,
        grid=(HEADS // QH,),
        out_shape=[
            jax.ShapeDtypeStruct((TOK, FEATS), F32),
            jax.ShapeDtypeStruct((TOK, FEATS), F32),
            jax.ShapeDtypeStruct((TOK, 2 * NS), F32),
        ],
        in_specs=[
            quarter(TOK, QR, False), quarter(TOK, QR, False), whole(TOK, NS), whole(TOK, NS),
            quarter(QH, TOK, True), quarter(QH, TOK, True), whole(8, NS),
        ],
        out_specs=[quarter(TOK, QR, False), quarter(TOK, QR, False), whole(TOK, 2 * NS)],
        scratch_shapes=[pltpu.VMEM((TOK, TOK), F32)],
        compiler_params=pltpu.CompilerParams(vmem_limit_bytes=VMEM_LIMIT),
    )(x, g, b, c, steps, logs, mine[0][1])

    gathered = []
    for i in range(CHUNKS):
        (total,) = call(group_kernel, [piece], 4)(where[0], *mine[i])
        gathered.append(mine[i] + [lax.ppermute(total, "ctx", group_pairs(n, k)) for k in range(1, 4)])
    ready = call(prefix_kernel, [(QR + QH, NS)] * 4, 7 * CHUNKS)(where[0], *sum(gathered, []))
    near = [ready[0]] + [lax.ppermute(ready[k], "ctx", chip_pairs(n, k)) for k in range(1, 4)]

    outs = None
    shapes = [
        jax.ShapeDtypeStruct((TOK, FEATS), BF16),
        jax.ShapeDtypeStruct((TOK, FEATS), BF16),
        jax.ShapeDtypeStruct((HEADS, TOK), F32),
        jax.ShapeDtypeStruct((HEADS, TOK), F32),
        jax.ShapeDtypeStruct((HEADS, TOK), F32),
    ]
    for k in range(4):
        last = k == 3
        passed = near[k] if k == 0 else tied(near[k], maps)
        far = lax.ppermute(passed, "ctx", core_pairs(n))
        cols = pl.BlockSpec((TOK, QR), lambda i, w: (0, w[2]))
        rows = pl.BlockSpec((QH, TOK), lambda i, w: (w[2], 0))
        state = pl.BlockSpec((QR, NS), lambda i, w: (w[2], 0))
        others = pl.BlockSpec((QH, NS), lambda i, w: (FEATS // QH + w[2], 0))
        fixed = lambda r, l: pl.BlockSpec((r, l), lambda i, w: (0, 0))
        in_specs = [
            cols, cols, cols, cols, rows, rows, pl.BlockSpec((1, QR), lambda i, w: (0, w[2])),
            fixed(TOK, NS), fixed(TOK, NS), fixed(QR + QH, NS), fixed(QR + QH, NS), state, others, state, state,
            fixed(TOK, 2 * NS),
        ]
        operands = [where[k], x, g, within, back, steps, logs, gains, b, c, passed, far, first, first, send, own, maps]
        aliases = {}
        if k > 0:
            in_specs += [pl.BlockSpec(memory_space=pl.ANY)] * 5
            aliases = {len(operands) + i: i for i in range(5)}
            operands += outs[:5]
        ends = [(TOK // 4, 2 * NS)] * 4 if last else [(TOK, 2 * NS)]
        outs = pl.pallas_call(
            lambda *refs, last=last: cross_kernel(last, *refs),
            grid_spec=pltpu.PrefetchScalarGridSpec(
                num_scalar_prefetch=1,
                grid=(1,),
                in_specs=in_specs,
                out_specs=[cols, cols, rows, rows, rows] + [fixed(*e) for e in ends],
            ),
            out_shape=shapes + [jax.ShapeDtypeStruct(e, F32) for e in ends],
            input_output_aliases=aliases,
            compiler_params=pltpu.CompilerParams(vmem_limit_bytes=VMEM_LIMIT),
        )(*operands)
        maps = outs[5]
    mixed, ginputs, gstep, gdecay, skips = outs[:5]
    reduced = outs[5]
    for k in range(1, 4):
        reduced = reduced + partners(outs[5 + k], "tp", k)
    skip = skips[:, 0]
    skip_total = skip + partners(skip, "dp", 1) + partners(skip, "dp", 2) + partners(skip, "dp", 3)
    factor = 1.0 / math.sqrt(lax.axis_size("dp") * TOK * n * PH)
    return (
        mixed[None],
        ginputs[None],
        gstep[None],
        gdecay[None],
        reduced[None, :, :NS],
        reduced[None, :, NS:],
        skip_total * factor,
    )


def solution(mesh):
    in_specs = (
        P("dp", "ctx", "tp"),
        P("dp", "ctx", "tp"),
        P("dp", "ctx", None),
        P("dp", "ctx", None),
        P("dp", "tp", "ctx"),
        P("dp", "tp", "ctx"),
        P("tp"),
    )
    out_specs = (
        P("dp", "ctx", "tp"),
        P("dp", "ctx", "tp"),
        P("dp", "tp", "ctx"),
        P("dp", "tp", "ctx"),
        P("dp", ("ctx", "tp"), None),
        P("dp", ("ctx", "tp"), None),
        P("tp"),
    )
    return jax.shard_map(shards, mesh=mesh, in_specs=in_specs, out_specs=out_specs, check_vma=False)
```

time: 458 us -> 170 us (0.37)
  the two profiles are of different devices: /device:TPU:1 before, /device:TPU:36 now
where the time goes in v2:
time: 170 us; the launch traced here: 168 us
  starting transfers between devices  66.8 us (39%)
  waiting for transfers between devices  59 us (35%)
  Pallas kernels  29.2 us (17%)
  local copies, waits for them, and re-layouts  11.6 us (7%)
    ppermute x6, waiting for transfers between devices, shards(): lax.ppermute(total, 'ctx', group_pairs(n, k))  31.5 us
    ppermute x6, starting transfers between devices, partners(): lax.ppermute(value, axis, [(i, i ^ k) for i in range(n) if i ^ k < n])  20.2 us
    ppermute x6, starting transfers between devices, shards(): lax.ppermute(parts[k * CHUNKS + i], 'ctx', chip_pairs(n, k))  19.7 us
    pallas_call x4, Pallas kernels, shards(): pl.pallas_call(lambda *refs, last=last: cross_kernel(last, *refs), grid_s...  16.4 us
    ppermute x3, waiting for transfers between devices, shards(): lax.ppermute(ready[k], 'ctx', chip_pairs(n, k))  13.2 us
    unnamed x42, local copies, waits for them, and re-layouts  10.3 us
    ppermute x3, starting transfers between devices, shards(): lax.ppermute(ready[k], 'ctx', chip_pairs(n, k))  8.9 us
    ppermute x4, starting transfers between devices, shards(): far = lax.ppermute(passed, 'ctx', core_pairs(n))  8.2 us
  transfers between devices with their start and end apart: 26, of which 11 were waited for; matrix products, arithmetic and copies ran while one was open for 1% of the time, Pallas kernels for 12%

profile of v2, /device:TPU:36, one launch (start us, length us, event | category | flops | bytes accessed | tf_op | source)
XLA Modules:
  0.0 168.3 jit_solution(12132608194786674226)
XLA Ops:
  0.8 1.0 copy-done.2
  1.8 1.0 copy-done.4
  2.8 0.8 copy-done.10
  3.6 0.8 copy-done.12
  4.4 0.7 copy-done.14
  5.1 0.7 copy-done.16
  5.8 1.9 %shard_map.126.refs_14_ = f32[2112,128]{1,0:T(8,128)S(1)} custom-call(s32[5]{0:T(128)S(1)} %stack.52.refs_0_.where_ref, bf16[128,2048]{1,0:T(8,128)(2,1)S(1)} %bitcast.21, bf16[128,2048]{1,0:T(8,128)(2,1)S(1)} %bitcast.28, bf16[128,128]{1,0:T(8,128)(2,1)S(1)} %bitcast.35, bf16[128,128]{1,0:T(8,128)(2,1)S(1)} %bitcast.42, f32[32,128]{1,0:T(8,128)S(1)} %bitcast.49, ...), custom_call_target="tpu_custom_call" | custom-call | tf_op jit(solution)/shard_map/pallas_call | solution.py:338
  7.7 1.9 %collective-permute-start = (f32[2112,128]{1,0:T(8,128)S(1)}, f32[2112,128]{1,0:T(8,128)S(1)}, u32[]{:S(2)}, u32[]{:S(2)}) collective-permute-start(f32[2112,128]{1,0:T(8,128)S(1)} %shard_map.126.refs_14_), channel_id=1, source_target_pairs={{0,4},{4,0},{8,12},{12,8},{16,20},{20,16},{24,28},{28,24},{32,36},... | collective-permute-start | bytes 3244040 | tf_op jit(solution)/shard_map/ppermute | solution.py:341
  9.7 1.9 %shard_map.127.own_ref.refs_15_ = f32[2112,128]{1,0:T(8,128)S(1)} custom-call(s32[5]{0:T(128)S(1)} %stack.52.refs_0_.where_ref, bf16[128,2048]{1,0:T(8,128)(2,1)S(1)} %bitcast.22, bf16[128,2048]{1,0:T(8,128)(2,1)S(1)} %bitcast.29, bf16[128,128]{1,0:T(8,128)(2,1)S(1)} %bitcast.36, bf16[128,128]{1,0:T(8,128)(2,1)S(1)} %bitcast.43, f32[32,128]{1,0:T(8,128)S(1)} %bitcast.50, ...), custom_call_target="tpu_custom_call" | custom-call | tf_op jit(solution)/shard_map/pallas_call | solution.py:338
  11.6 0.8 collective-permute-done.got_ref.refs_12_.refs_13_
  12.3 0.7 shard_map.128
  13.0 2.0 %collective-permute-start.1 = (f32[264,128]{1,0:T(8,128)S(1)}, f32[264,128]{1,0:T(8,128)S(1)}, u32[]{:S(2)}, u32[]{:S(2)}) collective-permute-start(f32[264,128]{1,0:T(8,128)S(1)} %get-tuple-element.52), channel_id=1, source_target_pairs={{0,8},{4,12},{8,0},{12,4},{16,24},{20,28},{24,16},{28,20},{32,40},... | collective-permute-start | bytes 405512 | tf_op jit(solution)/shard_map/ppermute | solution.py:347
  15.0 5.2 %collective-permute-start.2 = (f32[264,128]{1,0:T(8,128)S(1)}, f32[264,128]{1,0:T(8,128)S(1)}, u32[]{:S(2)}, u32[]{:S(2)}) collective-permute-start(f32[264,128]{1,0:T(8,128)S(1)} %get-tuple-element.56), channel_id=1, source_target_pairs={{0,16},{4,20},{8,24},{12,28},{16,0},{20,4},{24,8},{28,12},{32,48},... | collective-permute-start | bytes 405512 | tf_op jit(solution)/shard_map/ppermute | solution.py:347
  20.2 2.4 %collective-permute-start.3 = (f32[264,128]{1,0:T(8,128)S(1)}, f32[264,128]{1,0:T(8,128)S(1)}, u32[]{:S(2)}, u32[]{:S(2)}) collective-permute-start(f32[264,128]{1,0:T(8,128)S(1)} %get-tuple-element.57), channel_id=1, source_target_pairs={{0,24},{4,28},{8,16},{12,20},{16,8},{20,12},{24,0},{28,4},{32,56},... | collective-permute-start | bytes 405512 | tf_op jit(solution)/shard_map/ppermute | solution.py:347
  22.6 3.4 %collective-permute-start.7 = (f32[264,128]{1,0:T(8,128)S(1)}, f32[264,128]{1,0:T(8,128)S(1)}, u32[]{:S(2)}, u32[]{:S(2)}) collective-permute-start(f32[264,128]{1,0:T(8,128)S(1)} %get-tuple-element.59), channel_id=1, source_target_pairs={{0,8},{4,12},{8,0},{12,4},{16,24},{20,28},{24,16},{28,20},{32,40},... | collective-permute-start | bytes 405512 | tf_op jit(solution)/shard_map/ppermute | solution.py:347
  26.0 4.3 %collective-permute-start.8 = (f32[264,128]{1,0:T(8,128)S(1)}, f32[264,128]{1,0:T(8,128)S(1)}, u32[]{:S(2)}, u32[]{:S(2)}) collective-permute-start(f32[264,128]{1,0:T(8,128)S(1)} %get-tuple-element.60), channel_id=1, source_target_pairs={{0,16},{4,20},{8,24},{12,28},{16,0},{20,4},{24,8},{28,12},{32,48},... | collective-permute-start | bytes 405512 | tf_op jit(solution)/shard_map/ppermute | solution.py:347
  30.3 2.5 %collective-permute-start.9 = (f32[264,128]{1,0:T(8,128)S(1)}, f32[264,128]{1,0:T(8,128)S(1)}, u32[]{:S(2)}, u32[]{:S(2)}) collective-permute-start(f32[264,128]{1,0:T(8,128)S(1)} %get-tuple-element.61), channel_id=1, source_target_pairs={{0,24},{4,28},{8,16},{12,20},{16,8},{20,12},{24,0},{28,4},{32,56},... | collective-permute-start | bytes 405512 | tf_op jit(solution)/shard_map/ppermute | solution.py:347
  32.8 5.9 %collective-permute-done.3.refs_3_ = f32[264,128]{1,0:T(8,128)S(1)} collective-permute-done((f32[264,128]{1,0:T(8,128)S(1)}, f32[264,128]{1,0:T(8,128)S(1)}, u32[]{:S(2)}, u32[]{:S(2)}) %collective-permute-start.3) | collective-permute-done | bytes 135200 | tf_op jit(solution)/shard_map/ppermute | solution.py:347
  38.7 0.6 shard_map.130
  39.3 1.3 collective-permute-start.6
  40.6 1.3 collective-permute-start.5
  41.9 1.3 collective-permute-start.4
  43.2 1.4 collective-permute-done.9.refs_3_.refs_10_
  44.6 0.6 shard_map.131
  45.3 1.4 collective-permute-start.12
  46.7 1.3 collective-permute-start.11
  48.0 22.0 %collective-permute-done.6.refs_6_ = f32[264,128]{1,0:T(8,128)S(1)} collective-permute-done((f32[264,128]{1,0:T(8,128)S(1)}, f32[264,128]{1,0:T(8,128)S(1)}, u32[]{:S(2)}, u32[]{:S(2)}) %collective-permute-start.6) | collective-permute-done | bytes 135200 | tf_op jit(solution)/shard_map/ppermute | solution.py:371
  70.1 1.3 collective-permute-start.10
  71.4 1.3 collective-permute-done.12.refs_13_
  72.7 6.2 %collective-permute-done.11.refs_12_ = f32[264,128]{1,0:T(8,128)S(1)} collective-permute-done((f32[264,128]{1,0:T(8,128)S(1)}, f32[264,128]{1,0:T(8,128)S(1)}, u32[]{:S(2)}, u32[]{:S(2)}) %collective-permute-start.11) | collective-permute-done | bytes 135200 | tf_op jit(solution)/shard_map/ppermute | solution.py:371
  78.9 2.0 %collective-permute-done.10.refs_11_ = f32[264,128]{1,0:T(8,128)S(1)} collective-permute-done((f32[264,128]{1,0:T(8,128)S(1)}, f32[264,128]{1,0:T(8,128)S(1)}, u32[]{:S(2)}, u32[]{:S(2)}) %collective-permute-start.10) | collective-permute-done | bytes 135200 | tf_op jit(solution)/shard_map/ppermute | solution.py:371
  80.9 1.8 %shard_map.132 = (f32[520,128]{1,0:T(8,128)}, f32[520,128]{1,0:T(8,128)}, f32[520,128]{1,0:T(8,128)}, f32[520,128]{1,0:T(8,128)}) custom-call(s32[5]{0:T(128)S(1)} %stack.52.refs_0_.where_ref, f32[264,128]{1,0:T(8,128)S(1)} %get-tuple-element.55.refs_0_, f32[264,128]{1,0:T(8,128)S(1)} %collective-permute-done.1.after_ref.refs_1_, ...), custom_call_target="tpu_custom_call" | custom-call | tf_op jit(solution)/shard_map/pallas_call | solution.py:372
  82.7 1.9 %collective-permute-start.16 = (f32[520,128]{1,0:T(8,128)}, f32[520,128]{1,0:T(8,128)}, u32[]{:S(2)}, u32[]{:S(2)}) collective-permute-start(f32[520,128]{1,0:T(8,128)} %get-tuple-element.65.refs_10_), channel_id=1, source_target_pairs={{0,4},{4,0},{8,12},{12,8},{16,20},{20,16},{24,28},{28,24},{32,36},... | collective-permute-start | bytes 798728 | tf_op jit(solution)/shard_map/ppermute | solution.py:386
  84.6 1.9 %collective-permute-start.15 = (f32[520,128]{1,0:T(8,128)}, f32[520,128]{1,0:T(8,128)}, u32[]{:S(2)}, u32[]{:S(2)}) collective-permute-start(f32[520,128]{1,0:T(8,128)} %get-tuple-element.64), channel_id=1, source_target_pairs={{0,8},{4,12},{8,0},{12,4},{16,24},{20,28},{24,16},{28,20},{32,40},... | collective-permute-start | bytes 798728 | tf_op jit(solution)/shard_map/ppermute | solution.py:373
  86.8 5.3 %shard_map.129 = (f32[128,2048]{1,0:T(8,128)S(1)}, f32[128,2048]{1,0:T(8,128)S(1)}, f32[128,256]{1,0:T(8,128)S(1)}) custom-call(bf16[128,2048]{1,0:T(8,128)(2,1)S(1)} %bitcast.23, bf16[128,2048]{1,0:T(8,128)(2,1)S(1)} %bitcast.30, bf16[128,128]{1,0:T(8,128)(2,1)S(1)} %bitcast.37, bf16[128,128]{1,0:T(8,128)(2,1)S(1)} %bitcast.44, f32[32,128]{1,0:T(8,128)S(1)} %bitcast.51, ...), custom_call_target="tpu_custom_call" | custom-call | tf_op jit(solution)/shard_map/pallas_call | solution.py:351
  92.0 4.1 %shard_map.133 = (bf16[128,2048]{1,0:T(8,128)(2,1)}, bf16[128,2048]{1,0:T(8,128)(2,1)}, f32[32,128]{1,0:T(8,128)}, f32[32,128]{1,0:T(8,128)}, f32[32,128]{1,0:T(8,128)S(1)}, /*index=5*/f32[128,256]{1,0:T(8,128)S(1)}) custom-call(s32[5]{0:T(128)S(1)} %stack.52.refs_0_.where_ref, bf16[128,2048]{1,0:T(8,128)(2,1)S(1)} %bitcast.24, ...), custom_call_target="tpu_custom_call" | custom-call | tf_op jit(solution)/shard_map/pallas_call | solution.py:404
  96.2 2.4 %collective-permute-start.17 = (f32[520,128]{1,0:T(8,128)}, f32[520,128]{1,0:T(8,128)}, u32[]{:S(2)}, u32[]{:S(2)}) collective-permute-start(f32[520,128]{1,0:T(8,128)} %collective-permute-done.15.refs_10_), channel_id=1, source_target_pairs={{0,4},{4,0},{8,12},{12,8},{16,20},{20,16},{24,28},{28,24},{32,36},... | collective-permute-start | bytes 798728 | tf_op jit(solution)/shard_map/ppermute | solution.py:386
  98.6 4.2 %collective-permute-start.14 = (f32[520,128]{1,0:T(8,128)}, f32[520,128]{1,0:T(8,128)}, u32[]{:S(2)}, u32[]{:S(2)}) collective-permute-start(f32[520,128]{1,0:T(8,128)} %get-tuple-element.63), channel_id=1, source_target_pairs={{0,16},{4,20},{8,24},{12,28},{16,0},{20,4},{24,8},{28,12},{32,48},... | collective-permute-start | bytes 798728 | tf_op jit(solution)/shard_map/ppermute | solution.py:373
  102.8 0.1 stack.56.refs_0_
  102.9 1.2 copy-done.7
  104.2 4.1 %shard_map.134 = (bf16[128,2048]{1,0:T(8,128)(2,1)}, bf16[128,2048]{1,0:T(8,128)(2,1)}, f32[32,128]{1,0:T(8,128)}, f32[32,128]{1,0:T(8,128)}, f32[32,128]{1,0:T(8,128)S(1)}, /*index=5*/f32[128,256]{1,0:T(8,128)S(1)}) custom-call(s32[5]{0:T(128)S(1)} %stack.56.refs_0_, ...), custom_call_target="tpu_custom_call", output_to_operand_aliasing={{0}: (17, {}), {1}: (18, {}), {2}: (19, {}), {3}: (20, {}),... | custom-call | tf_op jit(solution)/shard_map/pallas_call | solution.py:404
  108.3 0.7 copy-done.18
  108.9 5.7 %collective-permute-done.14.refs_10_ = f32[520,128]{1,0:T(8,128)} collective-permute-done((f32[520,128]{1,0:T(8,128)}, f32[520,128]{1,0:T(8,128)}, u32[]{:S(2)}, u32[]{:S(2)}) %collective-permute-start.14) | collective-permute-done | bytes 266272 | tf_op jit(solution)/shard_map/ppermute | solution.py:373
  114.6 2.0 %collective-permute-start.18 = (f32[520,128]{1,0:T(8,128)}, f32[520,128]{1,0:T(8,128)}, u32[]{:S(2)}, u32[]{:S(2)}) collective-permute-start(f32[520,128]{1,0:T(8,128)} %collective-permute-done.14.refs_10_), channel_id=1, source_target_pairs={{0,4},{4,0},{8,12},{12,8},{16,20},{20,16},{24,28},{28,24},{32,36},... | collective-permute-start | bytes 798728 | tf_op jit(solution)/shard_map/ppermute | solution.py:386
  116.6 2.7 %collective-permute-start.13 = (f32[520,128]{1,0:T(8,128)}, f32[520,128]{1,0:T(8,128)}, u32[]{:S(2)}, u32[]{:S(2)}) collective-permute-start(f32[520,128]{1,0:T(8,128)} %get-tuple-element.62), channel_id=1, source_target_pairs={{0,24},{4,28},{8,16},{12,20},{16,8},{20,12},{24,0},{28,4},{32,56},... | collective-permute-start | bytes 798728 | tf_op jit(solution)/shard_map/ppermute | solution.py:373
  119.3 0.1 stack.54.refs_0_
  119.4 1.2 copy-done.8
  120.6 0.9 copy-done.19
  121.5 4.1 %shard_map.135 = (bf16[128,2048]{1,0:T(8,128)(2,1)}, bf16[128,2048]{1,0:T(8,128)(2,1)}, f32[32,128]{1,0:T(8,128)}, f32[32,128]{1,0:T(8,128)}, f32[32,128]{1,0:T(8,128)S(1)}, /*index=5*/f32[128,256]{1,0:T(8,128)S(1)}) custom-call(s32[5]{0:T(128)S(1)} %stack.54.refs_0_, ...), custom_call_target="tpu_custom_call", output_to_operand_aliasing={{0}: (17, {}), {1}: (18, {}), {2}: (19, {}), {3}: (20, {}),... | custom-call | tf_op jit(solution)/shard_map/pallas_call | solution.py:404
  125.7 7.6 %collective-permute-done.13.refs_10_ = f32[520,128]{1,0:T(8,128)} collective-permute-done((f32[520,128]{1,0:T(8,128)}, f32[520,128]{1,0:T(8,128)}, u32[]{:S(2)}, u32[]{:S(2)}) %collective-permute-start.13) | collective-permute-done | bytes 266272 | tf_op jit(solution)/shard_map/ppermute | solution.py:373
  133.2 1.9 %collective-permute-start.19 = (f32[520,128]{1,0:T(8,128)}, f32[520,128]{1,0:T(8,128)}, u32[]{:S(2)}, u32[]{:S(2)}) collective-permute-start(f32[520,128]{1,0:T(8,128)} %collective-permute-done.13.refs_10_), channel_id=1, source_target_pairs={{0,4},{4,0},{8,12},{12,8},{16,20},{20,16},{24,28},{28,24},{32,36},... | collective-permute-start | bytes 798728 | tf_op jit(solution)/shard_map/ppermute | solution.py:386
  135.2 1.8 %collective-permute-done.19.refs_11_ = f32[520,128]{1,0:T(8,128)} collective-permute-done((f32[520,128]{1,0:T(8,128)}, f32[520,128]{1,0:T(8,128)}, u32[]{:S(2)}, u32[]{:S(2)}) %collective-permute-start.19) | collective-permute-done | bytes 266272 | tf_op jit(solution)/shard_map/ppermute | solution.py:386
  137.0 1.2 copy-done.9
  138.2 4.1 %shard_map.136 = (bf16[128,2048]{1,0:T(8,128)(2,1)}, bf16[128,2048]{1,0:T(8,128)(2,1)}, f32[32,128]{1,0:T(8,128)}, f32[32,128]{1,0:T(8,128)}, f32[32,128]{1,0:T(...) custom-call(s32[5]{0:T(128)S(1)} %stack.51.refs_0_, ...), custom_call_target="tpu_custom_call", output_to_operand_aliasing={{0}: (17, {}), {1}: (18, {}), {2}: (19, {}), {3}: (20, {}),... | custom-call | tf_op jit(solution)/shard_map/pallas_call | solution.py:404
  142.3 0.1 slice_reduce_fusion
  142.4 2.5 %collective-permute-start.25 = (f32[32]{0:T(128)S(1)}, f32[32]{0:T(128)S(1)}, u32[]{:S(2)}, u32[]{:S(2)}) collective-permute-start(f32[32]{0:T(128)S(1)} %slice_reduce_fusion), channel_id=1, source_target_pairs={{0,384},{128,256},{256,128},{384,0},{1,385},{129,257},{257,129},{3... | collective-permute-start | bytes 392 | tf_op jit(solution)/shard_map/ppermute | solution.py:322
  144.9 4.6 %collective-permute-start.24 = (f32[32]{0:T(128)S(1)}, f32[32]{0:T(128)S(1)}, u32[]{:S(2)}, u32[]{:S(2)}) collective-permute-start(f32[32]{0:T(128)S(1)} %slice_reduce_fusion), channel_id=1, source_target_pairs={{0,256},{128,384},{256,0},{384,128},{1,257},{129,385},{257,1},{385... | collective-permute-start | bytes 392 | tf_op jit(solution)/shard_map/ppermute | solution.py:322
  149.5 2.7 %collective-permute-start.23 = (f32[32]{0:T(128)S(1)}, f32[32]{0:T(128)S(1)}, u32[]{:S(2)}, u32[]{:S(2)}) collective-permute-start(f32[32]{0:T(128)S(1)} %slice_reduce_fusion), channel_id=1, source_target_pairs={{0,128},{128,0},{256,384},{384,256},{1,129},{129,1},{257,385},{385... | collective-permute-start | bytes 392 | tf_op jit(solution)/shard_map/ppermute | solution.py:322
  152.3 3.5 %collective-permute-start.20 = (f32[32,256]{1,0:T(8,128)S(1)}, f32[32,256]{1,0:T(8,128)S(1)}, u32[]{:S(2)}, u32[]{:S(2)}) collective-permute-start(f32[32,256]{1,0:T(8,128)S(1)} %get-tuple-element.93), channel_id=1, source_target_pairs={{0,1},{1,0},{2,3},{3,2},{4,5},{5,4},{6,7},{7,6},{8,9},{9,8},{10,11... | collective-permute-start | bytes 98312 | tf_op jit(solution)/shard_map/ppermute | solution.py:322
  155.8 4.8 %collective-permute-start.21 = (f32[32,256]{1,0:T(8,128)S(1)}, f32[32,256]{1,0:T(8,128)S(1)}, u32[]{:S(2)}, u32[]{:S(2)}) collective-permute-start(f32[32,256]{1,0:T(8,128)S(1)} %get-tuple-element.94), channel_id=1, source_target_pairs={{0,2},{1,3},{2,0},{3,1},{4,6},{5,7},{6,4},{7,5},{8,10},{9,11},{10,... | collective-permute-start | bytes 98312 | tf_op jit(solution)/shard_map/ppermute | solution.py:322
  160.6 2.1 %collective-permute-start.22 = (f32[32,256]{1,0:T(8,128)S(1)}, f32[32,256]{1,0:T(8,128)S(1)}, u32[]{:S(2)}, u32[]{:S(2)}) collective-permute-start(f32[32,256]{1,0:T(8,128)S(1)} %get-tuple-element.95), channel_id=1, source_target_pairs={{0,3},{1,2},{2,1},{3,0},{4,7},{5,6},{6,5},{7,4},{8,11},{9,10},{10,... | collective-permute-start | bytes 98312 | tf_op jit(solution)/shard_map/ppermute | solution.py:322
  162.8 0.5 add_multiply_fusion
  163.3 4.4 %collective-permute-done.22 = f32[32,256]{1,0:T(8,128)S(1)} collective-permute-done((f32[32,256]{1,0:T(8,128)S(1)}, f32[32,256]{1,0:T(8,128)S(1)}, u32[]{:S(2)}, u32[]{:S(2)}) %collective-permute-start.22) | collective-permute-done | bytes 32800 | tf_op jit(solution)/shard_map/ppermute | solution.py:322
  167.6 0.6 slice_bitcast_fusion
  (51 shorter events, 0.4 us)
Async XLA Ops:
  0.8 1.0 copy-start.2
  1.8 1.0 copy-start.4
  2.8 0.8 copy-start.10
  3.6 0.8 copy-start.12
  4.4 0.7 copy-start.14
  5.1 0.7 copy-start.16
  7.7 3.8 %copy-start.1 = (f32[2112,128]{1,0:T(8,128)}, f32[2112,128]{1,0:T(8,128)S(1)}, u32[]{:S(2)}) copy-start(f32[2112,128]{1,0:T(8,128)S(1)} %shard_map.126.refs_14_) | copy-start | bytes 3244036
  7.7 4.6 %collective-permute-start = (f32[2112,128]{1,0:T(8,128)S(1)}, f32[2112,128]{1,0:T(8,128)S(1)}, u32[]{:S(2)}, u32[]{:S(2)}) collective-permute-start(f32[2112,128]{1,0:T(8,128)S(1)} %shard_map.126.refs_14_), channel_id=1, source_target_pairs={{0,4},{4,0},{8,12},{12,8},{16,20},{20,16},{24,28},{28,24},{32,36},... | collective-permute-start | bytes 3244040 | tf_op jit(solution)/shard_map/ppermute | solution.py:341
  11.6 1.4 copy-start
  13.0 17.3 %collective-permute-start.1 = (f32[264,128]{1,0:T(8,128)S(1)}, f32[264,128]{1,0:T(8,128)S(1)}, u32[]{:S(2)}, u32[]{:S(2)}) collective-permute-start(f32[264,128]{1,0:T(8,128)S(1)} %get-tuple-element.52), channel_id=1, source_target_pairs={{0,8},{4,12},{8,0},{12,4},{16,24},{20,28},{24,16},{28,20},{32,40},... | collective-permute-start | bytes 405512 | tf_op jit(solution)/shard_map/ppermute | solution.py:347
  15.0 17.7 %collective-permute-start.2 = (f32[264,128]{1,0:T(8,128)S(1)}, f32[264,128]{1,0:T(8,128)S(1)}, u32[]{:S(2)}, u32[]{:S(2)}) collective-permute-start(f32[264,128]{1,0:T(8,128)S(1)} %get-tuple-element.56), channel_id=1, source_target_pairs={{0,16},{4,20},{8,24},{12,28},{16,0},{20,4},{24,8},{28,12},{32,48},... | collective-permute-start | bytes 405512 | tf_op jit(solution)/shard_map/ppermute | solution.py:347
  20.2 18.4 %collective-permute-start.3 = (f32[264,128]{1,0:T(8,128)S(1)}, f32[264,128]{1,0:T(8,128)S(1)}, u32[]{:S(2)}, u32[]{:S(2)}) collective-permute-start(f32[264,128]{1,0:T(8,128)S(1)} %get-tuple-element.57), channel_id=1, source_target_pairs={{0,24},{4,28},{8,16},{12,20},{16,8},{20,12},{24,0},{28,4},{32,56},... | collective-permute-start | bytes 405512 | tf_op jit(solution)/shard_map/ppermute | solution.py:347
  22.6 19.3 %collective-permute-start.7 = (f32[264,128]{1,0:T(8,128)S(1)}, f32[264,128]{1,0:T(8,128)S(1)}, u32[]{:S(2)}, u32[]{:S(2)}) collective-permute-start(f32[264,128]{1,0:T(8,128)S(1)} %get-tuple-element.59), channel_id=1, source_target_pairs={{0,8},{4,12},{8,0},{12,4},{16,24},{20,28},{24,16},{28,20},{32,40},... | collective-permute-start | bytes 405512 | tf_op jit(solution)/shard_map/ppermute | solution.py:347
  26.0 17.2 %collective-permute-start.8 = (f32[264,128]{1,0:T(8,128)S(1)}, f32[264,128]{1,0:T(8,128)S(1)}, u32[]{:S(2)}, u32[]{:S(2)}) collective-permute-start(f32[264,128]{1,0:T(8,128)S(1)} %get-tuple-element.60), channel_id=1, source_target_pairs={{0,16},{4,20},{8,24},{12,28},{16,0},{20,4},{24,8},{28,12},{32,48},... | collective-permute-start | bytes 405512 | tf_op jit(solution)/shard_map/ppermute | solution.py:347
  30.3 14.3 %collective-permute-start.9 = (f32[264,128]{1,0:T(8,128)S(1)}, f32[264,128]{1,0:T(8,128)S(1)}, u32[]{:S(2)}, u32[]{:S(2)}) collective-permute-start(f32[264,128]{1,0:T(8,128)S(1)} %get-tuple-element.61), channel_id=1, source_target_pairs={{0,24},{4,28},{8,16},{12,20},{16,8},{20,12},{24,0},{28,4},{32,56},... | collective-permute-start | bytes 405512 | tf_op jit(solution)/shard_map/ppermute | solution.py:347
  39.3 30.8 %collective-permute-start.6 = (f32[264,128]{1,0:T(8,128)S(1)}, f32[264,128]{1,0:T(8,128)S(1)}, u32[]{:S(2)}, u32[]{:S(2)}) collective-permute-start(f32[264,128]{1,0:T(8,128)S(1)} %shard_map.130), channel_id=1, source_target_pairs={{4,100},{12,108},{20,116},{28,124},{36,68},{44,76},{52,84},{60,92}... | collective-permute-start | bytes 405512 | tf_op jit(solution)/shard_map/ppermute | solution.py:371
  40.6 30.8 %collective-permute-start.5 = (f32[264,128]{1,0:T(8,128)S(1)}, f32[264,128]{1,0:T(8,128)S(1)}, u32[]{:S(2)}, u32[]{:S(2)}) collective-permute-start(f32[264,128]{1,0:T(8,128)S(1)} %shard_map.130), channel_id=1, source_target_pairs={{4,68},{12,76},{20,84},{28,92},{36,100},{44,108},{52,116},{60,124}... | collective-permute-start | bytes 405512 | tf_op jit(solution)/shard_map/ppermute | solution.py:371
  41.9 29.5 %collective-permute-start.4 = (f32[264,128]{1,0:T(8,128)S(1)}, f32[264,128]{1,0:T(8,128)S(1)}, u32[]{:S(2)}, u32[]{:S(2)}) collective-permute-start(f32[264,128]{1,0:T(8,128)S(1)} %shard_map.130), channel_id=1, source_target_pairs={{4,36},{12,44},{20,52},{28,60},{32,0},{40,8},{48,16},{56,24},{68,1... | collective-permute-start | bytes 405512 | tf_op jit(solution)/shard_map/ppermute | solution.py:371
  45.2 41.3 %copy-start.20 = (f32[32]{0:T(128)S(1)}, f32[32]{0:T(128)}, u32[]{:S(2)}) copy-start(f32[32]{0:T(128)} %param.13) | copy-start | bytes 388
  45.2 41.5 %copy-start.3 = (bf16[1,128,2048]{2,1,0:T(8,128)(2,1)S(1)}, bf16[1,128,2048]{2,1,0:T(8,128)(2,1)}, u32[]{:S(2)}) copy-start(bf16[1,128,2048]{2,1,0:T(8,128)(2,1)} %param.7) | copy-start | bytes 1572868
  45.2 41.5 %copy-start.5 = (bf16[1,128,2048]{2,1,0:T(8,128)(2,1)S(1)}, bf16[1,128,2048]{2,1,0:T(8,128)(2,1)}, u32[]{:S(2)}) copy-start(bf16[1,128,2048]{2,1,0:T(8,128)(2,1)} %param.8) | copy-start | bytes 1572868
  45.2 41.5 %copy-start.11 = (bf16[1,128,128]{2,1,0:T(8,128)(2,1)S(1)}, bf16[1,128,128]{2,1,0:T(8,128)(2,1)}, u32[]{:S(2)}) copy-start(bf16[1,128,128]{2,1,0:T(8,128)(2,1)} %param.9) | copy-start | bytes 98308
  45.3 41.5 %copy-start.13 = (bf16[1,128,128]{2,1,0:T(8,128)(2,1)S(1)}, bf16[1,128,128]{2,1,0:T(8,128)(2,1)}, u32[]{:S(2)}) copy-start(bf16[1,128,128]{2,1,0:T(8,128)(2,1)} %param.10) | copy-start | bytes 98308
  45.3 41.5 %copy-start.15 = (f32[1,32,128]{2,1,0:T(8,128)S(1)}, f32[1,32,128]{2,1,0:T(8,128)}, u32[]{:S(2)}) copy-start(f32[1,32,128]{2,1,0:T(8,128)} %param.11) | copy-start | bytes 49156
  45.3 41.5 %copy-start.17 = (f32[1,32,128]{2,1,0:T(8,128)S(1)}, f32[1,32,128]{2,1,0:T(8,128)}, u32[]{:S(2)}) copy-start(f32[1,32,128]{2,1,0:T(8,128)} %param.12) | copy-start | bytes 49156
  45.3 27.4 %collective-permute-start.12 = (f32[264,128]{1,0:T(8,128)S(1)}, f32[264,128]{1,0:T(8,128)S(1)}, u32[]{:S(2)}, u32[]{:S(2)}) collective-permute-start(f32[264,128]{1,0:T(8,128)S(1)} %shard_map.131), channel_id=1, source_target_pairs={{4,100},{12,108},{20,116},{28,124},{36,68},{44,76},{52,84},{60,92}... | collective-permute-start | bytes 405512 | tf_op jit(solution)/shard_map/ppermute | solution.py:371
  46.7 32.2 %collective-permute-start.11 = (f32[264,128]{1,0:T(8,128)S(1)}, f32[264,128]{1,0:T(8,128)S(1)}, u32[]{:S(2)}, u32[]{:S(2)}) collective-permute-start(f32[264,128]{1,0:T(8,128)S(1)} %shard_map.131), channel_id=1, source_target_pairs={{4,68},{12,76},{20,84},{28,92},{36,100},{44,108},{52,116},{60,124}... | collective-permute-start | bytes 405512 | tf_op jit(solution)/shard_map/ppermute | solution.py:371
  70.1 10.8 %collective-permute-start.10 = (f32[264,128]{1,0:T(8,128)S(1)}, f32[264,128]{1,0:T(8,128)S(1)}, u32[]{:S(2)}, u32[]{:S(2)}) collective-permute-start(f32[264,128]{1,0:T(8,128)S(1)} %shard_map.131), channel_id=1, source_target_pairs={{4,36},{12,44},{20,52},{28,60},{32,0},{40,8},{48,16},{56,24},{68,1... | collective-permute-start | bytes 405512 | tf_op jit(solution)/shard_map/ppermute | solution.py:371
  82.7 9.3 %collective-permute-start.16 = (f32[520,128]{1,0:T(8,128)}, f32[520,128]{1,0:T(8,128)}, u32[]{:S(2)}, u32[]{:S(2)}) collective-permute-start(f32[520,128]{1,0:T(8,128)} %get-tuple-element.65.refs_10_), channel_id=1, source_target_pairs={{0,4},{4,0},{8,12},{12,8},{16,20},{20,16},{24,28},{28,24},{32,36},... | collective-permute-start | bytes 798728 | tf_op jit(solution)/shard_map/ppermute | solution.py:386
  84.6 11.6 %collective-permute-start.15 = (f32[520,128]{1,0:T(8,128)}, f32[520,128]{1,0:T(8,128)}, u32[]{:S(2)}, u32[]{:S(2)}) collective-permute-start(f32[520,128]{1,0:T(8,128)} %get-tuple-element.64), channel_id=1, source_target_pairs={{0,8},{4,12},{8,0},{12,4},{16,24},{20,28},{24,16},{28,20},{32,40},... | collective-permute-start | bytes 798728 | tf_op jit(solution)/shard_map/ppermute | solution.py:373
  92.0 4.1 %copy-start.6 = (f32[128,2048]{1,0:T(8,128)}, f32[128,2048]{1,0:T(8,128)S(1)}, u32[]{:S(2)}) copy-start(f32[128,2048]{1,0:T(8,128)S(1)} %get-tuple-element.54.refs_4_) | copy-start | bytes 3145732
  96.2 6.8 %collective-permute-start.17 = (f32[520,128]{1,0:T(8,128)}, f32[520,128]{1,0:T(8,128)}, u32[]{:S(2)}, u32[]{:S(2)}) collective-permute-start(f32[520,128]{1,0:T(8,128)} %collective-permute-done.15.refs_10_), channel_id=1, source_target_pairs={{0,4},{4,0},{8,12},{12,8},{16,20},{20,16},{24,28},{28,24},{32,36},... | collective-permute-start | bytes 798728 | tf_op jit(solution)/shard_map/ppermute | solution.py:386
  98.6 16.0 %collective-permute-start.14 = (f32[520,128]{1,0:T(8,128)}, f32[520,128]{1,0:T(8,128)}, u32[]{:S(2)}, u32[]{:S(2)}) collective-permute-start(f32[520,128]{1,0:T(8,128)} %get-tuple-element.63), channel_id=1, source_target_pairs={{0,16},{4,20},{8,24},{12,28},{16,0},{20,4},{24,8},{28,12},{32,48},... | collective-permute-start | bytes 798728 | tf_op jit(solution)/shard_map/ppermute | solution.py:373
  102.9 1.2 copy-start.7
  108.3 0.7 copy-start.18
  114.6 4.8 %collective-permute-start.18 = (f32[520,128]{1,0:T(8,128)}, f32[520,128]{1,0:T(8,128)}, u32[]{:S(2)}, u32[]{:S(2)}) collective-permute-start(f32[520,128]{1,0:T(8,128)} %collective-permute-done.14.refs_10_), channel_id=1, source_target_pairs={{0,4},{4,0},{8,12},{12,8},{16,20},{20,16},{24,28},{28,24},{32,36},... | collective-permute-start | bytes 798728 | tf_op jit(solution)/shard_map/ppermute | solution.py:386
  116.6 16.7 %collective-permute-start.13 = (f32[520,128]{1,0:T(8,128)}, f32[520,128]{1,0:T(8,128)}, u32[]{:S(2)}, u32[]{:S(2)}) collective-permute-start(f32[520,128]{1,0:T(8,128)} %get-tuple-element.62), channel_id=1, source_target_pairs={{0,24},{4,28},{8,16},{12,20},{16,8},{20,12},{24,0},{28,4},{32,56},... | collective-permute-start | bytes 798728 | tf_op jit(solution)/shard_map/ppermute | solution.py:373
  119.4 1.2 copy-start.8
  120.6 0.9 copy-start.19
  133.2 3.8 %collective-permute-start.19 = (f32[520,128]{1,0:T(8,128)}, f32[520,128]{1,0:T(8,128)}, u32[]{:S(2)}, u32[]{:S(2)}) collective-permute-start(f32[520,128]{1,0:T(8,128)} %collective-permute-done.13.refs_10_), channel_id=1, source_target_pairs={{0,4},{4,0},{8,12},{12,8},{16,20},{20,16},{24,28},{28,24},{32,36},... | collective-permute-start | bytes 798728 | tf_op jit(solution)/shard_map/ppermute | solution.py:386
  137.0 1.2 copy-start.9
  142.4 18.2 %collective-permute-start.25 = (f32[32]{0:T(128)S(1)}, f32[32]{0:T(128)S(1)}, u32[]{:S(2)}, u32[]{:S(2)}) collective-permute-start(f32[32]{0:T(128)S(1)} %slice_reduce_fusion), channel_id=1, source_target_pairs={{0,384},{128,256},{256,128},{384,0},{1,385},{129,257},{257,129},{3... | collective-permute-start | bytes 392 | tf_op jit(solution)/shard_map/ppermute | solution.py:322
  144.9 17.8 %collective-permute-start.24 = (f32[32]{0:T(128)S(1)}, f32[32]{0:T(128)S(1)}, u32[]{:S(2)}, u32[]{:S(2)}) collective-permute-start(f32[32]{0:T(128)S(1)} %slice_reduce_fusion), channel_id=1, source_target_pairs={{0,256},{128,384},{256,0},{384,128},{1,257},{129,385},{257,1},{385... | collective-permute-start | bytes 392 | tf_op jit(solution)/shard_map/ppermute | solution.py:322
  149.5 13.2 %collective-permute-start.23 = (f32[32]{0:T(128)S(1)}, f32[32]{0:T(128)S(1)}, u32[]{:S(2)}, u32[]{:S(2)}) collective-permute-start(f32[32]{0:T(128)S(1)} %slice_reduce_fusion), channel_id=1, source_target_pairs={{0,128},{128,0},{256,384},{384,256},{1,129},{129,1},{257,385},{385... | collective-permute-start | bytes 392 | tf_op jit(solution)/shard_map/ppermute | solution.py:322
  152.3 11.0 %collective-permute-start.20 = (f32[32,256]{1,0:T(8,128)S(1)}, f32[32,256]{1,0:T(8,128)S(1)}, u32[]{:S(2)}, u32[]{:S(2)}) collective-permute-start(f32[32,256]{1,0:T(8,128)S(1)} %get-tuple-element.93), channel_id=1, source_target_pairs={{0,1},{1,0},{2,3},{3,2},{4,5},{5,4},{6,7},{7,6},{8,9},{9,8},{10,11... | collective-permute-start | bytes 98312 | tf_op jit(solution)/shard_map/ppermute | solution.py:322
  155.8 7.5 %collective-permute-start.21 = (f32[32,256]{1,0:T(8,128)S(1)}, f32[32,256]{1,0:T(8,128)S(1)}, u32[]{:S(2)}, u32[]{:S(2)}) collective-permute-start(f32[32,256]{1,0:T(8,128)S(1)} %get-tuple-element.94), channel_id=1, source_target_pairs={{0,2},{1,3},{2,0},{3,1},{4,6},{5,7},{6,4},{7,5},{8,10},{9,11},{10,... | collective-permute-start | bytes 98312 | tf_op jit(solution)/shard_map/ppermute | solution.py:322
  160.6 7.0 %collective-permute-start.22 = (f32[32,256]{1,0:T(8,128)S(1)}, f32[32,256]{1,0:T(8,128)S(1)}, u32[]{:S(2)}, u32[]{:S(2)}) collective-permute-start(f32[32,256]{1,0:T(8,128)S(1)} %get-tuple-element.95), channel_id=1, source_target_pairs={{0,3},{1,2},{2,1},{3,0},{4,7},{5,6},{6,5},{7,4},{8,11},{9,10},{10,... | collective-permute-start | bytes 98312 | tf_op jit(solution)/shard_map/ppermute | solution.py:322

commit v3 on v2

v3 whole, which is shorter than its diff:
```python
import math

import jax
import jax.numpy as jnp
from jax import lax
from jax.experimental import pallas as pl
from jax.experimental.pallas import tpu as pltpu
from jax.sharding import PartitionSpec as P

F32 = jnp.float32
BF16 = jnp.bfloat16
HIGHEST = lax.Precision.HIGHEST
TOK = 128
HEADS = 32
PH = 64
NS = 128
FEATS = HEADS * PH
QH = 8
QR = QH * PH
PIECE = QR + 2 * QH
NEAR = QR + QH
SIDE = 2 * HEADS
VMEM_LIMIT = 48 * 1024 * 1024


def iota(shape, dim):
    return lax.broadcasted_iota(jnp.int32, shape, dim)


def split(value):
    high = value.astype(BF16)
    low = (value - high.astype(F32)).astype(BF16)
    return high, low


def dot(a, b, ca, cb, precision=None):
    return lax.dot_general(a, b, (((ca,), (cb,)), ((), ())), preferred_element_type=F32, precision=precision)


def running_sum(logs):
    upto = (iota((TOK, TOK), 0) <= iota((TOK, TOK), 1)).astype(F32)
    return dot(logs, upto, 1, 0, HIGHEST)


def expander(heads, first, width):
    row = iota((2 * heads, width), 0)
    row = jnp.where(row >= heads, row - heads, row)
    return (row == (iota((2 * heads, width), 1) + first) // PH).astype(F32).astype(BF16)


def spread_heads(factors, first, width):
    high, low = split(factors.T)
    return dot(jnp.concatenate([high, low], axis=1), expander(factors.shape[0], first, width), 1, 0)


def gate(flag, value):
    return jnp.where(flag, value, 0.0)


def states_kernel(own, where_ref, x_ref, g_ref, b_ref, c_ref, step_ref, log_ref, out_ref, *scratch):
    if scratch:
        held, sems = scratch[:6], scratch[6]
        copies = [
            pltpu.make_async_copy(ref, slot, sems.at[i])
            for i, (ref, slot) in enumerate(zip((x_ref, g_ref, b_ref, c_ref, step_ref, log_ref), held, strict=True))
        ]
        for copy in copies:
            copy.start()
        for copy in copies:
            copy.wait()
        x_ref, g_ref, b_ref, c_ref, step_ref, log_ref = held
    cum = running_sum(log_ref[...])

    def summed(values_ref, factors, map_ref):
        doubled = jnp.concatenate([map_ref[...], map_ref[...]], axis=0)
        for first in range(0, FEATS, QR):
            weighted = values_ref[:, first : first + QR].astype(F32) * spread_heads(factors, first, QR)
            high, low = split(weighted)
            out_ref[first : first + QR, :] = dot(jnp.concatenate([high, low], axis=0), doubled, 0, 0)

    forward = where_ref[0] == (1 if own else 0)

    @pl.when(forward)
    def _():
        summed(x_ref, step_ref[...] * jnp.exp(cum[:, TOK - 1 : TOK] - cum), b_ref)

    @pl.when(jnp.logical_not(forward))
    def _():
        summed(g_ref, jnp.exp(cum), c_ref)

    out_ref[FEATS : FEATS + HEADS, :] = jnp.broadcast_to(cum[:, TOK - 1 : TOK], (HEADS, NS))
    products = jnp.sum(x_ref[...].astype(F32) * g_ref[...].astype(F32), axis=0, keepdims=True)
    owner = (iota((HEADS, FEATS), 1) // PH == iota((HEADS, FEATS), 0)).astype(F32)
    skips = jnp.sum(owner * products, axis=1, keepdims=True)
    out_ref[FEATS + HEADS : FEATS + SIDE, :] = jnp.broadcast_to(skips, (HEADS, NS))


def chip_kernel(where_ref, got_ref, own_ref, *out_refs):
    place = where_ref[2]
    for k, out_ref in enumerate(out_refs):
        quarter = jnp.bitwise_xor(place, k)
        rows = pl.ds(pl.multiple_of(FEATS + quarter * QH, QH), QH)
        logs, got_logs = own_ref[rows, :], got_ref[rows, :]
        decay = jnp.exp(logs)
        for j in range(QH):
            rows = pl.ds(pl.multiple_of(quarter * QR + j * PH, PH), PH)
            out_ref[j * PH : (j + 1) * PH, :] = decay[j : j + 1, :] * got_ref[rows, :] + own_ref[rows, :]
        out_ref[QR : QR + QH, :] = logs + got_logs
        rows = pl.ds(pl.multiple_of(FEATS + HEADS + quarter * QH, QH), QH)
        out_ref[QR + QH : PIECE, :] = own_ref[rows, :] + got_ref[rows, :]


def group_kernel(where_ref, *refs):
    got, out_ref, parts_ref = refs[:4], refs[4], refs[5]
    forward = where_ref[0] == 1
    place = where_ref[2]
    for k in range(4):
        parts_ref[pl.ds(pl.multiple_of(jnp.bitwise_xor(place, k) * PIECE, 8), PIECE), :] = got[k][...]
    logs = [parts_ref[k * PIECE + QR : k * PIECE + QR + QH, :] for k in range(4)]
    none = jnp.zeros_like(logs[0])
    weights = [jnp.exp(jnp.where(forward, sum(logs[k + 1 :], none), sum(logs[:k], none))) for k in range(4)]
    for j in range(QH):
        terms = [
            weights[k][j : j + 1, :] * parts_ref[k * PIECE + j * PH : k * PIECE + (j + 1) * PH, :] for k in range(4)
        ]
        out_ref[j * PH : (j + 1) * PH, :] = (terms[0] + terms[1]) + (terms[2] + terms[3])
    side = [parts_ref[k * PIECE + QR : (k + 1) * PIECE, :] for k in range(4)]
    out_ref[QR:PIECE, :] = (side[0] + side[1]) + (side[2] + side[3])


def prefix_kernel(where_ref, parts_ref, *refs):
    forward = where_ref[0] == 1
    me = where_ref[1]
    group = [jnp.bitwise_xor(me, k) for k in range(4)]
    group = [jnp.where(forward, p, 3 - p) for p in group]
    tops, out_ref = refs[:3], refs[3]
    top_logs = [t[QR : QR + QH, :] for t in tops]
    weights = []
    for k in range(3):
        between = [
            gate((group[k + 1] < group[i + 1]) & (group[i + 1] < group[0]), top_logs[i]) for i in range(3) if i != k
        ]
        weights.append(jnp.exp(between[0] + between[1]))
    decays = [jnp.exp(parts_ref[k * PIECE + QR : k * PIECE + QR + QH, :]) for k in range(4)]

    def scan(sequence, carries_own):
        for j in range(QH):
            rows = slice(j * PH, (j + 1) * PH)
            at = slice(j, j + 1)
            state = weights[0][at, :] * tops[0][rows, :] + weights[1][at, :] * tops[1][rows, :]
            state = state + weights[2][at, :] * tops[2][rows, :]
            for k in sequence:
                out_ref[k * NEAR + j * PH : k * NEAR + (j + 1) * PH, :] = state
                if k != sequence[-1]:
                    state = decays[k][at, :] * state + parts_ref[k * PIECE + j * PH : k * PIECE + (j + 1) * PH, :]
        skips = tops[0][QR + QH :, :] + tops[1][QR + QH :, :] + tops[2][QR + QH :, :]
        if carries_own:
            for k in range(4):
                skips = skips + parts_ref[k * PIECE + QR + QH : (k + 1) * PIECE, :]
        for k in range(4):
            out_ref[k * NEAR + QR : (k + 1) * NEAR, :] = skips

    @pl.when(forward)
    def _():
        scan((0, 1, 2, 3), True)

    @pl.when(jnp.logical_not(forward))
    def _():
        scan((3, 2, 1, 0), False)


def slab_kernel(x_ref, g_ref, b_ref, c_ref, step_ref, log_ref, after_ref, within_ref, back_ref, maps_ref, summed):
    quarter = pl.program_id(0)

    @pl.when(quarter == 0)
    def _():
        summed[...] = jnp.zeros_like(summed)

    affinity = dot(c_ref[...], b_ref[...], 1, 1)
    causal = iota((TOK, TOK), 0) >= iota((TOK, TOK), 1)
    cum = running_sum(log_ref[...])
    columns = cum.T
    left = iota((TOK, 2 * PH), 1) < PH
    zero = jnp.zeros((TOK, 2 * PH), BF16)
    for pair in range(QH // 2):
        lanes = slice(pair * 2 * PH, (pair + 1) * 2 * PH)
        x, g = x_ref[:, lanes], g_ref[:, lanes]
        xs = (jnp.where(left, x, zero), jnp.where(left, zero, x))
        gs = (jnp.where(left, g, zero), jnp.where(left, zero, g))
        mixes = []
        for side in range(2):
            j = 2 * pair + side
            gap = columns[:, j : j + 1] - cum[j : j + 1, :]
            decays = jnp.exp(jnp.where(causal, gap, -1e30)) * step_ref[j : j + 1, :]
            summed[...] += decays * dot(gs[side], x, 1, 1)
            mixes.extend(split(affinity * decays))
        within_ref[:, lanes] = dot(
            jnp.concatenate(mixes, axis=1), jnp.concatenate([xs[0], xs[0], xs[1], xs[1]], axis=0), 1, 0
        )
        back_ref[:, lanes] = dot(
            jnp.concatenate(mixes, axis=0), jnp.concatenate([gs[0], gs[0], gs[1], gs[1]], axis=0), 0, 0
        )

    @pl.when(quarter == pl.num_programs(0) - 1)
    def _():
        high, low = split(summed[...])
        b, c = b_ref[...], c_ref[...]
        maps_ref[:, :NS] = dot(jnp.concatenate([high, low], axis=0), jnp.concatenate([c, c], axis=0), 0, 0)
        maps_ref[:, NS:] = dot(jnp.concatenate([high, low], axis=1), jnp.concatenate([b, b], axis=0), 1, 0)


def at_slab(quarter, near_ref, first_ref):
    decay = jnp.exp(first_ref[FEATS + quarter * QH : FEATS + (quarter + 1) * QH, :])
    slots = []
    for j in range(QH):
        near = near_ref[quarter * NEAR + j * PH : quarter * NEAR + (j + 1) * PH, :]
        first = quarter * QR + j * PH
        slots.append(decay[j : j + 1, :] * near + first_ref[first : first + PH, :])
    return jnp.concatenate(slots, axis=0)


def weighted_sum(forward, x_ref, g_ref, step_ref, log_ref, state_of):
    cum = running_sum(log_ref[...])
    factors = jnp.where(forward, jnp.exp(cum), step_ref[...] * jnp.exp(cum[:, TOK - 1 : TOK] - cum))
    total = jnp.zeros((TOK, NS), F32)
    for quarter in range(4):
        lanes = slice(quarter * QR, (quarter + 1) * QR)
        values = jnp.where(forward, g_ref[:, lanes].astype(F32), x_ref[:, lanes].astype(F32))
        high, low = split(values * spread_heads(factors, quarter * QR, QR))
        state_high, state_low = split(state_of(quarter))
        total = total + (dot(high, state_high, 1, 0) + (dot(low, state_high, 1, 0) + dot(high, state_low, 1, 0)))
    return total


def near_maps_kernel(where_ref, x_ref, g_ref, step_ref, log_ref, near_ref, first_ref, out_ref):
    out_ref[...] = weighted_sum(
        where_ref[0] == 1, x_ref, g_ref, step_ref, log_ref, lambda quarter: at_slab(quarter, near_ref, first_ref)
    )


def far_maps_kernel(
    where_ref, x_ref, g_ref, step_ref, log_ref, near_ref, far_ref, maps_in_ref, near_maps_ref, maps_ref, skip_ref
):
    forward = where_ref[0] == 1
    other = weighted_sum(
        where_ref[0] == 0, x_ref, g_ref, step_ref, log_ref,
        lambda quarter: far_ref[quarter * NEAR : quarter * NEAR + QR, :],
    )
    for quarter in range(4):
        side = slice(quarter * NEAR + QR, (quarter + 1) * NEAR)
        skip_ref[quarter * QH : (quarter + 1) * QH, :] = near_ref[side, :] + far_ref[side, :]
    mine = near_maps_ref[...]
    maps_ref[:, :NS] = maps_in_ref[:, :NS] + jnp.where(forward, other, mine)
    maps_ref[:, NS:] = maps_in_ref[:, NS:] + jnp.where(forward, mine, other)


def cross_kernel(
    where_ref, x_ref, g_ref, within_ref, back_ref, step_ref, log_ref, gain_ref, b_ref, c_ref,
    near_ref, far_ref, first_ref, send_ref, own_ref,
    mixed_ref, ginputs_ref, gstep_ref, gdecay_ref,
):
    forward = where_ref[0] == 1
    cums = running_sum(log_ref[...])
    b, c = b_ref[...], c_ref[...]
    two_b, two_c = jnp.concatenate([b, b], axis=1), jnp.concatenate([c, c], axis=1)
    owner = (iota((QR, QH), 0) // PH == iota((QR, QH), 1)).astype(F32).astype(BF16)
    doubled = jnp.concatenate([owner, owner], axis=0)
    after = (iota((TOK, TOK), 0) >= iota((TOK, TOK), 1)).astype(F32)

    def by_head(values):
        return dot(jnp.concatenate(split(values), axis=1), doubled, 1, 0).T

    for quarter in range(4):
        lanes = slice(quarter * QR, (quarter + 1) * QR)
        heads = slice(quarter * QH, (quarter + 1) * QH)
        cum, steps = cums[heads, :], step_ref[heads, :]
        through = jnp.exp(cum[:, TOK - 1 : TOK])
        scanned = at_slab(quarter, near_ref, first_ref)
        other = far_ref[quarter * NEAR : quarter * NEAR + QR, :]
        ent = jnp.where(forward, scanned, other)
        arr = jnp.where(forward, other, scanned)
        x, g = x_ref[:, lanes].astype(F32), g_ref[:, lanes].astype(F32)
        starts = spread_heads(jnp.exp(cum), 0, QR)
        sources = spread_heads(steps * jnp.exp(cum[:, TOK - 1 : TOK] - cum), 0, QR)
        output = within_ref[:, lanes] + dot(two_c, jnp.concatenate(split(ent), axis=1), 1, 1) * starts
        back = back_ref[:, lanes] + dot(two_b, jnp.concatenate(split(arr), axis=1), 1, 1) * sources
        gain = gain_ref[:, lanes]
        mixed_ref[:, lanes] = (output + gain * x).astype(BF16)
        ginputs_ref[:, lanes] = (back + gain * g).astype(BF16)
        steps_part = x * back
        gstep_ref[heads, :] = by_head(steps_part) / steps
        change = by_head(g * output - steps_part)
        edges = []
        for j in range(QH):
            rows = slice(quarter * QR + j * PH, quarter * QR + (j + 1) * PH)
            local = jnp.where(forward, own_ref[rows, :], send_ref[rows, :])
            rows = slice(j * PH, (j + 1) * PH)
            leaving = local + through[j : j + 1, :] * ent[rows, :]
            edges.append(jnp.sum(arr[rows, :] * leaving, axis=0, keepdims=True))
        edge = jnp.sum(jnp.concatenate(edges, axis=0), axis=1, keepdims=True)
        change = change + jnp.where(iota((QH, TOK), 1) == TOK - 1, edge, 0.0)
        gdecay_ref[heads, :] = dot(change, after, 1, 0, HIGHEST)


PARAMS = pltpu.CompilerParams(vmem_limit_bytes=VMEM_LIMIT)


def call(kernel, outs, n_in, space=pltpu.VMEM, scratch=()):
    smem = pl.BlockSpec(memory_space=pltpu.SMEM)
    vmem = pl.BlockSpec(memory_space=pltpu.VMEM)
    return pl.pallas_call(
        kernel,
        out_shape=[jax.ShapeDtypeStruct(s, k) for s, k in outs],
        in_specs=[smem] + [pl.BlockSpec(memory_space=space)] * n_in,
        out_specs=[vmem] * len(outs),
        scratch_shapes=list(scratch),
        compiler_params=PARAMS,
    )


def by_quarter(kernel, in_specs, out_specs, out_shape, scratch=()):
    return pl.pallas_call(
        kernel,
        grid=(HEADS // QH,),
        in_specs=in_specs,
        out_specs=out_specs,
        out_shape=out_shape,
        scratch_shapes=list(scratch),
        compiler_params=PARAMS,
    )


def core_pairs(n):
    return [(i, i ^ 1) for i in range(n)]


def chip_pairs(n, k):
    return [(i, i ^ (2 * k)) for i in range(n)]


def group_pairs(n, k):
    pairs = [(i, i ^ (8 * k)) for i in range(n)]
    return [(i, j) for i, j in pairs if (j > i) == (i % 2 == 1)]


def partners(value, axis, k):
    n = lax.axis_size(axis)
    return lax.ppermute(value, axis, [(i, i ^ k) for i in range(n) if i ^ k < n])


def shards(inputs, grad_out, input_map, output_map, step_size, log_decay, skip_gain):
    n = lax.axis_size("ctx")
    me = lax.axis_index("ctx")
    x, g = inputs[0], grad_out[0]
    b, c = input_map[0], output_map[0]
    steps, logs = step_size[0], log_decay[0]
    where = jnp.stack([me % 2, me // 8, (me // 2) % 4]).astype(jnp.int32)
    gains = jnp.repeat(skip_gain, PH)[None]
    groups = [[8 * j + 2 * i + core for i in range(4)] for j in range(n // 8) for core in range(2)]
    slab_inputs = (x, g, b, c, steps, logs)

    def states(own):
        if own:
            scratch, space = (), pltpu.VMEM
        else:
            scratch = [pltpu.VMEM(v.shape, v.dtype) for v in slab_inputs] + [pltpu.SemaphoreType.DMA((6,))]
            space = pltpu.HBM
        kernel = lambda *refs: states_kernel(own, *refs)
        return call(kernel, [((FEATS + SIDE, NS), F32)], 6, space, scratch)(where, *slab_inputs)[0]

    send = states(False)
    first = lax.ppermute(send, "ctx", core_pairs(n))
    own = states(True)
    parts = call(chip_kernel, [((PIECE, NS), F32)] * 4, 2)(where, first, own)
    mine = [parts[0]] + [lax.ppermute(parts[k], "ctx", chip_pairs(n, k)) for k in range(1, 4)]

    cols = pl.BlockSpec((TOK, QR), lambda i: (0, i))
    rows = pl.BlockSpec((QH, TOK), lambda i: (i, 0))
    fixed = lambda r, l: pl.BlockSpec((r, l), lambda i: (0, 0))
    wide = jax.ShapeDtypeStruct((TOK, FEATS), F32)
    within, back, maps = by_quarter(
        slab_kernel,
        [cols, cols, fixed(TOK, NS), fixed(TOK, NS), rows, rows, fixed(8, NS)],
        [cols, cols, fixed(TOK, 2 * NS)],
        [wide, wide, jax.ShapeDtypeStruct((TOK, 2 * NS), F32)],
        [pltpu.VMEM((TOK, TOK), F32)],
    )(*slab_inputs, parts[0])

    total, placed = call(group_kernel, [((PIECE, NS), F32), ((4 * PIECE, NS), F32)], 4)(where, *mine)
    tops = [lax.ppermute(total, "ctx", group_pairs(n, k)) for k in range(1, 4)]
    tops[-1], within, back, maps = lax.optimization_barrier((tops[-1], within, back, maps))
    (ready,) = call(prefix_kernel, [((4 * NEAR, NS), F32)], 4)(where, placed, *tops)
    near = lax.all_to_all(ready, "ctx", 0, 0, axis_index_groups=groups, tiled=True)
    far = lax.ppermute(near, "ctx", core_pairs(n))
    (near_maps,) = call(near_maps_kernel, [((TOK, NS), F32)], 6)(where, x, g, steps, logs, near, first)
    maps, skips = call(far_maps_kernel, [((TOK, 2 * NS), F32), ((HEADS, NS), F32)], 8)(
        where, x, g, steps, logs, near, far, maps, near_maps
    )
    tp = lax.axis_size("tp")
    swapped = lax.all_to_all(maps.reshape(tp, TOK // tp, 2 * NS), "tp", 0, 0)
    outs = [((TOK, FEATS), BF16)] * 2 + [((HEADS, TOK), F32)] * 2
    mixed, ginputs, gstep, gdecay = call(cross_kernel, outs, 14)(
        where, x, g, within, back, steps, logs, gains, b, c, near, far, first, send, own
    )
    reduced = jnp.sum(swapped, axis=0)
    skip = skips[:, 0]
    skip_total = skip + partners(skip, "dp", 1) + partners(skip, "dp", 2) + partners(skip, "dp", 3)
    factor = 1.0 / math.sqrt(lax.axis_size("dp") * TOK * n * PH)
    return (
        mixed[None],
        ginputs[None],
        gstep[None],
        gdecay[None],
        reduced[None, :, :NS],
        reduced[None, :, NS:],
        skip_total * factor,
    )


def solution(mesh):
    in_specs = (
        P("dp", "ctx", "tp"),
        P("dp", "ctx", "tp"),
        P("dp", "ctx", None),
        P("dp", "ctx", None),
        P("dp", "tp", "ctx"),
        P("dp", "tp", "ctx"),
        P("tp"),
    )
    out_specs = (
        P("dp", "ctx", "tp"),
        P("dp", "ctx", "tp"),
        P("dp", "tp", "ctx"),
        P("dp", "tp", "ctx"),
        P("dp", ("ctx", "tp"), None),
        P("dp", ("ctx", "tp"), None),
        P("tp"),
    )
    return jax.shard_map(shards, mesh=mesh, in_specs=in_specs, out_specs=out_specs, check_vma=False)
```

time: 170 us -> 144 us (0.85)
  the two profiles are of different devices: /device:TPU:36 before, /device:TPU:1 now
where the time goes in v3:
time: 144 us; the launch traced here: 143 us
  starting transfers between devices  51.2 us (36%)
  blocking collectives  31 us (22%)
  waiting for transfers between devices  25.7 us (18%)
  Pallas kernels  23.7 us (16%)
  local copies, waits for them, and re-layouts  9.47 us (7%)
    all_to_all x1, blocking collectives, shards(): lax.all_to_all(ready, 'ctx', 0, 0, axis_index_groups=groups, tiled=True)  31 us
    ppermute x3, starting transfers between devices, shards(): tops = [lax.ppermute(total, 'ctx', group_pairs(n, k)) for k in range(1, 4)]  15.8 us
    ppermute x3, waiting for transfers between devices, shards(): lax.ppermute(parts[k], 'ctx', chip_pairs(n, k))  14.8 us
    ppermute x3, waiting for transfers between devices, shards(): tops = [lax.ppermute(total, 'ctx', group_pairs(n, k)) for k in range(1, 4)]  10.4 us
    ppermute x3, starting transfers between devices, partners(): lax.ppermute(value, axis, [(i, i ^ k) for i in range(n) if i ^ k < n])  9.58 us
    ppermute x3, starting transfers between devices, shards(): lax.ppermute(parts[k], 'ctx', chip_pairs(n, k))  9.4 us
    ppermute x1, starting transfers between devices, shards(): first = lax.ppermute(send, 'ctx', core_pairs(n))  8.83 us
    unnamed x42, local copies, waits for them, and re-layouts  8.6 us
  transfers between devices with their start and end apart: 12, of which 5 were waited for; matrix products, arithmetic and copies ran while one was open for 0% of the time, Pallas kernels for 11%

profile of v3, /device:TPU:1, one launch (start us, length us, event | category | flops | bytes accessed | tf_op | source)
XLA Modules:
  0.0 142.6 jit_solution(12081768098246490161)
XLA Ops:
  0.7 0.1 pad_add_fusion.refs_0_.where_ref
  0.8 1.0 copy-done
  1.8 1.0 copy-done.2
  2.8 0.7 copy-done.12
  3.6 0.7 copy-done.14
  4.3 0.8 copy-done.16
  5.0 0.8 copy-done.18
  5.8 2.2 %shard_map.126.send_ref = f32[2112,128]{1,0:T(8,128)S(1)} custom-call(s32[3]{0:T(128)S(1)} %pad_add_fusion.refs_0_.where_ref, bf16[128,2048]{1,0:T(8,128)(2,1)S(1)} %bitcast.20, bf16[128,2048]{1,0:T(8,128)(2,1)S(1)} %bitcast.26, bf16[128,128]{1,0:T(8,128)(2,1)S(1)} %bitcast.49, bf16[128,128]{1,0:T(8,128)(2,1)S(1)} %bitcast.53, f32[32,128]{1,0:T(8,128)S(1)} %bitcast.37, ...), custom_call_target="tpu_custom_call" | custom-call | tf_op jit(solution)/shard_map/pallas_call | solution.py:369
  8.0 0.0 copy-start.7
  8.0 8.8 %collective-permute-start = (f32[2112,128]{1,0:T(8,128)S(1)}, f32[2112,128]{1,0:T(8,128)S(1)}, u32[]{:S(2)}, u32[]{:S(2)}) collective-permute-start(f32[2112,128]{1,0:T(8,128)S(1)} %shard_map.126.send_ref), channel_id=1, source_target_pairs={{0,4},{4,0},{8,12},{12,8},{16,20},{20,16},{24,28},{28,24},{32,36},... | collective-permute-start | bytes 3244040 | tf_op jit(solution)/shard_map/ppermute | solution.py:372
  16.8 1.9 %shard_map.127.own_ref = f32[2112,128]{1,0:T(8,128)S(1)} custom-call(s32[3]{0:T(128)S(1)} %pad_add_fusion.refs_0_.where_ref, bf16[128,2048]{1,0:T(8,128)(2,1)S(1)} %bitcast.21, bf16[128,2048]{1,0:T(8,128)(2,1)S(1)} %bitcast.27, bf16[128,128]{1,0:T(8,128)(2,1)S(1)} %bitcast.50, bf16[128,128]{1,0:T(8,128)(2,1)S(1)} %bitcast.54, f32[32,128]{1,0:T(8,128)S(1)} %bitcast.38, ...), custom_call_target="tpu_custom_call" | custom-call | tf_op jit(solution)/shard_map/pallas_call | solution.py:369
  18.8 0.0 copy-done.7
  18.8 0.0 copy-start.4
  18.8 0.3 collective-permute-done.got_ref.first_ref
  19.1 0.7 shard_map.128
  19.8 0.0 copy-done.4
  19.8 0.3 copy-done.5
  20.1 2.1 %collective-permute-start.1 = (f32[528,128]{1,0:T(8,128)S(1)}, f32[528,128]{1,0:T(8,128)S(1)}, u32[]{:S(2)}, u32[]{:S(2)}) collective-permute-start(f32[528,128]{1,0:T(8,128)S(1)} %get-tuple-element.27), channel_id=1, source_target_pairs={{0,8},{4,12},{8,0},{12,4},{16,24},{20,28},{24,16},{28,20},{32,40},... | collective-permute-start | bytes 811016 | tf_op jit(solution)/shard_map/ppermute | solution.py:375
  22.2 1.9 %collective-permute-start.2 = (f32[528,128]{1,0:T(8,128)S(1)}, f32[528,128]{1,0:T(8,128)S(1)}, u32[]{:S(2)}, u32[]{:S(2)}) collective-permute-start(f32[528,128]{1,0:T(8,128)S(1)} %get-tuple-element.28), channel_id=1, source_target_pairs={{0,16},{4,20},{8,24},{12,28},{16,0},{20,4},{24,8},{28,12},{32,48},... | collective-permute-start | bytes 811016 | tf_op jit(solution)/shard_map/ppermute | solution.py:375
  24.1 5.4 %collective-permute-start.3 = (f32[528,128]{1,0:T(8,128)S(1)}, f32[528,128]{1,0:T(8,128)S(1)}, u32[]{:S(2)}, u32[]{:S(2)}) collective-permute-start(f32[528,128]{1,0:T(8,128)S(1)} %get-tuple-element.29), channel_id=1, source_target_pairs={{0,24},{4,28},{8,16},{12,20},{16,8},{20,12},{24,0},{28,4},{32,56},... | collective-permute-start | bytes 811016 | tf_op jit(solution)/shard_map/ppermute | solution.py:375
  29.5 1.5 %collective-permute-done.1.refs_1_ = f32[528,128]{1,0:T(8,128)S(1)} collective-permute-done((f32[528,128]{1,0:T(8,128)S(1)}, f32[528,128]{1,0:T(8,128)S(1)}, u32[]{:S(2)}, u32[]{:S(2)}) %collective-permute-start.1) | collective-permute-done | bytes 270368 | tf_op jit(solution)/shard_map/ppermute | solution.py:375
  31.1 13.2 %collective-permute-done.2.refs_2_ = f32[528,128]{1,0:T(8,128)S(1)} collective-permute-done((f32[528,128]{1,0:T(8,128)S(1)}, f32[528,128]{1,0:T(8,128)S(1)}, u32[]{:S(2)}, u32[]{:S(2)}) %collective-permute-start.2) | collective-permute-done | bytes 270368 | tf_op jit(solution)/shard_map/ppermute | solution.py:375
  44.3 0.0 collective-permute-done.3.refs_3_
  44.3 0.7 shard_map.129
  45.0 7.5 %collective-permute-start.4 = (f32[528,128]{1,0:T(8,128)S(1)}, f32[528,128]{1,0:T(8,128)S(1)}, u32[]{:S(2)}, u32[]{:S(2)}) collective-permute-start(f32[528,128]{1,0:T(8,128)S(1)} %get-tuple-element.30), channel_id=1, source_target_pairs={{4,100},{12,108},{20,116},{28,124},{36,68},{44,76},{52,84},{60,92}... | collective-permute-start | bytes 811016 | tf_op jit(solution)/shard_map/ppermute | solution.py:390
  52.5 5.2 %collective-permute-start.5 = (f32[528,128]{1,0:T(8,128)S(1)}, f32[528,128]{1,0:T(8,128)S(1)}, u32[]{:S(2)}, u32[]{:S(2)}) collective-permute-start(f32[528,128]{1,0:T(8,128)S(1)} %get-tuple-element.30), channel_id=1, source_target_pairs={{4,36},{12,44},{20,52},{28,60},{32,0},{40,8},{48,16},{56,24},{68,1... | collective-permute-start | bytes 811016 | tf_op jit(solution)/shard_map/ppermute | solution.py:390
  57.7 3.1 %collective-permute-start.6 = (f32[528,128]{1,0:T(8,128)S(1)}, f32[528,128]{1,0:T(8,128)S(1)}, u32[]{:S(2)}, u32[]{:S(2)}) collective-permute-start(f32[528,128]{1,0:T(8,128)S(1)} %get-tuple-element.30), channel_id=1, source_target_pairs={{4,68},{12,76},{20,84},{28,92},{36,100},{44,108},{52,116},{60,124}... | collective-permute-start | bytes 811016 | tf_op jit(solution)/shard_map/ppermute | solution.py:390
  60.9 0.0 copy-done.17
  60.9 0.0 copy-done.19
  60.9 0.0 copy-done.1
  60.9 0.0 copy-done.3
  60.9 0.0 copy-done.13
  60.9 0.0 copy-done.15
  60.9 5.3 %shard_map.130 = (f32[128,2048]{1,0:T(8,128)S(1)}, f32[128,2048]{1,0:T(8,128)S(1)}, f32[128,256]{1,0:T(8,128)S(1)}) custom-call(bf16[128,2048]{1,0:T(8,128)(2,1)S(1)} %bitcast.22, bf16[128,2048]{1,0:T(8,128)(2,1)S(1)} %bitcast.28, bf16[128,128]{1,0:T(8,128)(2,1)S(1)} %bitcast.51, bf16[128,128]{1,0:T(8,128)(2,1)S(1)} %bitcast.55, f32[32,128]{1,0:T(8,128)S(1)} %bitcast.39, ...), custom_call_target="tpu_custom_call" | custom-call | tf_op jit(solution)/shard_map/pallas_call | solution.py:381
  66.2 0.0 copy-start.8
  66.2 1.0 copy-done.8
  67.2 1.0 copy-done.10
  68.2 0.0 collective-permute-done.4.refs_2_
  68.2 0.0 collective-permute-done.5.refs_0_
  68.2 10.4 %collective-permute-done.6.refs_1_ = f32[528,128]{1,0:T(8,128)S(1)} collective-permute-done((f32[528,128]{1,0:T(8,128)S(1)}, f32[528,128]{1,0:T(8,128)S(1)}, u32[]{:S(2)}, u32[]{:S(2)}) %collective-permute-start.6) | collective-permute-done | bytes 270368 | tf_op jit(solution)/shard_map/ppermute | solution.py:390
  78.6 0.7 shard_map.131
  79.3 0.0 copy-start.20
  79.3 0.0 copy-start.6
  79.3 31.0 %all_to_all.16 = f32[4,520,128]{2,1,0:T(8,128)S(1)} all-to-all(f32[4,520,128]{2,1,0:T(8,128)S(1)} %bitcast.36), channel_id=1, replica_groups={{0,8,16,24},{4,12,20,28},{32,40,48,56},{36,44,52,60},{64,72,80,88},{68,..., dimensions={0} | all-to-all | bytes 2129920 | tf_op jit(solution)/shard_map/all_to_all | solution.py:393
  110.3 4.0 %collective-permute-start.7 = (f32[2080,128]{1,0:T(8,128)S(1)}, f32[2080,128]{1,0:T(8,128)}, u32[]{:S(2)}, u32[]{:S(2)}) collective-permute-start(f32[2080,128]{1,0:T(8,128)S(1)} %bitcast.32), channel_id=1, source_target_pairs={{0,4},{4,0},{8,12},{12,8},{16,20},{20,16},{24,28},{28,24},{32,36},... | collective-permute-start | bytes 3194888 | tf_op jit(solution)/shard_map/ppermute | solution.py:394
  114.3 0.0 copy-done.20
  114.3 0.1 broadcast_in_dim.21
  114.4 0.1 broadcast_in_dim_reshape.3.gain_ref
  114.5 2.0 %shard_map.133.near_maps_ref = f32[128,128]{1,0:T(8,128)S(1)} custom-call(s32[3]{0:T(128)S(1)} %pad_add_fusion.refs_0_.where_ref, bf16[128,2048]{1,0:T(8,128)(2,1)S(1)} %bitcast.23, bf16[128,2048]{1,0:T(8,128)(2,1)S(1)} %bitcast.29, f32[32,128]{1,0:T(8,128)S(1)} %bitcast.40, f32[32,128]{1,0:T(8,128)S(1)} %bitcast.46, f32[2080,128]{1,0:T(8,128)S(1)} %bitcast.33, ...), custom_call_target="tpu_custom_call" | custom-call | tf_op jit(solution)/shard_map/pallas_call | solution.py:395
  116.5 0.2 collective-permute-done.7.far_ref
  116.7 3.5 %shard_map.134 = (f32[128,256]{1,0:T(8,128)}, f32[32,128]{1,0:T(8,128)S(1)}) custom-call(s32[3]{0:T(128)S(1)} %pad_add_fusion.refs_0_.where_ref, bf16[128,2048]{1,0:T(8,128)(2,1)S(1)} %bitcast.24, bf16[128,2048]{1,0:T(8,128)(2,1)S(1)} %bitcast.30, f32[32,128]{1,0:T(8,128)S(1)} %bitcast.41, f32[32,128]{1,0:T(8,128)S(1)} %bitcast.47, ...), custom_call_target="tpu_custom_call" | custom-call | tf_op jit(solution)/shard_map/pallas_call | solution.py:396
  120.2 0.1 slice_reduce_fusion
  120.3 3.7 %collective-permute-start.10 = (f32[32]{0:T(128)S(1)}, f32[32]{0:T(128)S(1)}, u32[]{:S(2)}, u32[]{:S(2)}) collective-permute-start(f32[32]{0:T(128)S(1)} %slice_reduce_fusion), channel_id=1, source_target_pairs={{0,384},{128,256},{256,128},{384,0},{1,385},{129,257},{257,129},{3... | collective-permute-start | bytes 392 | tf_op jit(solution)/shard_map/ppermute | solution.py:348
  124.1 1.9 %collective-permute-start.8 = (f32[32]{0:T(128)S(1)}, f32[32]{0:T(128)S(1)}, u32[]{:S(2)}, u32[]{:S(2)}) collective-permute-start(f32[32]{0:T(128)S(1)} %slice_reduce_fusion), channel_id=1, source_target_pairs={{0,128},{128,0},{256,384},{384,256},{1,129},{129,1},{257,385},{385... | collective-permute-start | bytes 392 | tf_op jit(solution)/shard_map/ppermute | solution.py:348
  126.0 3.9 %collective-permute-start.9 = (f32[32]{0:T(128)S(1)}, f32[32]{0:T(128)S(1)}, u32[]{:S(2)}, u32[]{:S(2)}) collective-permute-start(f32[32]{0:T(128)S(1)} %slice_reduce_fusion), channel_id=1, source_target_pairs={{0,256},{128,384},{256,0},{384,128},{1,257},{129,385},{257,1},{385... | collective-permute-start | bytes 392 | tf_op jit(solution)/shard_map/ppermute | solution.py:348
  129.9 3.5 %all-to-all-start.1 = ((f32[4,32,256]{2,1,0:T(8,128)}), f32[4,32,256]{2,1,0:T(8,128)S(1)}, u32[]{:S(2)}, u32[]{:S(2)}) async-start(f32[4,32,256]{2,1,0:T(8,128)} %bitcast.15), calls=%async_computation.1 | async-start | bytes 262144 | tf_op jit(solution)/shard_map/all_to_all | solution.py:400
  133.5 1.2 copy-done.11
  134.7 6.7 %shard_map.132 = (bf16[128,2048]{1,0:T(8,128)(2,1)}, bf16[128,2048]{1,0:T(8,128)(2,1)}, f32[32,128]{1,0:T(8,128)}, f32[32,128]{1,0:T(8,128)}) custom-call(s32[3]{0:T(128)S(1)} %pad_add_fusion.refs_0_.where_ref, bf16[128,2048]{1,0:T(8,128)(2,1)S(1)} %bitcast.25, bf16[128,2048]{1,0:T(8,128)(2,1)S(1)} %bitcast.31, f32[128,2048]{1,0:T(8,128)S(1)} %copy-done.9, ...), custom_call_target="tpu_custom_call" | custom-call | tf_op jit(solution)/shard_map/pallas_call | solution.py:402
  141.4 0.0 collective-permute-done.10
  141.4 0.0 collective-permute-done.8
  141.4 0.0 collective-permute-done.9
  141.4 0.5 add_multiply_fusion
  142.0 0.0 all-to-all-done.1
  142.0 0.6 slice_bitcast_fusion
  (19 shorter events, 0.0 us)
Async XLA Ops:
  0.7 1.0 copy-start
  1.8 1.0 copy-start.2
  2.8 0.7 copy-start.12
  3.6 0.7 copy-start.14
  4.3 0.8 copy-start.16
  5.0 0.8 copy-start.18
  8.0 10.8 %copy-start.7 = (f32[2112,128]{1,0:T(8,128)}, f32[2112,128]{1,0:T(8,128)S(1)}, u32[]{:S(2)}) copy-start(f32[2112,128]{1,0:T(8,128)S(1)} %shard_map.126.send_ref) | copy-start | bytes 3244036
  8.0 11.2 %collective-permute-start = (f32[2112,128]{1,0:T(8,128)S(1)}, f32[2112,128]{1,0:T(8,128)S(1)}, u32[]{:S(2)}, u32[]{:S(2)}) collective-permute-start(f32[2112,128]{1,0:T(8,128)S(1)} %shard_map.126.send_ref), channel_id=1, source_target_pairs={{0,4},{4,0},{8,12},{12,8},{16,20},{20,16},{24,28},{28,24},{32,36},... | collective-permute-start | bytes 3244040 | tf_op jit(solution)/shard_map/ppermute | solution.py:372
  18.8 1.0 copy-start.4
  19.1 1.0 copy-start.5
  19.1 41.7 %copy-start.17 = (bf16[1,128,128]{2,1,0:T(8,128)(2,1)S(1)}, bf16[1,128,128]{2,1,0:T(8,128)(2,1)}, u32[]{:S(2)}) copy-start(bf16[1,128,128]{2,1,0:T(8,128)(2,1)} %param.9) | copy-start | bytes 98308
  19.1 41.8 %copy-start.19 = (bf16[1,128,128]{2,1,0:T(8,128)(2,1)S(1)}, bf16[1,128,128]{2,1,0:T(8,128)(2,1)}, u32[]{:S(2)}) copy-start(bf16[1,128,128]{2,1,0:T(8,128)(2,1)} %param.10) | copy-start | bytes 98308
  20.1 40.8 %copy-start.1 = (bf16[1,128,2048]{2,1,0:T(8,128)(2,1)S(1)}, bf16[1,128,2048]{2,1,0:T(8,128)(2,1)}, u32[]{:S(2)}) copy-start(bf16[1,128,2048]{2,1,0:T(8,128)(2,1)} %param.7) | copy-start | bytes 1572868
  20.1 40.8 %copy-start.3 = (bf16[1,128,2048]{2,1,0:T(8,128)(2,1)S(1)}, bf16[1,128,2048]{2,1,0:T(8,128)(2,1)}, u32[]{:S(2)}) copy-start(bf16[1,128,2048]{2,1,0:T(8,128)(2,1)} %param.8) | copy-start | bytes 1572868
  20.1 40.8 %copy-start.13 = (f32[1,32,128]{2,1,0:T(8,128)S(1)}, f32[1,32,128]{2,1,0:T(8,128)}, u32[]{:S(2)}) copy-start(f32[1,32,128]{2,1,0:T(8,128)} %param.11) | copy-start | bytes 49156
  20.1 40.8 %copy-start.15 = (f32[1,32,128]{2,1,0:T(8,128)S(1)}, f32[1,32,128]{2,1,0:T(8,128)}, u32[]{:S(2)}) copy-start(f32[1,32,128]{2,1,0:T(8,128)} %param.12) | copy-start | bytes 49156
  20.1 10.9 %collective-permute-start.1 = (f32[528,128]{1,0:T(8,128)S(1)}, f32[528,128]{1,0:T(8,128)S(1)}, u32[]{:S(2)}, u32[]{:S(2)}) collective-permute-start(f32[528,128]{1,0:T(8,128)S(1)} %get-tuple-element.27), channel_id=1, source_target_pairs={{0,8},{4,12},{8,0},{12,4},{16,24},{20,28},{24,16},{28,20},{32,40},... | collective-permute-start | bytes 811016 | tf_op jit(solution)/shard_map/ppermute | solution.py:375
  22.2 22.1 %collective-permute-start.2 = (f32[528,128]{1,0:T(8,128)S(1)}, f32[528,128]{1,0:T(8,128)S(1)}, u32[]{:S(2)}, u32[]{:S(2)}) collective-permute-start(f32[528,128]{1,0:T(8,128)S(1)} %get-tuple-element.28), channel_id=1, source_target_pairs={{0,16},{4,20},{8,24},{12,28},{16,0},{20,4},{24,8},{28,12},{32,48},... | collective-permute-start | bytes 811016 | tf_op jit(solution)/shard_map/ppermute | solution.py:375
  24.1 20.2 %collective-permute-start.3 = (f32[528,128]{1,0:T(8,128)S(1)}, f32[528,128]{1,0:T(8,128)S(1)}, u32[]{:S(2)}, u32[]{:S(2)}) collective-permute-start(f32[528,128]{1,0:T(8,128)S(1)} %get-tuple-element.29), channel_id=1, source_target_pairs={{0,24},{4,28},{8,16},{12,20},{16,8},{20,12},{24,0},{28,4},{32,56},... | collective-permute-start | bytes 811016 | tf_op jit(solution)/shard_map/ppermute | solution.py:375
  45.0 23.2 %collective-permute-start.4 = (f32[528,128]{1,0:T(8,128)S(1)}, f32[528,128]{1,0:T(8,128)S(1)}, u32[]{:S(2)}, u32[]{:S(2)}) collective-permute-start(f32[528,128]{1,0:T(8,128)S(1)} %get-tuple-element.30), channel_id=1, source_target_pairs={{4,100},{12,108},{20,116},{28,124},{36,68},{44,76},{52,84},{60,92}... | collective-permute-start | bytes 811016 | tf_op jit(solution)/shard_map/ppermute | solution.py:390
  52.5 15.7 %collective-permute-start.5 = (f32[528,128]{1,0:T(8,128)S(1)}, f32[528,128]{1,0:T(8,128)S(1)}, u32[]{:S(2)}, u32[]{:S(2)}) collective-permute-start(f32[528,128]{1,0:T(8,128)S(1)} %get-tuple-element.30), channel_id=1, source_target_pairs={{4,36},{12,44},{20,52},{28,60},{32,0},{40,8},{48,16},{56,24},{68,1... | collective-permute-start | bytes 811016 | tf_op jit(solution)/shard_map/ppermute | solution.py:390
  57.7 20.8 %collective-permute-start.6 = (f32[528,128]{1,0:T(8,128)S(1)}, f32[528,128]{1,0:T(8,128)S(1)}, u32[]{:S(2)}, u32[]{:S(2)}) collective-permute-start(f32[528,128]{1,0:T(8,128)S(1)} %get-tuple-element.30), channel_id=1, source_target_pairs={{4,68},{12,76},{20,84},{28,92},{36,100},{44,108},{52,116},{60,124}... | collective-permute-start | bytes 811016 | tf_op jit(solution)/shard_map/ppermute | solution.py:390
  66.2 1.0 copy-start.8
  67.2 1.0 copy-start.10
  79.3 35.0 %copy-start.20 = (f32[32]{0:T(128)S(1)}, f32[32]{0:T(128)}, u32[]{:S(2)}) copy-start(f32[32]{0:T(128)} %param.13) | copy-start | bytes 388
  79.3 35.2 %copy-start.6 = (f32[2112,128]{1,0:T(8,128)S(1)}, f32[2112,128]{1,0:T(8,128)}, u32[]{:S(2)}) copy-start(f32[2112,128]{1,0:T(8,128)} %copy-done.5) | copy-start | bytes 3244036
  110.3 6.4 %collective-permute-start.7 = (f32[2080,128]{1,0:T(8,128)S(1)}, f32[2080,128]{1,0:T(8,128)}, u32[]{:S(2)}, u32[]{:S(2)}) collective-permute-start(f32[2080,128]{1,0:T(8,128)S(1)} %bitcast.32), channel_id=1, source_target_pairs={{0,4},{4,0},{8,12},{12,8},{16,20},{20,16},{24,28},{28,24},{32,36},... | collective-permute-start | bytes 3194888 | tf_op jit(solution)/shard_map/ppermute | solution.py:394
  116.5 17.0 %copy-start.9 = (f32[128,2048]{1,0:T(8,128)S(1)}, f32[128,2048]{1,0:T(8,128)}, u32[]{:S(2)}) copy-start(f32[128,2048]{1,0:T(8,128)} %copy-done.8) | copy-start | bytes 3145732
  120.3 21.1 %collective-permute-start.10 = (f32[32]{0:T(128)S(1)}, f32[32]{0:T(128)S(1)}, u32[]{:S(2)}, u32[]{:S(2)}) collective-permute-start(f32[32]{0:T(128)S(1)} %slice_reduce_fusion), channel_id=1, source_target_pairs={{0,384},{128,256},{256,128},{384,0},{1,385},{129,257},{257,129},{3... | collective-permute-start | bytes 392 | tf_op jit(solution)/shard_map/ppermute | solution.py:348
  124.1 17.4 %collective-permute-start.8 = (f32[32]{0:T(128)S(1)}, f32[32]{0:T(128)S(1)}, u32[]{:S(2)}, u32[]{:S(2)}) collective-permute-start(f32[32]{0:T(128)S(1)} %slice_reduce_fusion), channel_id=1, source_target_pairs={{0,128},{128,0},{256,384},{384,256},{1,129},{129,1},{257,385},{385... | collective-permute-start | bytes 392 | tf_op jit(solution)/shard_map/ppermute | solution.py:348
  126.0 15.4 %collective-permute-start.9 = (f32[32]{0:T(128)S(1)}, f32[32]{0:T(128)S(1)}, u32[]{:S(2)}, u32[]{:S(2)}) collective-permute-start(f32[32]{0:T(128)S(1)} %slice_reduce_fusion), channel_id=1, source_target_pairs={{0,256},{128,384},{256,0},{384,128},{1,257},{129,385},{257,1},{385... | collective-permute-start | bytes 392 | tf_op jit(solution)/shard_map/ppermute | solution.py:348
  129.9 12.0 %all-to-all-start.1 = ((f32[4,32,256]{2,1,0:T(8,128)}), f32[4,32,256]{2,1,0:T(8,128)S(1)}, u32[]{:S(2)}, u32[]{:S(2)}) async-start(f32[4,32,256]{2,1,0:T(8,128)} %bitcast.15), calls=%async_computation.1 | async-start | bytes 262144 | tf_op jit(solution)/shard_map/all_to_all | solution.py:400
  133.5 1.2 copy-start.11

commit v4 on v3

--- a/solution.py
+++ b/solution.py
@@ -57,18 +57,18 @@
     return jnp.where(flag, value, 0.0)
 
 
-def states_kernel(own, where_ref, x_ref, g_ref, b_ref, c_ref, step_ref, log_ref, out_ref, *scratch):
-    if scratch:
-        held, sems = scratch[:6], scratch[6]
-        copies = [
-            pltpu.make_async_copy(ref, slot, sems.at[i])
-            for i, (ref, slot) in enumerate(zip((x_ref, g_ref, b_ref, c_ref, step_ref, log_ref), held, strict=True))
-        ]
-        for copy in copies:
-            copy.start()
-        for copy in copies:
-            copy.wait()
-        x_ref, g_ref, b_ref, c_ref, step_ref, log_ref = held
+def fetch(refs, held, sems):
+    copies = [pltpu.make_async_copy(ref, slot, sems.at[i]) for i, (ref, slot) in enumerate(zip(refs, held, strict=True))]
+    for copy in copies:
+        copy.start()
+    for copy in copies:
+        copy.wait()
+
+
+def states_kernel(own, where_ref, *refs):
+    out_ref, held = refs[6], refs[7:13]
+    fetch(refs[:6], held, refs[13])
+    x_ref, g_ref, b_ref, c_ref, step_ref, log_ref = held
     cum = running_sum(log_ref[...])
 
     def summed(values_ref, factors, map_ref):
@@ -219,33 +219,37 @@
     return jnp.concatenate(slots, axis=0)
 
 
-def weighted_sum(forward, x_ref, g_ref, step_ref, log_ref, state_of):
+def weights_kernel(where_ref, x_ref, g_ref, step_ref, log_ref, after_ref, *out_refs):
+    forward = where_ref[0] == 1
     cum = running_sum(log_ref[...])
-    factors = jnp.where(forward, jnp.exp(cum), step_ref[...] * jnp.exp(cum[:, TOK - 1 : TOK] - cum))
+    starts = jnp.exp(cum)
+    sources = step_ref[...] * jnp.exp(cum[:, TOK - 1 : TOK] - cum)
+    for scanned, high_ref, low_ref in ((forward, *out_refs[:2]), (jnp.logical_not(forward), *out_refs[2:])):
+        factors = jnp.where(scanned, starts, sources)
+        for quarter in range(4):
+            lanes = slice(quarter * QR, (quarter + 1) * QR)
+            values = jnp.where(scanned, g_ref[:, lanes].astype(F32), x_ref[:, lanes].astype(F32))
+            high_ref[:, lanes], low_ref[:, lanes] = split(values * spread_heads(factors, quarter * QR, QR))
+
+
+def weighted_sum(high_ref, low_ref, state_of):
     total = jnp.zeros((TOK, NS), F32)
     for quarter in range(4):
         lanes = slice(quarter * QR, (quarter + 1) * QR)
-        values = jnp.where(forward, g_ref[:, lanes].astype(F32), x_ref[:, lanes].astype(F32))
-        high, low = split(values * spread_heads(factors, quarter * QR, QR))
+        high, low = high_ref[:, lanes], low_ref[:, lanes]
         state_high, state_low = split(state_of(quarter))
         total = total + (dot(high, state_high, 1, 0) + (dot(low, state_high, 1, 0) + dot(high, state_low, 1, 0)))
     return total
 
 
-def near_maps_kernel(where_ref, x_ref, g_ref, step_ref, log_ref, near_ref, first_ref, out_ref):
-    out_ref[...] = weighted_sum(
-        where_ref[0] == 1, x_ref, g_ref, step_ref, log_ref, lambda quarter: at_slab(quarter, near_ref, first_ref)
-    )
-
-
-def far_maps_kernel(
-    where_ref, x_ref, g_ref, step_ref, log_ref, near_ref, far_ref, maps_in_ref, near_maps_ref, maps_ref, skip_ref
-):
+def near_maps_kernel(where_ref, high_far, low_far, near_ref, first_ref, out_ref, high_ref, low_ref, sems):
+    fetch((high_far, low_far), (high_ref, low_ref), sems)
+    out_ref[...] = weighted_sum(high_ref, low_ref, lambda quarter: at_slab(quarter, near_ref, first_ref))
+
+
+def far_maps_kernel(where_ref, high_ref, low_ref, near_ref, far_ref, maps_in_ref, near_maps_ref, maps_ref, skip_ref):
     forward = where_ref[0] == 1
-    other = weighted_sum(
-        where_ref[0] == 0, x_ref, g_ref, step_ref, log_ref,
-        lambda quarter: far_ref[quarter * NEAR : quarter * NEAR + QR, :],
-    )
+    other = weighted_sum(high_ref, low_ref, lambda quarter: far_ref[quarter * NEAR : quarter * NEAR + QR, :])
     for quarter in range(4):
         side = slice(quarter * NEAR + QR, (quarter + 1) * NEAR)
         skip_ref[quarter * QH : (quarter + 1) * QH, :] = near_ref[side, :] + far_ref[side, :]
@@ -255,16 +259,30 @@
 
 
 def cross_kernel(
-    where_ref, x_ref, g_ref, within_ref, back_ref, step_ref, log_ref, gain_ref, b_ref, c_ref,
-    near_ref, far_ref, first_ref, send_ref, own_ref,
+    where_ref, within_far, back_far, x_ref, g_ref, step_ref, log_ref, gain_ref, b_ref, c_ref,
+    near_ref, far_ref, first_ref,
     mixed_ref, ginputs_ref, gstep_ref, gdecay_ref,
+    within_ref, back_ref, sems,
 ):
+    copies = []
+    for quarter in range(4):
+        lanes = slice(quarter * QR, (quarter + 1) * QR)
+        pairs = ((within_far, within_ref), (back_far, back_ref))
+        copies.append(
+            [
+                pltpu.make_async_copy(source.at[:, lanes], slot.at[:, lanes], sems.at[quarter, i])
+                for i, (source, slot) in enumerate(pairs)
+            ]
+        )
+        for copy in copies[-1]:
+            copy.start()
     forward = where_ref[0] == 1
     cums = running_sum(log_ref[...])
     b, c = b_ref[...], c_ref[...]
     two_b, two_c = jnp.concatenate([b, b], axis=1), jnp.concatenate([c, c], axis=1)
     owner = (iota((QR, QH), 0) // PH == iota((QR, QH), 1)).astype(F32).astype(BF16)
     doubled = jnp.concatenate([owner, owner], axis=0)
+    heads_of = (iota((QH, QR), 1) // PH == iota((QH, QR), 0)).astype(F32)
     after = (iota((TOK, TOK), 0) >= iota((TOK, TOK), 1)).astype(F32)
 
     def by_head(values):
@@ -279,25 +297,26 @@
         other = far_ref[quarter * NEAR : quarter * NEAR + QR, :]
         ent = jnp.where(forward, scanned, other)
         arr = jnp.where(forward, other, scanned)
+        for copy in copies[quarter]:
+            copy.wait()
         x, g = x_ref[:, lanes].astype(F32), g_ref[:, lanes].astype(F32)
         starts = spread_heads(jnp.exp(cum), 0, QR)
         sources = spread_heads(steps * jnp.exp(cum[:, TOK - 1 : TOK] - cum), 0, QR)
         output = within_ref[:, lanes] + dot(two_c, jnp.concatenate(split(ent), axis=1), 1, 1) * starts
-        back = back_ref[:, lanes] + dot(two_b, jnp.concatenate(split(arr), axis=1), 1, 1) * sources
+        later = dot(two_b, jnp.concatenate(split(arr), axis=1), 1, 1) * sources
+        back = back_ref[:, lanes] + later
         gain = gain_ref[:, lanes]
         mixed_ref[:, lanes] = (output + gain * x).astype(BF16)
         ginputs_ref[:, lanes] = (back + gain * g).astype(BF16)
         steps_part = x * back
         gstep_ref[heads, :] = by_head(steps_part) / steps
         change = by_head(g * output - steps_part)
-        edges = []
-        for j in range(QH):
-            rows = slice(quarter * QR + j * PH, quarter * QR + (j + 1) * PH)
-            local = jnp.where(forward, own_ref[rows, :], send_ref[rows, :])
-            rows = slice(j * PH, (j + 1) * PH)
-            leaving = local + through[j : j + 1, :] * ent[rows, :]
-            edges.append(jnp.sum(arr[rows, :] * leaving, axis=0, keepdims=True))
-        edge = jnp.sum(jnp.concatenate(edges, axis=0), axis=1, keepdims=True)
+        local = jnp.sum(heads_of * jnp.sum(x * later, axis=0, keepdims=True), axis=1, keepdims=True)
+        carried = [
+            jnp.sum(arr[j * PH : (j + 1) * PH, :] * ent[j * PH : (j + 1) * PH, :], axis=0, keepdims=True)
+            for j in range(QH)
+        ]
+        edge = local + through * jnp.sum(jnp.concatenate(carried, axis=0), axis=1, keepdims=True)
         change = change + jnp.where(iota((QH, TOK), 1) == TOK - 1, edge, 0.0)
         gdecay_ref[heads, :] = dot(change, after, 1, 0, HIGHEST)
 
@@ -305,17 +324,23 @@
 PARAMS = pltpu.CompilerParams(vmem_limit_bytes=VMEM_LIMIT)
 
 
-def call(kernel, outs, n_in, space=pltpu.VMEM, scratch=()):
+def call(kernel, outs, n_in, n_far=0, scratch=()):
     smem = pl.BlockSpec(memory_space=pltpu.SMEM)
     vmem = pl.BlockSpec(memory_space=pltpu.VMEM)
-    return pl.pallas_call(
+    run = pl.pallas_call(
         kernel,
         out_shape=[jax.ShapeDtypeStruct(s, k) for s, k in outs],
-        in_specs=[smem] + [pl.BlockSpec(memory_space=space)] * n_in,
+        in_specs=[smem] + [pl.BlockSpec(memory_space=pltpu.HBM)] * n_far + [vmem] * n_in,
         out_specs=[vmem] * len(outs),
         scratch_shapes=list(scratch),
         compiler_params=PARAMS,
     )
+
+    def place(where, *arrays):
+        far = [pltpu.with_memory_space_constraint(v, pltpu.HBM) for v in arrays[:n_far]]
+        return run(where, *far, *arrays[n_far:])
+
+    return place
 
 
 def by_quarter(kernel, in_specs, out_specs, out_shape, scratch=()):
@@ -360,18 +385,16 @@
     slab_inputs = (x, g, b, c, steps, logs)
 
     def states(own):
-        if own:
-            scratch, space = (), pltpu.VMEM
-        else:
-            scratch = [pltpu.VMEM(v.shape, v.dtype) for v in slab_inputs] + [pltpu.SemaphoreType.DMA((6,))]
-            space = pltpu.HBM
+        scratch = [pltpu.VMEM(v.shape, v.dtype) for v in slab_inputs] + [pltpu.SemaphoreType.DMA((6,))]
         kernel = lambda *refs: states_kernel(own, *refs)
-        return call(kernel, [((FEATS + SIDE, NS), F32)], 6, space, scratch)(where, *slab_inputs)[0]
+        return call(kernel, [((FEATS + SIDE, NS), F32)], 0, 6, scratch)(where, *slab_inputs)[0]
 
     send = states(False)
     first = lax.ppermute(send, "ctx", core_pairs(n))
     own = states(True)
-    parts = call(chip_kernel, [((PIECE, NS), F32)] * 4, 2)(where, first, own)
+    parts = list(call(chip_kernel, [((PIECE, NS), F32)] * 4, 2)(where, first, own))
+    *slab_inputs, parts[0] = lax.optimization_barrier((*slab_inputs, parts[0]))
+    x, g, b, c, steps, logs = slab_inputs
     mine = [parts[0]] + [lax.ppermute(parts[k], "ctx", chip_pairs(n, k)) for k in range(1, 4)]
 
     cols = pl.BlockSpec((TOK, QR), lambda i: (0, i))
@@ -388,19 +411,22 @@
 
     total, placed = call(group_kernel, [((PIECE, NS), F32), ((4 * PIECE, NS), F32)], 4)(where, *mine)
     tops = [lax.ppermute(total, "ctx", group_pairs(n, k)) for k in range(1, 4)]
-    tops[-1], within, back, maps = lax.optimization_barrier((tops[-1], within, back, maps))
+    weights = call(weights_kernel, [((TOK, FEATS), BF16)] * 4, 5)(where, x, g, steps, logs, parts[0])
+    tops[-1], within, back, maps, *weights = lax.optimization_barrier((tops[-1], within, back, maps, *weights))
     (ready,) = call(prefix_kernel, [((4 * NEAR, NS), F32)], 4)(where, placed, *tops)
     near = lax.all_to_all(ready, "ctx", 0, 0, axis_index_groups=groups, tiled=True)
     far = lax.ppermute(near, "ctx", core_pairs(n))
-    (near_maps,) = call(near_maps_kernel, [((TOK, NS), F32)], 6)(where, x, g, steps, logs, near, first)
-    maps, skips = call(far_maps_kernel, [((TOK, 2 * NS), F32), ((HEADS, NS), F32)], 8)(
-        where, x, g, steps, logs, near, far, maps, near_maps
+    halves = [pltpu.VMEM((TOK, FEATS), BF16)] * 2 + [pltpu.SemaphoreType.DMA((2,))]
+    (near_maps,) = call(near_maps_kernel, [((TOK, NS), F32)], 2, 2, halves)(where, *weights[:2], near, first)
+    maps, skips = call(far_maps_kernel, [((TOK, 2 * NS), F32), ((HEADS, NS), F32)], 6)(
+        where, *weights[2:], near, far, maps, near_maps
     )
     tp = lax.axis_size("tp")
     swapped = lax.all_to_all(maps.reshape(tp, TOK // tp, 2 * NS), "tp", 0, 0)
+    slots = [pltpu.VMEM((TOK, FEATS), F32)] * 2 + [pltpu.SemaphoreType.DMA((4, 2))]
     outs = [((TOK, FEATS), BF16)] * 2 + [((HEADS, TOK), F32)] * 2
-    mixed, ginputs, gstep, gdecay = call(cross_kernel, outs, 14)(
-        where, x, g, within, back, steps, logs, gains, b, c, near, far, first, send, own
+    mixed, ginputs, gstep, gdecay = call(cross_kernel, outs, 10, 2, slots)(
+        where, within, back, x, g, steps, logs, gains, b, c, near, far, first
     )
     reduced = jnp.sum(swapped, axis=0)
     skip = skips[:, 0]

time: 144 us -> 140 us (0.972)
  local copies, waits for them, and re-layouts: 9.47 us -> 4.49 us
  Pallas kernels: 23.7 us -> 27.8 us
  waiting for transfers between devices: 25.7 us -> 21.7 us
  starting transfers between devices: 51.2 us -> 53.1 us
    unnamed x42 -> x30, local copies, waits for them, and re-layouts: 8.6 us -> 3.61 us
    pallas_call x8 -> x9, Pallas kernels: 18.4 us -> 22.5 us  [place(): return run(where, *far, *arrays[n_far:])]
    ppermute x3, waiting for transfers between devices: 10.4 us -> 6.52 us  [shards(): tops = [lax.ppermute(total, 'ctx', group_pairs(n, k)) for k in range(1, 4)]]
  transfers between devices with their start and end apart: 12 -> 12, of which waited for: 5 -> 3; matrix products, arithmetic and copies ran while one was open for 0% -> 0% of each run, Pallas kernels for 11% -> 14%
where the time goes in v4:
time: 140 us; the launch traced here: 139 us
  starting transfers between devices  53.1 us (38%)
  blocking collectives  29.9 us (21%)
  Pallas kernels  27.8 us (20%)
  waiting for transfers between devices  21.7 us (16%)
  local copies, waits for them, and re-layouts  4.49 us (3%)
    all_to_all x1, blocking collectives, shards(): lax.all_to_all(ready, 'ctx', 0, 0, axis_index_groups=groups, tiled=True)  29.9 us
    pallas_call x9, Pallas kernels, place(): return run(where, *far, *arrays[n_far:])  22.5 us
    ppermute x3, starting transfers between devices, shards(): tops = [lax.ppermute(total, 'ctx', group_pairs(n, k)) for k in range(1, 4)]  15.8 us
    ppermute x3, waiting for transfers between devices, shards(): lax.ppermute(parts[k], 'ctx', chip_pairs(n, k))  15.2 us
    ppermute x3, starting transfers between devices, partners(): lax.ppermute(value, axis, [(i, i ^ k) for i in range(n) if i ^ k < n])  10.1 us
    ppermute x3, starting transfers between devices, shards(): lax.ppermute(parts[k], 'ctx', chip_pairs(n, k))  9.4 us
    ppermute x1, starting transfers between devices, shards(): first = lax.ppermute(send, 'ctx', core_pairs(n))  8.82 us
    ppermute x3, waiting for transfers between devices, shards(): tops = [lax.ppermute(total, 'ctx', group_pairs(n, k)) for k in range(1, 4)]  6.52 us
  transfers between devices with their start and end apart: 12, of which 3 were waited for; matrix products, arithmetic and copies ran while one was open for 0% of the time, Pallas kernels for 14%

profile of v4, /device:TPU:1, one launch (start us, length us, event | category | flops | bytes accessed | tf_op | source)
XLA Modules:
  0.0 138.6 jit_solution(2257947421142783573)
XLA Ops:
  0.7 0.1 pad_add_fusion.refs_0_.where_ref
  0.7 3.2 %shard_map.126 = f32[2112,128]{1,0:T(8,128)S(1)} custom-call(s32[3]{0:T(128)S(1)} %pad_add_fusion.refs_0_.where_ref, bf16[128,2048]{1,0:T(8,128)(2,1)} %bitcast.24, bf16[128,2048]{1,0:T(8,128)(2,1)} %bitcast.29, bf16[128,128]{1,0:T(8,128)(2,1)} %bitcast.35, bf16[128,128]{1,0:T(8,128)(2,1)} %bitcast.39, f32[32,128]{1,0:T(8,128)} %bitcast.43, f32[32,128]{1,0:T(8,128)} %bitcast.48), custom_call_target="tpu_custom_call" | custom-call | tf_op jit(solution)/shard_map/pallas_call | solution.py:341
  3.9 8.8 %collective-permute-start = (f32[2112,128]{1,0:T(8,128)S(1)}, f32[2112,128]{1,0:T(8,128)S(1)}, u32[]{:S(2)}, u32[]{:S(2)}) collective-permute-start(f32[2112,128]{1,0:T(8,128)S(1)} %shard_map.126), channel_id=1, source_target_pairs={{0,4},{4,0},{8,12},{12,8},{16,20},{20,16},{24,28},{28,24},{32,36},... | collective-permute-start | bytes 3244040 | tf_op jit(solution)/shard_map/ppermute | solution.py:393
  12.7 3.2 %shard_map.127.own_ref = f32[2112,128]{1,0:T(8,128)S(1)} custom-call(s32[3]{0:T(128)S(1)} %pad_add_fusion.refs_0_.where_ref, bf16[128,2048]{1,0:T(8,128)(2,1)} %bitcast.25, bf16[128,2048]{1,0:T(8,128)(2,1)} %bitcast.30, bf16[128,128]{1,0:T(8,128)(2,1)} %bitcast.36, bf16[128,128]{1,0:T(8,128)(2,1)} %bitcast.40, f32[32,128]{1,0:T(8,128)} %bitcast.44, ...), custom_call_target="tpu_custom_call" | custom-call | tf_op jit(solution)/shard_map/pallas_call | solution.py:341
  16.0 0.0 collective-permute-done.got_ref.first_ref
  16.0 0.7 shard_map.128
  16.7 0.0 copy-start
  16.7 0.0 copy-start.1
  16.7 0.0 copy-start.12
  16.7 0.0 copy-start.13
  16.7 2.1 %collective-permute-start.1 = (f32[528,128]{1,0:T(8,128)S(1)}, f32[528,128]{1,0:T(8,128)S(1)}, u32[]{:S(2)}, u32[]{:S(2)}) collective-permute-start(f32[528,128]{1,0:T(8,128)S(1)} %get-tuple-element.43), channel_id=1, source_target_pairs={{0,8},{4,12},{8,0},{12,4},{16,24},{20,28},{24,16},{28,20},{32,40},... | collective-permute-start | bytes 811016 | tf_op jit(solution)/shard_map/ppermute | solution.py:398
  18.8 1.9 %collective-permute-start.2 = (f32[528,128]{1,0:T(8,128)S(1)}, f32[528,128]{1,0:T(8,128)S(1)}, u32[]{:S(2)}, u32[]{:S(2)}) collective-permute-start(f32[528,128]{1,0:T(8,128)S(1)} %get-tuple-element.44), channel_id=1, source_target_pairs={{0,16},{4,20},{8,24},{12,28},{16,0},{20,4},{24,8},{28,12},{32,48},... | collective-permute-start | bytes 811016 | tf_op jit(solution)/shard_map/ppermute | solution.py:398
  20.7 5.4 %collective-permute-start.3 = (f32[528,128]{1,0:T(8,128)S(1)}, f32[528,128]{1,0:T(8,128)S(1)}, u32[]{:S(2)}, u32[]{:S(2)}) collective-permute-start(f32[528,128]{1,0:T(8,128)S(1)} %get-tuple-element.45), channel_id=1, source_target_pairs={{0,24},{4,28},{8,16},{12,20},{16,8},{20,12},{24,0},{28,4},{32,56},... | collective-permute-start | bytes 811016 | tf_op jit(solution)/shard_map/ppermute | solution.py:398
  26.2 0.0 copy-start.4
  26.2 0.0 copy-start.5
  26.2 1.9 %collective-permute-done.1.refs_1_ = f32[528,128]{1,0:T(8,128)S(1)} collective-permute-done((f32[528,128]{1,0:T(8,128)S(1)}, f32[528,128]{1,0:T(8,128)S(1)}, u32[]{:S(2)}, u32[]{:S(2)}) %collective-permute-start.1) | collective-permute-done | bytes 270368 | tf_op jit(solution)/shard_map/ppermute | solution.py:398
  28.1 13.2 %collective-permute-done.2.refs_2_ = f32[528,128]{1,0:T(8,128)S(1)} collective-permute-done((f32[528,128]{1,0:T(8,128)S(1)}, f32[528,128]{1,0:T(8,128)S(1)}, u32[]{:S(2)}, u32[]{:S(2)}) %collective-permute-start.2) | collective-permute-done | bytes 270368 | tf_op jit(solution)/shard_map/ppermute | solution.py:398
  41.4 0.0 collective-permute-done.3.refs_3_
  41.4 0.7 shard_map.129
  42.1 7.5 %collective-permute-start.4 = (f32[528,128]{1,0:T(8,128)S(1)}, f32[528,128]{1,0:T(8,128)S(1)}, u32[]{:S(2)}, u32[]{:S(2)}) collective-permute-start(f32[528,128]{1,0:T(8,128)S(1)} %get-tuple-element.46), channel_id=1, source_target_pairs={{4,100},{12,108},{20,116},{28,124},{36,68},{44,76},{52,84},{60,92}... | collective-permute-start | bytes 811016 | tf_op jit(solution)/shard_map/ppermute | solution.py:413
  49.6 5.2 %collective-permute-start.5 = (f32[528,128]{1,0:T(8,128)S(1)}, f32[528,128]{1,0:T(8,128)S(1)}, u32[]{:S(2)}, u32[]{:S(2)}) collective-permute-start(f32[528,128]{1,0:T(8,128)S(1)} %get-tuple-element.46), channel_id=1, source_target_pairs={{4,36},{12,44},{20,52},{28,60},{32,0},{40,8},{48,16},{56,24},{68,1... | collective-permute-start | bytes 811016 | tf_op jit(solution)/shard_map/ppermute | solution.py:413
  54.8 3.1 %collective-permute-start.6 = (f32[528,128]{1,0:T(8,128)S(1)}, f32[528,128]{1,0:T(8,128)S(1)}, u32[]{:S(2)}, u32[]{:S(2)}) collective-permute-start(f32[528,128]{1,0:T(8,128)S(1)} %get-tuple-element.46), channel_id=1, source_target_pairs={{4,68},{12,76},{20,84},{28,92},{36,100},{44,108},{52,116},{60,124}... | collective-permute-start | bytes 811016 | tf_op jit(solution)/shard_map/ppermute | solution.py:413
  57.9 0.0 copy-done
  57.9 0.0 copy-done.1
  57.9 0.0 copy-done.12
  57.9 0.0 copy-done.13
  57.9 1.6 %shard_map.131 = (bf16[128,2048]{1,0:T(8,128)(2,1)S(1)}, bf16[128,2048]{1,0:T(8,128)(2,1)S(1)}, bf16[128,2048]{1,0:T(8,128)(2,1)S(1)}, bf16[128,2048]{1,0:T(8,128)(2,1)S(1)}) custom-call(s32[3]{0:T(128)S(1)} %pad_add_fusion.refs_0_.where_ref, bf16[128,2048]{1,0:T(8,128)(2,1)S(1)} %bitcast.26, bf16[128,2048]{1,0:T(8,128)(2,1)S(1)} %bitcast.31, ...), custom_call_target="tpu_custom_call" | custom-call | tf_op jit(solution)/shard_map/pallas_call | solution.py:341
  59.5 0.0 copy-start.10
  59.6 0.8 copy-done.10
  60.4 0.8 copy-done.11
  61.2 0.0 copy-done.4
  61.2 0.0 copy-done.5
  61.2 5.3 %shard_map.130 = (f32[128,2048]{1,0:T(8,128)S(1)}, f32[128,2048]{1,0:T(8,128)S(1)}, f32[128,256]{1,0:T(8,128)S(1)}) custom-call(bf16[128,2048]{1,0:T(8,128)(2,1)S(1)} %bitcast.27, bf16[128,2048]{1,0:T(8,128)(2,1)S(1)} %bitcast.32, bf16[128,128]{1,0:T(8,128)(2,1)S(1)} %bitcast.37, bf16[128,128]{1,0:T(8,128)(2,1)S(1)} %bitcast.41, f32[32,128]{1,0:T(8,128)S(1)} %bitcast.46, ...), custom_call_target="tpu_custom_call" | custom-call | tf_op jit(solution)/shard_map/pallas_call | solution.py:404
  66.4 0.0 copy-start.2
  66.5 1.0 copy-done.2
  67.4 1.0 copy-done.3
  68.4 0.0 collective-permute-done.4.refs_2_
  68.4 0.0 collective-permute-done.5.refs_0_
  68.4 6.5 %collective-permute-done.6.refs_1_ = f32[528,128]{1,0:T(8,128)S(1)} collective-permute-done((f32[528,128]{1,0:T(8,128)S(1)}, f32[528,128]{1,0:T(8,128)S(1)}, u32[]{:S(2)}, u32[]{:S(2)}) %collective-permute-start.6) | collective-permute-done | bytes 270368 | tf_op jit(solution)/shard_map/ppermute | solution.py:413
  74.9 0.0 copy-done.6
  74.9 0.0 copy-done.8
  74.9 0.7 shard_map.132
  75.6 0.0 copy-start.14
  75.6 29.9 %all_to_all.16 = f32[4,520,128]{2,1,0:T(8,128)S(1)} all-to-all(f32[4,520,128]{2,1,0:T(8,128)S(1)} %bitcast.34), channel_id=1, replica_groups={{0,8,16,24},{4,12,20,28},{32,40,48,56},{36,44,52,60},{64,72,80,88},{68,..., dimensions={0} | all-to-all | bytes 2129920 | tf_op jit(solution)/shard_map/all_to_all | solution.py:417
  105.5 4.6 %collective-permute-start.7 = (f32[2080,128]{1,0:T(8,128)S(1)}, f32[2080,128]{1,0:T(8,128)}, u32[]{:S(2)}, u32[]{:S(2)}) collective-permute-start(f32[2080,128]{1,0:T(8,128)S(1)} %bitcast.20), channel_id=1, source_target_pairs={{0,4},{4,0},{8,12},{12,8},{16,20},{20,16},{24,28},{28,24},{32,36},... | collective-permute-start | bytes 3194888 | tf_op jit(solution)/shard_map/ppermute | solution.py:418
  110.1 0.0 copy-done.14
  110.1 0.1 broadcast_in_dim.21
  110.2 0.1 broadcast_in_dim_reshape.3.gain_ref
  110.3 0.0 copy-start.9
  110.3 2.4 %shard_map.134.near_maps_ref = f32[128,128]{1,0:T(8,128)S(1)} custom-call(s32[3]{0:T(128)S(1)} %pad_add_fusion.refs_0_.where_ref, bf16[128,2048]{1,0:T(8,128)(2,1)} %copy-done.10, bf16[128,2048]{1,0:T(8,128)(2,1)} %copy-done.11, f32[2080,128]{1,0:T(8,128)S(1)} %bitcast.21, f32[2112,128]{1,0:T(8,128)S(1)} %collective-permute-done.got_ref.first_ref), custom_call_target="tpu_custom_call" | custom-call | tf_op jit(solution)/shard_map/pallas_call | solution.py:341
  112.7 0.0 collective-permute-done.7.far_ref
  112.7 2.5 %shard_map.135 = (f32[128,256]{1,0:T(8,128)}, f32[32,128]{1,0:T(8,128)S(1)}) custom-call(s32[3]{0:T(128)S(1)} %pad_add_fusion.refs_0_.where_ref, bf16[128,2048]{1,0:T(8,128)(2,1)S(1)} %copy-done.7, bf16[128,2048]{1,0:T(8,128)(2,1)S(1)} %copy-done.9, f32[2080,128]{1,0:T(8,128)S(1)} %bitcast.22, f32[2080,128]{1,0:T(8,128)} %collective-permute-done.7.far_ref, ...), custom_call_target="tpu_custom_call" | custom-call | tf_op jit(solution)/shard_map/pallas_call | solution.py:341
  115.2 0.1 slice_reduce_fusion
  115.3 5.0 %collective-permute-start.10 = (f32[32]{0:T(128)S(1)}, f32[32]{0:T(128)S(1)}, u32[]{:S(2)}, u32[]{:S(2)}) collective-permute-start(f32[32]{0:T(128)S(1)} %slice_reduce_fusion), channel_id=1, source_target_pairs={{0,384},{128,256},{256,128},{384,0},{1,385},{129,257},{257,129},{3... | collective-permute-start | bytes 392 | tf_op jit(solution)/shard_map/ppermute | solution.py:373
  120.3 1.9 %collective-permute-start.8 = (f32[32]{0:T(128)S(1)}, f32[32]{0:T(128)S(1)}, u32[]{:S(2)}, u32[]{:S(2)}) collective-permute-start(f32[32]{0:T(128)S(1)} %slice_reduce_fusion), channel_id=1, source_target_pairs={{0,128},{128,0},{256,384},{384,256},{1,129},{129,1},{257,385},{385... | collective-permute-start | bytes 392 | tf_op jit(solution)/shard_map/ppermute | solution.py:373
  122.3 3.1 %collective-permute-start.9 = (f32[32]{0:T(128)S(1)}, f32[32]{0:T(128)S(1)}, u32[]{:S(2)}, u32[]{:S(2)}) collective-permute-start(f32[32]{0:T(128)S(1)} %slice_reduce_fusion), channel_id=1, source_target_pairs={{0,256},{128,384},{256,0},{384,128},{1,257},{129,385},{257,1},{385... | collective-permute-start | bytes 392 | tf_op jit(solution)/shard_map/ppermute | solution.py:373
  125.4 4.4 %all-to-all-start.1 = ((f32[4,32,256]{2,1,0:T(8,128)}), f32[4,32,256]{2,1,0:T(8,128)S(1)}, u32[]{:S(2)}, u32[]{:S(2)}) async-start(f32[4,32,256]{2,1,0:T(8,128)} %bitcast.15), calls=%async_computation.1 | async-start | bytes 262144 | tf_op jit(solution)/shard_map/all_to_all | solution.py:425
  129.8 7.7 %shard_map.133 = (bf16[128,2048]{1,0:T(8,128)(2,1)}, bf16[128,2048]{1,0:T(8,128)(2,1)}, f32[32,128]{1,0:T(8,128)}, f32[32,128]{1,0:T(8,128)}) custom-call(s32[3]{0:T(128)S(1)} %pad_add_fusion.refs_0_.where_ref, f32[128,2048]{1,0:T(8,128)} %copy-done.2, f32[128,2048]{1,0:T(8,128)} %copy-done.3, bf16[128,2048]{1,0:T(8,128)(2,1)S(1)} %bitcast.28, ...), custom_call_target="tpu_custom_call" | custom-call | tf_op jit(solution)/shard_map/pallas_call | solution.py:341
  137.4 0.0 collective-permute-done.10
  137.4 0.0 collective-permute-done.8
  137.4 0.0 collective-permute-done.9
  137.4 0.5 add_multiply_fusion
  138.0 0.0 all-to-all-done.1
  138.0 0.6 slice_bitcast_fusion
  (8 shorter events, 0.0 us)
Async XLA Ops:
  3.9 12.0 %collective-permute-start = (f32[2112,128]{1,0:T(8,128)S(1)}, f32[2112,128]{1,0:T(8,128)S(1)}, u32[]{:S(2)}, u32[]{:S(2)}) collective-permute-start(f32[2112,128]{1,0:T(8,128)S(1)} %shard_map.126), channel_id=1, source_target_pairs={{0,4},{4,0},{8,12},{12,8},{16,20},{20,16},{24,28},{28,24},{32,36},... | collective-permute-start | bytes 3244040 | tf_op jit(solution)/shard_map/ppermute | solution.py:393
  16.7 41.2 %copy-start = (bf16[1,128,2048]{2,1,0:T(8,128)(2,1)S(1)}, bf16[1,128,2048]{2,1,0:T(8,128)(2,1)}, u32[]{:S(2)}) copy-start(bf16[1,128,2048]{2,1,0:T(8,128)(2,1)} %param.7) | copy-start | bytes 1572868
  16.7 41.2 %copy-start.1 = (bf16[1,128,2048]{2,1,0:T(8,128)(2,1)S(1)}, bf16[1,128,2048]{2,1,0:T(8,128)(2,1)}, u32[]{:S(2)}) copy-start(bf16[1,128,2048]{2,1,0:T(8,128)(2,1)} %param.8) | copy-start | bytes 1572868
  16.7 41.2 %copy-start.12 = (f32[1,32,128]{2,1,0:T(8,128)S(1)}, f32[1,32,128]{2,1,0:T(8,128)}, u32[]{:S(2)}) copy-start(f32[1,32,128]{2,1,0:T(8,128)} %param.11) | copy-start | bytes 49156
  16.7 41.2 %copy-start.13 = (f32[1,32,128]{2,1,0:T(8,128)S(1)}, f32[1,32,128]{2,1,0:T(8,128)}, u32[]{:S(2)}) copy-start(f32[1,32,128]{2,1,0:T(8,128)} %param.12) | copy-start | bytes 49156
  16.7 11.4 %collective-permute-start.1 = (f32[528,128]{1,0:T(8,128)S(1)}, f32[528,128]{1,0:T(8,128)S(1)}, u32[]{:S(2)}, u32[]{:S(2)}) collective-permute-start(f32[528,128]{1,0:T(8,128)S(1)} %get-tuple-element.43), channel_id=1, source_target_pairs={{0,8},{4,12},{8,0},{12,4},{16,24},{20,28},{24,16},{28,20},{32,40},... | collective-permute-start | bytes 811016 | tf_op jit(solution)/shard_map/ppermute | solution.py:398
  18.8 22.6 %collective-permute-start.2 = (f32[528,128]{1,0:T(8,128)S(1)}, f32[528,128]{1,0:T(8,128)S(1)}, u32[]{:S(2)}, u32[]{:S(2)}) collective-permute-start(f32[528,128]{1,0:T(8,128)S(1)} %get-tuple-element.44), channel_id=1, source_target_pairs={{0,16},{4,20},{8,24},{12,28},{16,0},{20,4},{24,8},{28,12},{32,48},... | collective-permute-start | bytes 811016 | tf_op jit(solution)/shard_map/ppermute | solution.py:398
  20.7 20.7 %collective-permute-start.3 = (f32[528,128]{1,0:T(8,128)S(1)}, f32[528,128]{1,0:T(8,128)S(1)}, u32[]{:S(2)}, u32[]{:S(2)}) collective-permute-start(f32[528,128]{1,0:T(8,128)S(1)} %get-tuple-element.45), channel_id=1, source_target_pairs={{0,24},{4,28},{8,16},{12,20},{16,8},{20,12},{24,0},{28,4},{32,56},... | collective-permute-start | bytes 811016 | tf_op jit(solution)/shard_map/ppermute | solution.py:398
  26.2 35.0 %copy-start.4 = (bf16[1,128,128]{2,1,0:T(8,128)(2,1)S(1)}, bf16[1,128,128]{2,1,0:T(8,128)(2,1)}, u32[]{:S(2)}) copy-start(bf16[1,128,128]{2,1,0:T(8,128)(2,1)} %param.9) | copy-start | bytes 98308
  26.2 35.0 %copy-start.5 = (bf16[1,128,128]{2,1,0:T(8,128)(2,1)S(1)}, bf16[1,128,128]{2,1,0:T(8,128)(2,1)}, u32[]{:S(2)}) copy-start(bf16[1,128,128]{2,1,0:T(8,128)(2,1)} %param.10) | copy-start | bytes 98308
  42.1 26.3 %collective-permute-start.4 = (f32[528,128]{1,0:T(8,128)S(1)}, f32[528,128]{1,0:T(8,128)S(1)}, u32[]{:S(2)}, u32[]{:S(2)}) collective-permute-start(f32[528,128]{1,0:T(8,128)S(1)} %get-tuple-element.46), channel_id=1, source_target_pairs={{4,100},{12,108},{20,116},{28,124},{36,68},{44,76},{52,84},{60,92}... | collective-permute-start | bytes 811016 | tf_op jit(solution)/shard_map/ppermute | solution.py:413
  49.6 18.8 %collective-permute-start.5 = (f32[528,128]{1,0:T(8,128)S(1)}, f32[528,128]{1,0:T(8,128)S(1)}, u32[]{:S(2)}, u32[]{:S(2)}) collective-permute-start(f32[528,128]{1,0:T(8,128)S(1)} %get-tuple-element.46), channel_id=1, source_target_pairs={{4,36},{12,44},{20,52},{28,60},{32,0},{40,8},{48,16},{56,24},{68,1... | collective-permute-start | bytes 811016 | tf_op jit(solution)/shard_map/ppermute | solution.py:413
  54.8 20.1 %collective-permute-start.6 = (f32[528,128]{1,0:T(8,128)S(1)}, f32[528,128]{1,0:T(8,128)S(1)}, u32[]{:S(2)}, u32[]{:S(2)}) collective-permute-start(f32[528,128]{1,0:T(8,128)S(1)} %get-tuple-element.46), channel_id=1, source_target_pairs={{4,68},{12,76},{20,84},{28,92},{36,100},{44,108},{52,116},{60,124}... | collective-permute-start | bytes 811016 | tf_op jit(solution)/shard_map/ppermute | solution.py:413
  59.5 0.8 copy-start.10
  60.4 0.8 copy-start.11
  61.2 13.8 %copy-start.6 = (bf16[128,2048]{1,0:T(8,128)(2,1)}, bf16[128,2048]{1,0:T(8,128)(2,1)S(1)}, u32[]{:S(2)}) copy-start(bf16[128,2048]{1,0:T(8,128)(2,1)S(1)} %get-tuple-element.68.high_ref) | copy-start | bytes 1572868
  61.2 13.8 %copy-start.8 = (bf16[128,2048]{1,0:T(8,128)(2,1)}, bf16[128,2048]{1,0:T(8,128)(2,1)S(1)}, u32[]{:S(2)}) copy-start(bf16[128,2048]{1,0:T(8,128)(2,1)S(1)} %get-tuple-element.69.low_ref) | copy-start | bytes 1572868
  66.4 1.0 copy-start.2
  67.4 1.0 copy-start.3
  75.6 34.5 %copy-start.14 = (f32[32]{0:T(128)S(1)}, f32[32]{0:T(128)}, u32[]{:S(2)}) copy-start(f32[32]{0:T(128)} %param.13) | copy-start | bytes 388
  105.5 7.2 %collective-permute-start.7 = (f32[2080,128]{1,0:T(8,128)S(1)}, f32[2080,128]{1,0:T(8,128)}, u32[]{:S(2)}, u32[]{:S(2)}) collective-permute-start(f32[2080,128]{1,0:T(8,128)S(1)} %bitcast.20), channel_id=1, source_target_pairs={{0,4},{4,0},{8,12},{12,8},{16,20},{20,16},{24,28},{28,24},{32,36},... | collective-permute-start | bytes 3194888 | tf_op jit(solution)/shard_map/ppermute | solution.py:418
  110.3 2.4 %copy-start.7 = (bf16[128,2048]{1,0:T(8,128)(2,1)S(1)}, bf16[128,2048]{1,0:T(8,128)(2,1)}, u32[]{:S(2)}) copy-start(bf16[128,2048]{1,0:T(8,128)(2,1)} %copy-done.6) | copy-start | bytes 1572868
  110.3 2.4 %copy-start.9 = (bf16[128,2048]{1,0:T(8,128)(2,1)S(1)}, bf16[128,2048]{1,0:T(8,128)(2,1)}, u32[]{:S(2)}) copy-start(bf16[128,2048]{1,0:T(8,128)(2,1)} %copy-done.8) | copy-start | bytes 1572868
  115.3 22.1 %collective-permute-start.10 = (f32[32]{0:T(128)S(1)}, f32[32]{0:T(128)S(1)}, u32[]{:S(2)}, u32[]{:S(2)}) collective-permute-start(f32[32]{0:T(128)S(1)} %slice_reduce_fusion), channel_id=1, source_target_pairs={{0,384},{128,256},{256,128},{384,0},{1,385},{129,257},{257,129},{3... | collective-permute-start | bytes 392 | tf_op jit(solution)/shard_map/ppermute | solution.py:373
  120.3 17.1 %collective-permute-start.8 = (f32[32]{0:T(128)S(1)}, f32[32]{0:T(128)S(1)}, u32[]{:S(2)}, u32[]{:S(2)}) collective-permute-start(f32[32]{0:T(128)S(1)} %slice_reduce_fusion), channel_id=1, source_target_pairs={{0,128},{128,0},{256,384},{384,256},{1,129},{129,1},{257,385},{385... | collective-permute-start | bytes 392 | tf_op jit(solution)/shard_map/ppermute | solution.py:373
  122.3 15.2 %collective-permute-start.9 = (f32[32]{0:T(128)S(1)}, f32[32]{0:T(128)S(1)}, u32[]{:S(2)}, u32[]{:S(2)}) collective-permute-start(f32[32]{0:T(128)S(1)} %slice_reduce_fusion), channel_id=1, source_target_pairs={{0,256},{128,384},{256,0},{384,128},{1,257},{129,385},{257,1},{385... | collective-permute-start | bytes 392 | tf_op jit(solution)/shard_map/ppermute | solution.py:373
  125.4 12.6 %all-to-all-start.1 = ((f32[4,32,256]{2,1,0:T(8,128)}), f32[4,32,256]{2,1,0:T(8,128)S(1)}, u32[]{:S(2)}, u32[]{:S(2)}) async-start(f32[4,32,256]{2,1,0:T(8,128)} %bitcast.15), calls=%async_computation.1 | async-start | bytes 262144 | tf_op jit(solution)/shard_map/all_to_all | solution.py:425

commit v5 on v4

--- a/solution.py
+++ b/solution.py
@@ -17,9 +17,10 @@
 FEATS = HEADS * PH
 QH = 8
 QR = QH * PH
-PIECE = QR + 2 * QH
+PIECE = QR + QH
+TOP = PIECE + QH
 NEAR = QR + QH
-SIDE = 2 * HEADS
+SIDE = HEADS
 VMEM_LIMIT = 48 * 1024 * 1024
 
 
@@ -66,8 +67,8 @@
 
 
 def states_kernel(own, where_ref, *refs):
-    out_ref, held = refs[6], refs[7:13]
-    fetch(refs[:6], held, refs[13])
+    out_ref, skip_ref, held = refs[6], refs[7] if own else None, refs[-7:-1]
+    fetch(refs[:6], held, refs[-1])
     x_ref, g_ref, b_ref, c_ref, step_ref, log_ref = held
     cum = running_sum(log_ref[...])
 
@@ -89,10 +90,15 @@
         summed(g_ref, jnp.exp(cum), c_ref)
 
     out_ref[FEATS : FEATS + HEADS, :] = jnp.broadcast_to(cum[:, TOK - 1 : TOK], (HEADS, NS))
-    products = jnp.sum(x_ref[...].astype(F32) * g_ref[...].astype(F32), axis=0, keepdims=True)
-    owner = (iota((HEADS, FEATS), 1) // PH == iota((HEADS, FEATS), 0)).astype(F32)
-    skips = jnp.sum(owner * products, axis=1, keepdims=True)
-    out_ref[FEATS + HEADS : FEATS + SIDE, :] = jnp.broadcast_to(skips, (HEADS, NS))
+    if own:
+        products = jnp.sum(x_ref[...].astype(F32) * g_ref[...].astype(F32), axis=0, keepdims=True)
+        owner = (iota((HEADS, FEATS), 1) // PH == iota((HEADS, FEATS), 0)).astype(F32)
+        sums = jnp.sum(owner * products, axis=1, keepdims=True)
+        lane = iota((QH, NS), 1) // 32
+        tile = jnp.where(lane == 0, sums[:QH, :], 0.0)
+        for quarter in range(1, 4):
+            tile = jnp.where(lane == quarter, sums[quarter * QH : (quarter + 1) * QH, :], tile)
+        skip_ref[...] = tile
 
 
 def chip_kernel(where_ref, got_ref, own_ref, *out_refs):
@@ -106,12 +112,10 @@
             rows = pl.ds(pl.multiple_of(quarter * QR + j * PH, PH), PH)
             out_ref[j * PH : (j + 1) * PH, :] = decay[j : j + 1, :] * got_ref[rows, :] + own_ref[rows, :]
         out_ref[QR : QR + QH, :] = logs + got_logs
-        rows = pl.ds(pl.multiple_of(FEATS + HEADS + quarter * QH, QH), QH)
-        out_ref[QR + QH : PIECE, :] = own_ref[rows, :] + got_ref[rows, :]
 
 
 def group_kernel(where_ref, *refs):
-    got, out_ref, parts_ref = refs[:4], refs[4], refs[5]
+    got, skip_ref, out_ref, parts_ref = refs[:4], refs[4], refs[5], refs[6]
     forward = where_ref[0] == 1
     place = where_ref[2]
     for k in range(4):
@@ -126,9 +130,10 @@
         out_ref[j * PH : (j + 1) * PH, :] = (terms[0] + terms[1]) + (terms[2] + terms[3])
     side = [parts_ref[k * PIECE + QR : (k + 1) * PIECE, :] for k in range(4)]
     out_ref[QR:PIECE, :] = (side[0] + side[1]) + (side[2] + side[3])
-
-
-def prefix_kernel(where_ref, parts_ref, *refs):
+    out_ref[PIECE:TOP, :] = skip_ref[...]
+
+
+def prefix_kernel(where_ref, parts_ref, skip_ref, *refs):
     forward = where_ref[0] == 1
     me = where_ref[1]
     group = [jnp.bitwise_xor(me, k) for k in range(4)]
@@ -153,10 +158,9 @@
                 out_ref[k * NEAR + j * PH : k * NEAR + (j + 1) * PH, :] = state
                 if k != sequence[-1]:
                     state = decays[k][at, :] * state + parts_ref[k * PIECE + j * PH : k * PIECE + (j + 1) * PH, :]
-        skips = tops[0][QR + QH :, :] + tops[1][QR + QH :, :] + tops[2][QR + QH :, :]
+        skips = tops[0][PIECE:, :] + tops[1][PIECE:, :] + tops[2][PIECE:, :]
         if carries_own:
-            for k in range(4):
-                skips = skips + parts_ref[k * PIECE + QR + QH : (k + 1) * PIECE, :]
+            skips = skips + skip_ref[...]
         for k in range(4):
             out_ref[k * NEAR + QR : (k + 1) * NEAR, :] = skips
 
@@ -250,9 +254,8 @@
 def far_maps_kernel(where_ref, high_ref, low_ref, near_ref, far_ref, maps_in_ref, near_maps_ref, maps_ref, skip_ref):
     forward = where_ref[0] == 1
     other = weighted_sum(high_ref, low_ref, lambda quarter: far_ref[quarter * NEAR : quarter * NEAR + QR, :])
-    for quarter in range(4):
-        side = slice(quarter * NEAR + QR, (quarter + 1) * NEAR)
-        skip_ref[quarter * QH : (quarter + 1) * QH, :] = near_ref[side, :] + far_ref[side, :]
+    sides = [slice(quarter * NEAR + QR, (quarter + 1) * NEAR) for quarter in range(4)]
+    skip_ref[...] = sum([near_ref[side, :] + far_ref[side, :] for side in sides], jnp.zeros((QH, NS), F32))
     mine = near_maps_ref[...]
     maps_ref[:, :NS] = maps_in_ref[:, :NS] + jnp.where(forward, other, mine)
     maps_ref[:, NS:] = maps_in_ref[:, NS:] + jnp.where(forward, mine, other)
@@ -387,11 +390,12 @@
     def states(own):
         scratch = [pltpu.VMEM(v.shape, v.dtype) for v in slab_inputs] + [pltpu.SemaphoreType.DMA((6,))]
         kernel = lambda *refs: states_kernel(own, *refs)
-        return call(kernel, [((FEATS + SIDE, NS), F32)], 0, 6, scratch)(where, *slab_inputs)[0]
-
-    send = states(False)
+        outs = [((FEATS + SIDE, NS), F32)] + ([((QH, NS), F32)] if own else [])
+        return call(kernel, outs, 0, 6, scratch)(where, *slab_inputs)
+
+    (send,) = states(False)
     first = lax.ppermute(send, "ctx", core_pairs(n))
-    own = states(True)
+    own, skip = states(True)
     parts = list(call(chip_kernel, [((PIECE, NS), F32)] * 4, 2)(where, first, own))
     *slab_inputs, parts[0] = lax.optimization_barrier((*slab_inputs, parts[0]))
     x, g, b, c, steps, logs = slab_inputs
@@ -409,16 +413,19 @@
         [pltpu.VMEM((TOK, TOK), F32)],
     )(*slab_inputs, parts[0])
 
-    total, placed = call(group_kernel, [((PIECE, NS), F32), ((4 * PIECE, NS), F32)], 4)(where, *mine)
+    mine[1], skip = lax.optimization_barrier((mine[1], skip))
+    skip = skip + partners(skip, "dp", 1) + partners(skip, "dp", 2) + partners(skip, "dp", 3)
+    skip = skip + lax.ppermute(skip, "ctx", core_pairs(n))
+    total, placed = call(group_kernel, [((TOP, NS), F32), ((4 * PIECE, NS), F32)], 5)(where, *mine, skip)
     tops = [lax.ppermute(total, "ctx", group_pairs(n, k)) for k in range(1, 4)]
     weights = call(weights_kernel, [((TOK, FEATS), BF16)] * 4, 5)(where, x, g, steps, logs, parts[0])
     tops[-1], within, back, maps, *weights = lax.optimization_barrier((tops[-1], within, back, maps, *weights))
-    (ready,) = call(prefix_kernel, [((4 * NEAR, NS), F32)], 4)(where, placed, *tops)
+    (ready,) = call(prefix_kernel, [((4 * NEAR, NS), F32)], 5)(where, placed, skip, *tops)
     near = lax.all_to_all(ready, "ctx", 0, 0, axis_index_groups=groups, tiled=True)
     far = lax.ppermute(near, "ctx", core_pairs(n))
     halves = [pltpu.VMEM((TOK, FEATS), BF16)] * 2 + [pltpu.SemaphoreType.DMA((2,))]
     (near_maps,) = call(near_maps_kernel, [((TOK, NS), F32)], 2, 2, halves)(where, *weights[:2], near, first)
-    maps, skips = call(far_maps_kernel, [((TOK, 2 * NS), F32), ((HEADS, NS), F32)], 6)(
+    maps, skips = call(far_maps_kernel, [((TOK, 2 * NS), F32), ((QH, NS), F32)], 6)(
         where, *weights[2:], near, far, maps, near_maps
     )
     tp = lax.axis_size("tp")
@@ -429,8 +436,7 @@
         where, within, back, x, g, steps, logs, gains, b, c, near, far, first
     )
     reduced = jnp.sum(swapped, axis=0)
-    skip = skips[:, 0]
-    skip_total = skip + partners(skip, "dp", 1) + partners(skip, "dp", 2) + partners(skip, "dp", 3)
+    skip_total = skips[:, ::32].T.reshape(HEADS)
     factor = 1.0 / math.sqrt(lax.axis_size("dp") * TOK * n * PH)
     return (
         mixed[None],

time: 140 us -> 134 us (0.957)
  waiting for transfers between devices: 21.7 us -> 9.92 us
  starting transfers between devices: 53.1 us -> 59.7 us
    ppermute x3, waiting for transfers between devices: 15.2 us -> 1.9 us  [shards(): lax.ppermute(parts[k], 'ctx', chip_pairs(n, k))]
    ppermute x3, starting transfers between devices: 15.8 us -> 20 us  [shards(): tops = [lax.ppermute(total, 'ctx', group_pairs(n, k)) for k in range(1, 4)]]
    ppermute x0 -> x1, starting transfers between devices: none -> 3.93 us  [shards(): skip = skip + lax.ppermute(skip, 'ctx', core_pairs(n))]
    ppermute x1, starting transfers between devices: 4.61 us -> 1.91 us  [shards(): far = lax.ppermute(near, 'ctx', core_pairs(n))]
    all_to_all x1, starting transfers between devices: 4.38 us -> 5.99 us  [shards(): swapped = lax.all_to_all(maps.reshape(tp, TOK // tp, 2 * NS), 'tp', 0, 0)]
  transfers between devices with their start and end apart: 12 -> 13, of which waited for: 3 -> 6; matrix products, arithmetic and copies ran while one was open for 0% -> 1% of each run, Pallas kernels for 14% -> 15%
where the time goes in v5:
time: 134 us; the launch traced here: 133 us
  starting transfers between devices  59.7 us (45%)
  blocking collectives  29.7 us (22%)
  Pallas kernels  27.7 us (21%)
  waiting for transfers between devices  9.92 us (7%)
  local copies, waits for them, and re-layouts  5.11 us (4%)
    all_to_all x1, blocking collectives, shards(): lax.all_to_all(ready, 'ctx', 0, 0, axis_index_groups=groups, tiled=True)  29.7 us
    pallas_call x9, Pallas kernels, place(): return run(where, *far, *arrays[n_far:])  22.5 us
    ppermute x3, starting transfers between devices, shards(): tops = [lax.ppermute(total, 'ctx', group_pairs(n, k)) for k in range(1, 4)]  20 us
    ppermute x3, starting transfers between devices, partners(): lax.ppermute(value, axis, [(i, i ^ k) for i in range(n) if i ^ k < n])  9.57 us
    ppermute x3, starting transfers between devices, shards(): lax.ppermute(parts[k], 'ctx', chip_pairs(n, k))  9.4 us
    ppermute x1, starting transfers between devices, shards(): first = lax.ppermute(send, 'ctx', core_pairs(n))  8.82 us
    all_to_all x1, starting transfers between devices, shards(): swapped = lax.all_to_all(maps.reshape(tp, TOK // tp, 2 * NS), 'tp', 0, 0)  5.99 us
    ppermute x3, waiting for transfers between devices, shards(): tops = [lax.ppermute(total, 'ctx', group_pairs(n, k)) for k in range(1, 4)]  5.88 us
  transfers between devices with their start and end apart: 13, of which 6 were waited for; matrix products, arithmetic and copies ran while one was open for 1% of the time, Pallas kernels for 15%

profile of v5, /device:TPU:1, one launch (start us, length us, event | category | flops | bytes accessed | tf_op | source)
XLA Modules:
  0.0 133.2 jit_solution(9298454094342006511)
XLA Ops:
  0.7 0.1 pad_add_fusion.refs_0_.where_ref
  0.7 3.1 %shard_map.126 = f32[2080,128]{1,0:T(8,128)S(1)} custom-call(s32[3]{0:T(128)S(1)} %pad_add_fusion.refs_0_.where_ref, bf16[128,2048]{1,0:T(8,128)(2,1)} %bitcast.26, bf16[128,2048]{1,0:T(8,128)(2,1)} %bitcast.31, bf16[128,128]{1,0:T(8,128)(2,1)} %bitcast.37, bf16[128,128]{1,0:T(8,128)(2,1)} %bitcast.41, f32[32,128]{1,0:T(8,128)} %bitcast.45, f32[32,128]{1,0:T(8,128)} %bitcast.50), custom_call_target="tpu_custom_call" | custom-call | tf_op jit(solution)/shard_map/pallas_call | solution.py:344
  3.8 8.8 %collective-permute-start = (f32[2080,128]{1,0:T(8,128)S(1)}, f32[2080,128]{1,0:T(8,128)S(1)}, u32[]{:S(2)}, u32[]{:S(2)}) collective-permute-start(f32[2080,128]{1,0:T(8,128)S(1)} %shard_map.126), channel_id=1, source_target_pairs={{0,4},{4,0},{8,12},{12,8},{16,20},{20,16},{24,28},{28,24},{32,36},... | collective-permute-start | bytes 3194888 | tf_op jit(solution)/shard_map/ppermute | solution.py:397
  12.7 3.2 %shard_map.127 = (f32[2080,128]{1,0:T(8,128)S(1)}, f32[8,128]{1,0:T(8,128)S(1)}) custom-call(s32[3]{0:T(128)S(1)} %pad_add_fusion.refs_0_.where_ref, bf16[128,2048]{1,0:T(8,128)(2,1)} %bitcast.27, bf16[128,2048]{1,0:T(8,128)(2,1)} %bitcast.32, bf16[128,128]{1,0:T(8,128)(2,1)} %bitcast.38, bf16[128,128]{1,0:T(8,128)(2,1)} %bitcast.42, f32[32,128]{1,0:T(8,128)} %bitcast.46, ...), custom_call_target="tpu_custom_call" | custom-call | tf_op jit(solution)/shard_map/pallas_call | solution.py:344
  15.9 0.0 collective-permute-done.got_ref.first_ref
  15.9 0.7 shard_map.128
  16.6 0.0 copy-start
  16.6 0.0 copy-start.1
  16.6 0.0 copy-start.12
  16.6 0.0 copy-start.13
  16.7 2.1 %collective-permute-start.1 = (f32[520,128]{1,0:T(8,128)S(1)}, f32[520,128]{1,0:T(8,128)S(1)}, u32[]{:S(2)}, u32[]{:S(2)}) collective-permute-start(f32[520,128]{1,0:T(8,128)S(1)} %get-tuple-element.48), channel_id=1, source_target_pairs={{0,8},{4,12},{8,0},{12,4},{16,24},{20,28},{24,16},{28,20},{32,40},... | collective-permute-start | bytes 798728 | tf_op jit(solution)/shard_map/ppermute | solution.py:402
  18.7 1.9 %collective-permute-start.2 = (f32[520,128]{1,0:T(8,128)S(1)}, f32[520,128]{1,0:T(8,128)S(1)}, u32[]{:S(2)}, u32[]{:S(2)}) collective-permute-start(f32[520,128]{1,0:T(8,128)S(1)} %get-tuple-element.51), channel_id=1, source_target_pairs={{0,16},{4,20},{8,24},{12,28},{16,0},{20,4},{24,8},{28,12},{32,48},... | collective-permute-start | bytes 798728 | tf_op jit(solution)/shard_map/ppermute | solution.py:402
  20.6 5.4 %collective-permute-start.3 = (f32[520,128]{1,0:T(8,128)S(1)}, f32[520,128]{1,0:T(8,128)S(1)}, u32[]{:S(2)}, u32[]{:S(2)}) collective-permute-start(f32[520,128]{1,0:T(8,128)S(1)} %get-tuple-element.52), channel_id=1, source_target_pairs={{0,24},{4,28},{8,16},{12,20},{16,8},{20,12},{24,0},{28,4},{32,56},... | collective-permute-start | bytes 798728 | tf_op jit(solution)/shard_map/ppermute | solution.py:402
  26.1 1.9 %collective-permute-done.1.refs_1_ = f32[520,128]{1,0:T(8,128)S(1)} collective-permute-done((f32[520,128]{1,0:T(8,128)S(1)}, f32[520,128]{1,0:T(8,128)S(1)}, u32[]{:S(2)}, u32[]{:S(2)}) %collective-permute-start.1) | collective-permute-done | bytes 266272 | tf_op jit(solution)/shard_map/ppermute | solution.py:402
  28.0 1.9 %collective-permute-start.4 = (f32[8,128]{1,0:T(8,128)S(1)}, f32[8,128]{1,0:T(8,128)S(1)}, u32[]{:S(2)}, u32[]{:S(2)}) collective-permute-start(f32[8,128]{1,0:T(8,128)S(1)} %get-tuple-element.53), channel_id=1, source_target_pairs={{0,128},{128,0},{256,384},{384,256},{1,129},{129,1},{257,385},{385... | collective-permute-start | bytes 12296 | tf_op jit(solution)/shard_map/ppermute | solution.py:376
  29.9 2.8 %collective-permute-start.5 = (f32[8,128]{1,0:T(8,128)S(1)}, f32[8,128]{1,0:T(8,128)S(1)}, u32[]{:S(2)}, u32[]{:S(2)}) collective-permute-start(f32[8,128]{1,0:T(8,128)S(1)} %get-tuple-element.53), channel_id=1, source_target_pairs={{0,256},{128,384},{256,0},{384,128},{1,257},{129,385},{257,1},{385... | collective-permute-start | bytes 12296 | tf_op jit(solution)/shard_map/ppermute | solution.py:376
  32.7 4.9 %collective-permute-start.6 = (f32[8,128]{1,0:T(8,128)S(1)}, f32[8,128]{1,0:T(8,128)S(1)}, u32[]{:S(2)}, u32[]{:S(2)}) collective-permute-start(f32[8,128]{1,0:T(8,128)S(1)} %get-tuple-element.53), channel_id=1, source_target_pairs={{0,384},{128,256},{256,128},{384,0},{1,385},{129,257},{257,129},{3... | collective-permute-start | bytes 12296 | tf_op jit(solution)/shard_map/ppermute | solution.py:376
  37.6 0.0 collective-permute-done.4
  37.6 0.0 collective-permute-done.5
  37.6 1.1 collective-permute-done.6
  38.7 3.9 %collective-permute-start.7 = (f32[8,128]{1,0:T(8,128)S(1)}, f32[8,128]{1,0:T(8,128)S(1)}, u32[]{:S(2)}, u32[]{:S(2)}) collective-permute-start(f32[8,128]{1,0:T(8,128)S(1)} %add_add_fusion), channel_id=1, source_target_pairs={{0,4},{4,0},{8,12},{12,8},{16,20},{20,16},{24,28},{28,24},{32,36},... | collective-permute-start | bytes 12296 | tf_op jit(solution)/shard_map/ppermute | solution.py:418
  42.6 0.8 collective-permute-done.7
  43.4 0.0 collective-permute-done.2.refs_2_
  43.4 0.0 collective-permute-done.3.refs_3_
  43.5 0.7 shard_map.129
  44.2 11.7 %collective-permute-start.8 = (f32[528,128]{1,0:T(8,128)S(1)}, f32[528,128]{1,0:T(8,128)S(1)}, u32[]{:S(2)}, u32[]{:S(2)}) collective-permute-start(f32[528,128]{1,0:T(8,128)S(1)} %get-tuple-element.54), channel_id=1, source_target_pairs={{4,100},{12,108},{20,116},{28,124},{36,68},{44,76},{52,84},{60,92}... | collective-permute-start | bytes 811016 | tf_op jit(solution)/shard_map/ppermute | solution.py:420
  55.9 4.3 %collective-permute-start.10 = (f32[528,128]{1,0:T(8,128)S(1)}, f32[528,128]{1,0:T(8,128)S(1)}, u32[]{:S(2)}, u32[]{:S(2)}) collective-permute-start(f32[528,128]{1,0:T(8,128)S(1)} %get-tuple-element.54), channel_id=1, source_target_pairs={{4,68},{12,76},{20,84},{28,92},{36,100},{44,108},{52,116},{60,124}... | collective-permute-start | bytes 811016 | tf_op jit(solution)/shard_map/ppermute | solution.py:420
  60.2 4.0 %collective-permute-start.9 = (f32[528,128]{1,0:T(8,128)S(1)}, f32[528,128]{1,0:T(8,128)S(1)}, u32[]{:S(2)}, u32[]{:S(2)}) collective-permute-start(f32[528,128]{1,0:T(8,128)S(1)} %get-tuple-element.54), channel_id=1, source_target_pairs={{4,36},{12,44},{20,52},{28,60},{32,0},{40,8},{48,16},{56,24},{68,1... | collective-permute-start | bytes 811016 | tf_op jit(solution)/shard_map/ppermute | solution.py:420
  64.2 0.0 copy-done
  64.2 0.0 copy-done.1
  64.2 0.0 copy-done.12
  64.2 0.0 copy-done.13
  64.2 1.6 %shard_map.131 = (bf16[128,2048]{1,0:T(8,128)(2,1)S(1)}, bf16[128,2048]{1,0:T(8,128)(2,1)S(1)}, bf16[128,2048]{1,0:T(8,128)(2,1)S(1)}, bf16[128,2048]{1,0:T(8,128)(2,1)S(1)}) custom-call(s32[3]{0:T(128)S(1)} %pad_add_fusion.refs_0_.where_ref, bf16[128,2048]{1,0:T(8,128)(2,1)S(1)} %bitcast.28, bf16[128,2048]{1,0:T(8,128)(2,1)S(1)} %bitcast.33, ...), custom_call_target="tpu_custom_call" | custom-call | tf_op jit(solution)/shard_map/pallas_call | solution.py:344
  65.8 0.0 copy-start.10
  65.8 0.8 copy-done.10
  66.6 0.8 copy-done.11
  67.4 0.0 copy-done.4
  67.4 0.0 copy-done.5
  67.4 5.3 %shard_map.130 = (f32[128,2048]{1,0:T(8,128)S(1)}, f32[128,2048]{1,0:T(8,128)S(1)}, f32[128,256]{1,0:T(8,128)S(1)}) custom-call(bf16[128,2048]{1,0:T(8,128)(2,1)S(1)} %bitcast.29, bf16[128,2048]{1,0:T(8,128)(2,1)S(1)} %bitcast.34, bf16[128,128]{1,0:T(8,128)(2,1)S(1)} %bitcast.39, bf16[128,128]{1,0:T(8,128)(2,1)S(1)} %bitcast.43, f32[32,128]{1,0:T(8,128)S(1)} %bitcast.48, ...), custom_call_target="tpu_custom_call" | custom-call | tf_op jit(solution)/shard_map/pallas_call | solution.py:408
  72.7 0.0 copy-start.2
  72.7 1.0 copy-done.2
  73.7 1.0 copy-done.3
  74.7 4.5 %collective-permute-done.8.refs_2_ = f32[528,128]{1,0:T(8,128)S(1)} collective-permute-done((f32[528,128]{1,0:T(8,128)S(1)}, f32[528,128]{1,0:T(8,128)S(1)}, u32[]{:S(2)}, u32[]{:S(2)}) %collective-permute-start.8) | collective-permute-done | bytes 270368 | tf_op jit(solution)/shard_map/ppermute | solution.py:420
  79.2 0.0 collective-permute-done.10.refs_1_
  79.2 1.4 %collective-permute-done.9.refs_0_ = f32[528,128]{1,0:T(8,128)S(1)} collective-permute-done((f32[528,128]{1,0:T(8,128)S(1)}, f32[528,128]{1,0:T(8,128)S(1)}, u32[]{:S(2)}, u32[]{:S(2)}) %collective-permute-start.9) | collective-permute-done | bytes 270368 | tf_op jit(solution)/shard_map/ppermute | solution.py:420
  80.5 0.0 copy-done.6
  80.6 0.7 shard_map.132
  81.2 0.0 copy-start.14
  81.2 29.7 %all_to_all.16 = f32[4,520,128]{2,1,0:T(8,128)S(1)} all-to-all(f32[4,520,128]{2,1,0:T(8,128)S(1)} %bitcast.36), channel_id=1, replica_groups={{0,8,16,24},{4,12,20,28},{32,40,48,56},{36,44,52,60},{64,72,80,88},{68,..., dimensions={0} | all-to-all | bytes 2129920 | tf_op jit(solution)/shard_map/all_to_all | solution.py:424
  111.0 1.9 %collective-permute-start.11 = (f32[2080,128]{1,0:T(8,128)S(1)}, f32[2080,128]{1,0:T(8,128)}, u32[]{:S(2)}, u32[]{:S(2)}) collective-permute-start(f32[2080,128]{1,0:T(8,128)S(1)} %bitcast.22), channel_id=1, source_target_pairs={{0,4},{4,0},{8,12},{12,8},{16,20},{20,16},{24,28},{28,24},{32,36},... | collective-permute-start | bytes 3194888 | tf_op jit(solution)/shard_map/ppermute | solution.py:425
  112.9 0.0 copy-done.14
  112.9 0.1 broadcast_in_dim.21
  113.0 0.1 broadcast_in_dim_reshape.3.gain_ref
  113.1 0.0 copy-start.9
  113.1 2.4 %shard_map.134.near_maps_ref = f32[128,128]{1,0:T(8,128)S(1)} custom-call(s32[3]{0:T(128)S(1)} %pad_add_fusion.refs_0_.where_ref, bf16[128,2048]{1,0:T(8,128)(2,1)} %copy-done.10, bf16[128,2048]{1,0:T(8,128)(2,1)} %copy-done.11, f32[2080,128]{1,0:T(8,128)S(1)} %bitcast.23, f32[2080,128]{1,0:T(8,128)S(1)} %collective-permute-done.got_ref.first_ref), custom_call_target="tpu_custom_call" | custom-call | tf_op jit(solution)/shard_map/pallas_call | solution.py:344
  115.4 0.2 collective-permute-done.11.far_ref
  115.7 2.5 %shard_map.135 = (f32[128,256]{1,0:T(8,128)}, f32[8,128]{1,0:T(8,128)S(1)}) custom-call(s32[3]{0:T(128)S(1)} %pad_add_fusion.refs_0_.where_ref, bf16[128,2048]{1,0:T(8,128)(2,1)S(1)} %copy-done.7, bf16[128,2048]{1,0:T(8,128)(2,1)S(1)} %copy-done.9, f32[2080,128]{1,0:T(8,128)S(1)} %bitcast.24, f32[2080,128]{1,0:T(8,128)} %collective-permute-done.11.far_ref, ...), custom_call_target="tpu_custom_call" | custom-call | tf_op jit(solution)/shard_map/pallas_call | solution.py:344
  118.2 6.0 %all-to-all-start.1 = ((f32[4,32,256]{2,1,0:T(8,128)}), f32[4,32,256]{2,1,0:T(8,128)S(1)}, u32[]{:S(2)}, u32[]{:S(2)}) async-start(f32[4,32,256]{2,1,0:T(8,128)} %bitcast.15), calls=%async_computation.1 | async-start | bytes 262144 | tf_op jit(solution)/shard_map/all_to_all | solution.py:432
  124.2 0.1 slice.11
  124.2 0.1 copy.14
  124.3 0.6 mul.15
  124.9 7.7 %shard_map.133 = (bf16[128,2048]{1,0:T(8,128)(2,1)}, bf16[128,2048]{1,0:T(8,128)(2,1)}, f32[32,128]{1,0:T(8,128)}, f32[32,128]{1,0:T(8,128)}) custom-call(s32[3]{0:T(128)S(1)} %pad_add_fusion.refs_0_.where_ref, f32[128,2048]{1,0:T(8,128)} %copy-done.2, f32[128,2048]{1,0:T(8,128)} %copy-done.3, bf16[128,2048]{1,0:T(8,128)(2,1)S(1)} %bitcast.30, ...), custom_call_target="tpu_custom_call" | custom-call | tf_op jit(solution)/shard_map/pallas_call | solution.py:344
  132.6 0.0 all-to-all-done.1
  132.6 0.6 slice_bitcast_fusion
  (14 shorter events, 0.0 us)
Async XLA Ops:
  3.8 12.0 %collective-permute-start = (f32[2080,128]{1,0:T(8,128)S(1)}, f32[2080,128]{1,0:T(8,128)S(1)}, u32[]{:S(2)}, u32[]{:S(2)}) collective-permute-start(f32[2080,128]{1,0:T(8,128)S(1)} %shard_map.126), channel_id=1, source_target_pairs={{0,4},{4,0},{8,12},{12,8},{16,20},{20,16},{24,28},{28,24},{32,36},... | collective-permute-start | bytes 3194888 | tf_op jit(solution)/shard_map/ppermute | solution.py:397
  16.6 47.6 %copy-start = (bf16[1,128,2048]{2,1,0:T(8,128)(2,1)S(1)}, bf16[1,128,2048]{2,1,0:T(8,128)(2,1)}, u32[]{:S(2)}) copy-start(bf16[1,128,2048]{2,1,0:T(8,128)(2,1)} %param.7) | copy-start | bytes 1572868
  16.6 47.6 %copy-start.1 = (bf16[1,128,2048]{2,1,0:T(8,128)(2,1)S(1)}, bf16[1,128,2048]{2,1,0:T(8,128)(2,1)}, u32[]{:S(2)}) copy-start(bf16[1,128,2048]{2,1,0:T(8,128)(2,1)} %param.8) | copy-start | bytes 1572868
  16.6 47.6 %copy-start.12 = (f32[1,32,128]{2,1,0:T(8,128)S(1)}, f32[1,32,128]{2,1,0:T(8,128)}, u32[]{:S(2)}) copy-start(f32[1,32,128]{2,1,0:T(8,128)} %param.11) | copy-start | bytes 49156
  16.6 47.6 %copy-start.13 = (f32[1,32,128]{2,1,0:T(8,128)S(1)}, f32[1,32,128]{2,1,0:T(8,128)}, u32[]{:S(2)}) copy-start(f32[1,32,128]{2,1,0:T(8,128)} %param.12) | copy-start | bytes 49156
  16.7 11.3 %collective-permute-start.1 = (f32[520,128]{1,0:T(8,128)S(1)}, f32[520,128]{1,0:T(8,128)S(1)}, u32[]{:S(2)}, u32[]{:S(2)}) collective-permute-start(f32[520,128]{1,0:T(8,128)S(1)} %get-tuple-element.48), channel_id=1, source_target_pairs={{0,8},{4,12},{8,0},{12,4},{16,24},{20,28},{24,16},{28,20},{32,40},... | collective-permute-start | bytes 798728 | tf_op jit(solution)/shard_map/ppermute | solution.py:402
  18.7 24.7 %collective-permute-start.2 = (f32[520,128]{1,0:T(8,128)S(1)}, f32[520,128]{1,0:T(8,128)S(1)}, u32[]{:S(2)}, u32[]{:S(2)}) collective-permute-start(f32[520,128]{1,0:T(8,128)S(1)} %get-tuple-element.51), channel_id=1, source_target_pairs={{0,16},{4,20},{8,24},{12,28},{16,0},{20,4},{24,8},{28,12},{32,48},... | collective-permute-start | bytes 798728 | tf_op jit(solution)/shard_map/ppermute | solution.py:402
  20.6 22.8 %collective-permute-start.3 = (f32[520,128]{1,0:T(8,128)S(1)}, f32[520,128]{1,0:T(8,128)S(1)}, u32[]{:S(2)}, u32[]{:S(2)}) collective-permute-start(f32[520,128]{1,0:T(8,128)S(1)} %get-tuple-element.52), channel_id=1, source_target_pairs={{0,24},{4,28},{8,16},{12,20},{16,8},{20,12},{24,0},{28,4},{32,56},... | collective-permute-start | bytes 798728 | tf_op jit(solution)/shard_map/ppermute | solution.py:402
  28.0 9.6 %collective-permute-start.4 = (f32[8,128]{1,0:T(8,128)S(1)}, f32[8,128]{1,0:T(8,128)S(1)}, u32[]{:S(2)}, u32[]{:S(2)}) collective-permute-start(f32[8,128]{1,0:T(8,128)S(1)} %get-tuple-element.53), channel_id=1, source_target_pairs={{0,128},{128,0},{256,384},{384,256},{1,129},{129,1},{257,385},{385... | collective-permute-start | bytes 12296 | tf_op jit(solution)/shard_map/ppermute | solution.py:376
  29.9 7.7 %collective-permute-start.5 = (f32[8,128]{1,0:T(8,128)S(1)}, f32[8,128]{1,0:T(8,128)S(1)}, u32[]{:S(2)}, u32[]{:S(2)}) collective-permute-start(f32[8,128]{1,0:T(8,128)S(1)} %get-tuple-element.53), channel_id=1, source_target_pairs={{0,256},{128,384},{256,0},{384,128},{1,257},{129,385},{257,1},{385... | collective-permute-start | bytes 12296 | tf_op jit(solution)/shard_map/ppermute | solution.py:376
  32.7 6.0 %collective-permute-start.6 = (f32[8,128]{1,0:T(8,128)S(1)}, f32[8,128]{1,0:T(8,128)S(1)}, u32[]{:S(2)}, u32[]{:S(2)}) collective-permute-start(f32[8,128]{1,0:T(8,128)S(1)} %get-tuple-element.53), channel_id=1, source_target_pairs={{0,384},{128,256},{256,128},{384,0},{1,385},{129,257},{257,129},{3... | collective-permute-start | bytes 12296 | tf_op jit(solution)/shard_map/ppermute | solution.py:376
  38.7 4.7 %collective-permute-start.7 = (f32[8,128]{1,0:T(8,128)S(1)}, f32[8,128]{1,0:T(8,128)S(1)}, u32[]{:S(2)}, u32[]{:S(2)}) collective-permute-start(f32[8,128]{1,0:T(8,128)S(1)} %add_add_fusion), channel_id=1, source_target_pairs={{0,4},{4,0},{8,12},{12,8},{16,20},{20,16},{24,28},{28,24},{32,36},... | collective-permute-start | bytes 12296 | tf_op jit(solution)/shard_map/ppermute | solution.py:418
  43.4 24.0 %copy-start.4 = (bf16[1,128,128]{2,1,0:T(8,128)(2,1)S(1)}, bf16[1,128,128]{2,1,0:T(8,128)(2,1)}, u32[]{:S(2)}) copy-start(bf16[1,128,128]{2,1,0:T(8,128)(2,1)} %param.9) | copy-start | bytes 98308
  43.4 24.0 %copy-start.5 = (bf16[1,128,128]{2,1,0:T(8,128)(2,1)S(1)}, bf16[1,128,128]{2,1,0:T(8,128)(2,1)}, u32[]{:S(2)}) copy-start(bf16[1,128,128]{2,1,0:T(8,128)(2,1)} %param.10) | copy-start | bytes 98308
  44.2 35.0 %collective-permute-start.8 = (f32[528,128]{1,0:T(8,128)S(1)}, f32[528,128]{1,0:T(8,128)S(1)}, u32[]{:S(2)}, u32[]{:S(2)}) collective-permute-start(f32[528,128]{1,0:T(8,128)S(1)} %get-tuple-element.54), channel_id=1, source_target_pairs={{4,100},{12,108},{20,116},{28,124},{36,68},{44,76},{52,84},{60,92}... | collective-permute-start | bytes 811016 | tf_op jit(solution)/shard_map/ppermute | solution.py:420
  55.9 23.3 %collective-permute-start.10 = (f32[528,128]{1,0:T(8,128)S(1)}, f32[528,128]{1,0:T(8,128)S(1)}, u32[]{:S(2)}, u32[]{:S(2)}) collective-permute-start(f32[528,128]{1,0:T(8,128)S(1)} %get-tuple-element.54), channel_id=1, source_target_pairs={{4,68},{12,76},{20,84},{28,92},{36,100},{44,108},{52,116},{60,124}... | collective-permute-start | bytes 811016 | tf_op jit(solution)/shard_map/ppermute | solution.py:420
  60.2 20.4 %collective-permute-start.9 = (f32[528,128]{1,0:T(8,128)S(1)}, f32[528,128]{1,0:T(8,128)S(1)}, u32[]{:S(2)}, u32[]{:S(2)}) collective-permute-start(f32[528,128]{1,0:T(8,128)S(1)} %get-tuple-element.54), channel_id=1, source_target_pairs={{4,36},{12,44},{20,52},{28,60},{32,0},{40,8},{48,16},{56,24},{68,1... | collective-permute-start | bytes 811016 | tf_op jit(solution)/shard_map/ppermute | solution.py:420
  65.8 0.8 copy-start.10
  66.6 0.8 copy-start.11
  67.4 13.1 %copy-start.6 = (bf16[128,2048]{1,0:T(8,128)(2,1)}, bf16[128,2048]{1,0:T(8,128)(2,1)S(1)}, u32[]{:S(2)}) copy-start(bf16[128,2048]{1,0:T(8,128)(2,1)S(1)} %get-tuple-element.76.high_ref) | copy-start | bytes 1572868
  67.4 13.1 %copy-start.8 = (bf16[128,2048]{1,0:T(8,128)(2,1)}, bf16[128,2048]{1,0:T(8,128)(2,1)S(1)}, u32[]{:S(2)}) copy-start(bf16[128,2048]{1,0:T(8,128)(2,1)S(1)} %get-tuple-element.77.low_ref) | copy-start | bytes 1572868
  72.7 1.0 copy-start.2
  73.7 1.0 copy-start.3
  81.2 31.7 %copy-start.14 = (f32[32]{0:T(128)S(1)}, f32[32]{0:T(128)}, u32[]{:S(2)}) copy-start(f32[32]{0:T(128)} %param.13) | copy-start | bytes 388
  111.0 4.7 %collective-permute-start.11 = (f32[2080,128]{1,0:T(8,128)S(1)}, f32[2080,128]{1,0:T(8,128)}, u32[]{:S(2)}, u32[]{:S(2)}) collective-permute-start(f32[2080,128]{1,0:T(8,128)S(1)} %bitcast.22), channel_id=1, source_target_pairs={{0,4},{4,0},{8,12},{12,8},{16,20},{20,16},{24,28},{28,24},{32,36},... | collective-permute-start | bytes 3194888 | tf_op jit(solution)/shard_map/ppermute | solution.py:425
  113.1 2.6 %copy-start.7 = (bf16[128,2048]{1,0:T(8,128)(2,1)S(1)}, bf16[128,2048]{1,0:T(8,128)(2,1)}, u32[]{:S(2)}) copy-start(bf16[128,2048]{1,0:T(8,128)(2,1)} %copy-done.6) | copy-start | bytes 1572868
  113.1 2.6 %copy-start.9 = (bf16[128,2048]{1,0:T(8,128)(2,1)S(1)}, bf16[128,2048]{1,0:T(8,128)(2,1)}, u32[]{:S(2)}) copy-start(bf16[128,2048]{1,0:T(8,128)(2,1)} %copy-done.8) | copy-start | bytes 1572868
  118.2 14.4 %all-to-all-start.1 = ((f32[4,32,256]{2,1,0:T(8,128)}), f32[4,32,256]{2,1,0:T(8,128)S(1)}, u32[]{:S(2)}, u32[]{:S(2)}) async-start(f32[4,32,256]{2,1,0:T(8,128)} %bitcast.15), calls=%async_computation.1 | async-start | bytes 262144 | tf_op jit(solution)/shard_map/all_to_all | solution.py:432
